TPU v7x, 512 devices: a whole 4x4x16 slice. The times are simulated.
512 devices in a mesh: gx: 8 (over x, core), gy: 8 (over z_hi, y), gz: 8 (over z_lo).
Axes of the slice: x: 4, y: 4, z: 16 (z_hi: 2, z_lo: 8; z = z_hi * 8 + z_lo), core: 2. Of those that a mesh axis runs over, the one named last changes fastest.
Arguments:
- magnet: float32 [3, 32, 256, 2048], P(None, 'gz', 'gx', 'gy'), may hold values from -1 to 1, as said below
- grains: int32 [32, 256, 2048], P('gz', 'gx', 'gy'), may hold values from 0 to 15
- stiffness_table: float32 [16], replicated, may hold values from 0.2 to 1
- saturation_table: float32 [16], replicated, may hold values from 0.6 to 1.4
- kernel_x: bfloat16 [8, 256], replicated, may hold values from -3 to 3
- kernel_y: bfloat16 [8, 2048], replicated, may hold values from -3 to 3
- kernel_z: bfloat16 [8, 32], replicated, may hold values from -3 to 3
- mixing: float32 [8, 3, 3], replicated, may hold values from -1.25 to 1.25
Outputs:
- magnet_next: float32 [3, 32, 256, 2048], P(None, 'gz', 'gx', 'gy')
- demag_field: float32 [16, 3, 128, 1024], P('gz', None, 'gx', 'gy')
Inputs may be any that keep to these rules, and one draw needn't show every extreme that they name: `magnet`: every cell's three components form a unit vector.
All inputs are finite; a program needn't handle non-finite values.
Results may differ from a plain program's by a relative error of at most 0.00085.
The roundings to bfloat16 on the way count: a program that leaves them out, or rounds other values in their place, can miss the bound.
Values may be sent and summed in bfloat16 or wider, within the bound.
No kernel may reach another device: no remote copies, remote signals or barrier semaphores. Data moves between devices by JAX's collectives and lax.ppermute only.
A program may use at most 128 MiB of HBM per device.

v0:
```python
import jax
import jax.numpy as jnp
from jax import lax
from jax.sharding import PartitionSpec as P

SUBSTEPS = 3


time_step = 0.02
damping = 0.3


def with_halo(x, sides, width):
    for axis, dim in sides:
        count, length = (lax.axis_size(axis), x.shape[dim])
        up = [(i, (i + 1) % count) for i in range(count - 1)]
        down = [(j, i) for i, j in up]
        last = lax.slice_in_dim(x, length - width, length, axis=dim)
        leading = lax.slice_in_dim(x, 0, width, axis=dim)
        before = lax.ppermute(last, axis, up)
        after = lax.ppermute(leading, axis, down)
        x = jnp.concatenate([before, x, after], axis=dim)
    return x


def toeplitz_rows(kernel, offset, extent):
    length = kernel.shape[1] // 2
    flipped = kernel[:, ::-1]
    row_ids = offset + jnp.arange(extent, dtype=jnp.int32)
    picked = jax.vmap(
        lambda row_index: lax.dynamic_slice_in_dim(flipped, length - 1 - row_index, length, 1)
    )(row_ids)
    return jnp.transpose(picked, (1, 0, 2))


def interior(values):
    return values[..., 1:-1, 1:-1, 1:-1]


def shifted(values, along, begin_at):
    slicer = [slice(1, -1), slice(1, -1), slice(1, -1)]
    slicer[along] = slice(begin_at, begin_at + values.shape[along - 3] - 2)
    leading = [slice(None)] * (values.ndim - 3)
    return values[tuple(leading + slicer)]


def cross_product(first_vec, second_vec):
    return jnp.stack(
        [
            first_vec[1] * second_vec[2] - first_vec[2] * second_vec[1],
            first_vec[2] * second_vec[0] - first_vec[0] * second_vec[2],
            first_vec[0] * second_vec[1] - first_vec[1] * second_vec[0],
        ]
    )


def exchange_update(magnet_rim, stiff_rim, saturation, demag_fine):
    centre = interior(magnet_rim)
    stiff_centre = interior(stiff_rim)
    coupled = jnp.zeros_like(centre)
    for along in range(3):
        for begin_at in (0, 2):
            stiff_near = shifted(stiff_rim, along, begin_at)
            denominator = stiff_centre + stiff_near
            weight = (
                2.0 * stiff_centre * stiff_near / jnp.where(denominator > 0.0, denominator, 1.0)
            )
            coupled = coupled + weight[None] * (shifted(magnet_rim, along, begin_at) - centre)
    inside = saturation > 0.0
    safe_sat = jnp.where(inside, saturation, 1.0)
    field_total = 2.0 * coupled / safe_sat[None] + demag_fine
    torque = cross_product(centre, field_total)
    raw_next = centre - time_step * (torque + damping * cross_product(centre, torque))
    length_sq = jnp.sqrt(jnp.sum(raw_next * raw_next, axis=0))
    safe_len = jnp.where(inside, length_sq, 1.0)
    return jnp.where(inside[None], raw_next / safe_len[None], 0.0)


def coarsen(magnet, saturation):
    weighted = saturation[None] * magnet
    comps, depth, width, height = weighted.shape
    shaped = weighted.reshape(comps, depth // 2, 2, width // 2, 2, height // 2, 2)
    return jnp.mean(shaped, axis=(2, 4, 6)).astype(jnp.bfloat16)


def prolong(demag):
    moved = jnp.transpose(demag, (1, 0, 2, 3))
    return jnp.repeat(jnp.repeat(jnp.repeat(moved, 2, axis=1), 2, axis=2), 2, axis=3)


def material_field(grains, lookup):
    labels = jnp.arange(lookup.shape[0], dtype=jnp.int32)
    matches = grains[None] == labels[:, None, None, None]
    return jnp.sum(jnp.where(matches, lookup[:, None, None, None], 0.0), axis=0)


def local(magnet, grains, stiffness_table, saturation_table, kernel_x, kernel_y, kernel_z, mixing):
    stiffness = material_field(grains, stiffness_table)
    saturation = material_field(grains, saturation_table)
    coarse = coarsen(magnet, saturation)
    rows_z = coarse.shape[1]
    rows_x = coarse.shape[2]
    rows_y = coarse.shape[3]
    block_x = toeplitz_rows(kernel_x, lax.axis_index("gx") * rows_x, rows_x)
    columns = block_x
    along_x = jnp.einsum(
        "rab,jzby->rjzay",
        columns,
        lax.all_gather(coarse, "gx", axis=2, tiled=True),
        preferred_element_type=jnp.float32,
    ).astype(jnp.bfloat16)
    block_y = toeplitz_rows(kernel_y, lax.axis_index("gy") * rows_y, rows_y)
    columns = block_y
    along_y = jnp.einsum(
        "rby,rjzxy->rjzxb",
        columns,
        lax.all_gather(along_x, "gy", axis=4, tiled=True),
        preferred_element_type=jnp.float32,
    ).astype(jnp.bfloat16)
    whole_z = toeplitz_rows(kernel_z, 0, kernel_z.shape[1] // 2).astype(jnp.float32)
    offset = lax.axis_index("gz") * rows_z
    own_rows = lax.dynamic_slice_in_dim(whole_z, offset, rows_z, 1)
    weights = jnp.einsum("rij,raz->airjz", mixing, own_rows, precision=lax.Precision.HIGHEST)
    columns = weights
    demag = jnp.einsum(
        "airjz,rjzxy->aixy",
        columns,
        lax.all_gather(along_y, "gz", axis=2, tiled=True).astype(jnp.float32),
        precision=lax.Precision.HIGHEST,
    )
    demag_fine = prolong(demag)
    stiff_rim = with_halo(
        stiffness[None].astype(jnp.bfloat16), (("gx", 2), ("gy", 3), ("gz", 1)), 1
    ).astype(jnp.float32)[0]
    state = magnet
    for substep in range(SUBSTEPS):
        magnet_rim = with_halo(state, (("gx", 2), ("gy", 3), ("gz", 1)), 1)
        state = exchange_update(magnet_rim, stiff_rim, saturation, demag_fine)
    return (state, demag)


def solution(mesh):
    in_specs = (P(None, "gz", "gx", "gy"), P("gz", "gx", "gy"), P(), P(), P(), P(), P(), P())
    out_specs = (P(None, "gz", "gx", "gy"), P("gz", None, "gx", "gy"))
    return jax.shard_map(local, mesh=mesh, in_specs=in_specs, out_specs=out_specs, check_vma=False)
```

profile of v0, /device:TPU:322, one launch (start us, length us, event | category | flops | bytes accessed | tf_op | source)
XLA Modules:
  0.0 572.9 jit_solution(10090580710956281949)
XLA Ops:
  7.2 1.3 select_reduce_fusion
  9.6 26.6 %reshape.132 = f32[3,2,2,16,2,128,2]{6,5,4,3,2,1,0:T(8,128)} reshape(f32[3,4,32,256]{3,2,1,0:T(8,128)S(1)} %broadcast_multiply_fusion) | data formatting | bytes 786432 | tf_op jit(solution)/shard_map/reshape | solution.py:82
  36.2 9.5 %reduce_sum.56 = f32[3,2,16,128]{3,2,1,0:T(8,128)S(1)} reduce(f32[3,2,2,16,2,128,2]{6,5,4,3,2,1,0:T(8,128)} %reshape.132, f32[]{:T(128)} %constant.19.clone.1), dimensions={2,4,6}, to_apply=%region_2.3 | reduce | flops 86016 | bytes 442372 | tf_op jit(solution)/shard_map/reduce_sum | solution.py:83
  45.6 12.8 %all_gather.9 = bf16[3,2,128,128]{3,2,1,0:T(8,128)(2,1)S(1)} all-gather(bf16[3,2,16,128]{3,2,1,0:T(8,128)(2,1)S(1)} %multiply_convert_fusion), channel_id=1, replica_groups=mesh['gx'=8,'gy'=8,'gz'=8] {'gx'}, dimensions={2}, use_global_device_ids=true | all-gather | bytes 221184 | tf_op jit(solution)/shard_map/all_gather | solution.py:109
  58.7 21.6 %while.4 = (s32[]{:T(128)}, bf16[8,256]{1,0:T(8,128)(2,1)S(1)}, s32[16,2]{0,1:T(2,128)S(1)}, bf16[16,8,128]{2,1,0:T(8,128)(2,1)S(1)}, s32[]{:T(128)}) while((s32[]{:T(128)}, bf16[8,256]{1,0:T(8,128)(2,1)S(1)}, s32[16,2]{0,1:T(2,128)S(1)}, bf16[16,8,128]{2,1,0:T(8,128)(2,1)S(1)}, s32[]{:T(128)}) %tuple.89), condition=%wide.while_cond.1, body=%wide.while_body.1.sunk | while | flops 2 | bytes 4201 | solution.py:31
  81.3 2.7 collective-permute-start.7
  84.0 1.9 collective-permute-start.6
  85.9 3.2 collective-permute-start
  89.2 2.4 collective-permute-start.1
  92.9 252.3 %while.5 = (s32[]{:T(128)}, bf16[8,2048]{1,0:T(8,128)(2,1)S(1)}, s32[128,2]{0,1:T(2,128)S(1)}, bf16[128,8,1024]{2,1,0:T(8,128)(2,1)}, s32[]{:T(128)}) while((s32[]{:T(128)}, bf16[8,2048]{1,0:T(8,128)(2,1)S(1)}, s32[128,2]{0,1:T(2,128)S(1)}, bf16[128,8,1024]{2,1,0:T(8,128)(2,1)}, s32[]{:T(128)}) %tuple.86), condition=%wide.while_cond.2, body=%wide.while_body.2.sunk | while | flops 2 | bytes 33381 | solution.py:31
  109.3 1.3 bitcast_dynamic-update-slice_fusion.8
  345.3 21.9 %while.3 = (s32[]{:T(128)}, bf16[8,32]{1,0:T(8,128)(2,1)S(1)}, s32[16,2]{0,1:T(2,128)S(1)}, bf16[16,8,16]{2,1,0:T(8,128)(2,1)S(1)}, s32[]{:T(128)}) while((s32[]{:T(128)}, bf16[8,32]{1,0:T(8,128)(2,1)S(1)}, s32[16,2]{0,1:T(2,128)S(1)}, bf16[16,8,16]{2,1,0:T(8,128)(2,1)S(1)}, s32[]{:T(128)}) %tuple.92), condition=%wide.while_cond, body=%wide.while_body.sunk | while | flops 2 | bytes 4201 | solution.py:31
  367.2 4.2 fusion.6
  371.7 3.1 collective-permute-start.3
  374.8 2.8 collective-permute-start.2
  377.7 14.0 %collective-permute-done.2 = bf16[1,4,34,1]{3,1,2,0:T(4,128)(2,1)S(1)} collective-permute-done((bf16[1,4,34,1]{3,1,2,0:T(4,128)(2,1)S(1)}, bf16[1,4,34,1]{3,1,2,0:T(4,128)(2,1)S(1)}, u32[]{:S(2)}, u32[]{:S(2)}) %collective-permute-start.2) | collective-permute-done | bytes 304 | tf_op jit(solution)/shard_map/ppermute | solution.py:20
  392.3 1.9 collective-permute-start.9
  394.2 3.9 collective-permute-start.8
  398.3 1.9 collective-permute-start.5
  400.2 3.9 collective-permute-start.4
  404.2 7.6 %collective-permute-done.9 = f32[3,4,34,1]{3,1,2,0:T(4,128)S(1)} collective-permute-done((f32[3,4,34,1]{3,1,2,0:T(4,128)S(1)}, f32[3,4,34,1]{3,1,2,0:T(4,128)S(1)}, u32[]{:S(2)}, u32[]{:S(2)}) %collective-permute-start.9) | collective-permute-done | bytes 1664 | tf_op jit(solution)/shard_map/ppermute | solution.py:21
  411.8 14.9 %collective-permute-done.8 = f32[3,4,34,1]{3,1,2,0:T(4,128)S(1)} collective-permute-done((f32[3,4,34,1]{3,1,2,0:T(4,128)S(1)}, f32[3,4,34,1]{3,1,2,0:T(4,128)S(1)}, u32[]{:S(2)}, u32[]{:S(2)}) %collective-permute-start.8) | collective-permute-done | bytes 1664 | tf_op jit(solution)/shard_map/ppermute | solution.py:20
  428.1 14.1 %collective-permute-start.11 = (f32[3,1,34,258]{3,2,1,0:T(8,128)}, f32[3,1,34,258]{3,2,1,0:T(8,128)}, u32[]{:S(2)}, u32[]{:S(2)}) collective-permute-start(f32[3,1,34,258]{3,2,1,0:T(8,128)} %get-tuple-element.96), channel_id=1, source_target_pairs={{1,0},{2,1},{3,2},{4,3},{5,4},{6,5},{7,6},{9,8},{10,9},{11,10},{12... | collective-permute-start | bytes 315800 | tf_op jit(solution)/shard_map/ppermute | solution.py:21
  442.2 1.9 collective-permute-start.10
  444.1 1.4 pad_maximum_fusion.16
  446.7 2.9 fusion.2
  451.5 1.7 broadcast_in_dim.120
  453.6 2.0 fusion.51
  456.0 1.9 collective-permute-start.12
  458.0 3.8 collective-permute-start.13
  463.2 2.3 collective-permute-start.15
  465.5 3.6 collective-permute-start.14
  469.1 4.0 collective-permute-done.15
  473.1 12.6 %collective-permute-done.14 = f32[3,4,34,1]{3,1,2,0:T(4,128)S(1)} collective-permute-done((f32[3,4,34,1]{3,1,2,0:T(4,128)S(1)}, f32[3,4,34,1]{3,1,2,0:T(4,128)S(1)}, u32[]{:S(2)}, u32[]{:S(2)}) %collective-permute-start.14) | collective-permute-done | bytes 1664 | tf_op jit(solution)/shard_map/ppermute | solution.py:20
  486.4 16.5 %collective-permute-start.17 = (f32[3,1,34,258]{3,2,1,0:T(8,128)S(1)}, f32[3,1,34,258]{3,2,1,0:T(8,128)S(1)}, u32[]{:S(2)}, u32[]{:S(2)}) collective-permute-start(f32[3,1,34,258]{3,2,1,0:T(8,128)S(1)} %get-tuple-element.94), channel_id=1, source_target_pairs={{1,0},{2,1},{3,2},{4,3},{5,4},{6,5},{7,6},{9,8},{10,9},{11,10},{12... | collective-permute-start | bytes 315800 | tf_op jit(solution)/shard_map/ppermute | solution.py:21
  502.9 1.9 collective-permute-start.16
  505.4 1.6 collective-permute-done.17
  507.0 4.1 collective-permute-done.16
  512.2 1.9 collective-permute-start.18
  514.1 3.6 collective-permute-start.19
  519.3 1.9 collective-permute-start.21
  521.3 3.9 collective-permute-start.20
  525.9 4.1 collective-permute-done.21
  529.9 15.4 %collective-permute-done.20 = f32[3,4,34,1]{3,1,2,0:T(4,128)S(1)} collective-permute-done((f32[3,4,34,1]{3,1,2,0:T(4,128)S(1)}, f32[3,4,34,1]{3,1,2,0:T(4,128)S(1)}, u32[]{:S(2)}, u32[]{:S(2)}) %collective-permute-start.20) | collective-permute-done | bytes 1664 | tf_op jit(solution)/shard_map/ppermute | solution.py:20
  545.9 10.1 %collective-permute-start.23 = (f32[3,1,34,258]{3,2,1,0:T(8,128)S(1)}, f32[3,1,34,258]{3,2,1,0:T(8,128)S(1)}, u32[]{:S(2)}, u32[]{:S(2)}) collective-permute-start(f32[3,1,34,258]{3,2,1,0:T(8,128)S(1)} %get-tuple-element.92), channel_id=1, source_target_pairs={{1,0},{2,1},{3,2},{4,3},{5,4},{6,5},{7,6},{9,8},{10,9},{11,10},{12... | collective-permute-start | bytes 315800 | tf_op jit(solution)/shard_map/ppermute | solution.py:21
  556.0 1.9 collective-permute-start.22
  558.5 1.6 collective-permute-done.23
  560.2 4.1 collective-permute-done.22
  (613 shorter events, 312.9 us)
Async XLA Ops:
  7.2 360.1 %all-gather.3.cloned.1.call-start = ((), (), s32[]{:S(2)}) async-start(), calls=%async_computation | async-start | bytes 1769472 | tf_op jit(solution)/shard_map/all_gather | solution.py:117
  36.1 22.3 %copy-start.9 = (bf16[8,256]{1,0:T(8,128)(2,1)S(1)}, bf16[8,256]{1,0:T(8,128)(2,1)}, u32[]{:S(2)}) copy-start(bf16[8,256]{1,0:T(8,128)(2,1)} %param.12) | copy-start | bytes 12292
  36.1 45.1 %copy-start = (f32[3,4,32,256]{3,2,1,0:T(8,128)S(1)}, f32[3,4,32,256]{3,2,1,0:T(8,128)}, u32[]{:S(2)}) copy-start(f32[3,4,32,256]{3,2,1,0:T(8,128)} %param.8) | copy-start | bytes 1179652
  36.2 55.4 %copy-start.7 = (bf16[8,2048]{1,0:T(8,128)(2,1)S(1)}, bf16[8,2048]{1,0:T(8,128)(2,1)}, u32[]{:S(2)}) copy-start(bf16[8,2048]{1,0:T(8,128)(2,1)} %param.13) | copy-start | bytes 98308
  36.2 309.0 %copy-start.10 = (bf16[8,32]{1,0:T(8,128)(2,1)S(1)}, bf16[8,32]{1,0:T(8,128)(2,1)}, u32[]{:S(2)}) copy-start(bf16[8,32]{1,0:T(8,128)(2,1)} %param.14) | copy-start | bytes 1540
  81.2 365.5 %all-gather.5.cloned.1.call-start = ((), (), s32[]{:S(2)}) async-start(), calls=%async_computation.1 | async-start | bytes 1769472 | tf_op jit(solution)/shard_map/all_gather | solution.py:128
  81.3 310.8 %collective-permute-start.7 = (f32[3,4,1,256]{3,1,2,0:T(4,128)S(1)}, f32[3,4,1,256]{3,1,2,0:T(4,128)S(1)}, u32[]{:S(2)}, u32[]{:S(2)}) collective-permute-start(f32[3,4,1,256]{3,1,2,0:T(4,128)S(1)} %copy.552), channel_id=1, source_target_pairs={{64,0},{128,64},{192,128},{256,192},{320,256},{384,320},{448,384},... | collective-permute-start | bytes 36872 | tf_op jit(solution)/shard_map/ppermute | solution.py:21
  84.0 307.8 %collective-permute-start.6 = (f32[3,4,1,256]{3,1,2,0:T(4,128)S(1)}, f32[3,4,1,256]{3,1,2,0:T(4,128)S(1)}, u32[]{:S(2)}, u32[]{:S(2)}) collective-permute-start(f32[3,4,1,256]{3,1,2,0:T(4,128)S(1)} %copy.553), channel_id=1, source_target_pairs={{0,64},{64,128},{128,192},{192,256},{256,320},{320,384},{384,448},... | collective-permute-start | bytes 36872 | tf_op jit(solution)/shard_map/ppermute | solution.py:20
  85.9 285.5 %collective-permute-start = (bf16[1,4,1,256]{3,2,1,0:T(2,128)(2,1)S(1)}, bf16[1,4,1,256]{3,2,1,0:T(2,128)(2,1)S(1)}, u32[]{:S(2)}, u32[]{:S(2)}) collective-permute-start(bf16[1,4,1,256]{3,2,1,0:T(2,128)(2,1)S(1)} %get-tuple-element.126), channel_id=1, source_target_pairs={{0,64},{64,128},{128,192},{192,256},{256,320},{320,384},{384,448},... | collective-permute-start | bytes 6152 | tf_op jit(solution)/shard_map/ppermute | solution.py:20
  89.2 282.4 %collective-permute-start.1 = (bf16[1,4,1,256]{3,2,1,0:T(2,128)(2,1)S(1)}, bf16[1,4,1,256]{3,2,1,0:T(2,128)(2,1)S(1)}, u32[]{:S(2)}, u32[]{:S(2)}) collective-permute-start(bf16[1,4,1,256]{3,2,1,0:T(2,128)(2,1)S(1)} %get-tuple-element.125), channel_id=1, source_target_pairs={{64,0},{128,64},{192,128},{256,192},{320,256},{384,320},{448,384},... | collective-permute-start | bytes 6152 | tf_op jit(solution)/shard_map/ppermute | solution.py:21
  367.2 10.3 %copy-start.8 = (f32[8,3,3]{0,2,1:T(4,128)S(1)}, f32[8,3,3]{0,2,1:T(4,128)}, u32[]{:S(2)}) copy-start(f32[8,3,3]{0,2,1:T(4,128)} %param.15) | copy-start | bytes 868
  371.7 6.0 %collective-permute-start.3 = (bf16[1,4,34,1]{3,1,2,0:T(4,128)(2,1)S(1)}, bf16[1,4,34,1]{3,1,2,0:T(4,128)(2,1)S(1)}, u32[]{:S(2)}, u32[]{:S(2)}) collective-permute-start(bf16[1,4,34,1]{3,1,2,0:T(4,128)(2,1)S(1)} %get-tuple-element.124), channel_id=1, source_target_pairs={{8,0},{16,8},{24,16},{32,24},{40,32},{48,40},{56,48},{9,1},{17,9},... | collective-permute-start | bytes 824 | tf_op jit(solution)/shard_map/ppermute | solution.py:21
  374.8 16.9 %collective-permute-start.2 = (bf16[1,4,34,1]{3,1,2,0:T(4,128)(2,1)S(1)}, bf16[1,4,34,1]{3,1,2,0:T(4,128)(2,1)S(1)}, u32[]{:S(2)}, u32[]{:S(2)}) collective-permute-start(bf16[1,4,34,1]{3,1,2,0:T(4,128)(2,1)S(1)} %get-tuple-element.123), channel_id=1, source_target_pairs={{0,8},{8,16},{16,24},{24,32},{32,40},{40,48},{48,56},{1,9},{9,17},... | collective-permute-start | bytes 824 | tf_op jit(solution)/shard_map/ppermute | solution.py:20
  392.3 19.5 %collective-permute-start.9 = (f32[3,4,34,1]{3,1,2,0:T(4,128)S(1)}, f32[3,4,34,1]{3,1,2,0:T(4,128)S(1)}, u32[]{:S(2)}, u32[]{:S(2)}) collective-permute-start(f32[3,4,34,1]{3,1,2,0:T(4,128)S(1)} %get-tuple-element.108), channel_id=1, source_target_pairs={{8,0},{16,8},{24,16},{32,24},{40,32},{48,40},{56,48},{9,1},{17,9},... | collective-permute-start | bytes 4904 | tf_op jit(solution)/shard_map/ppermute | solution.py:21
  394.2 32.5 %collective-permute-start.8 = (f32[3,4,34,1]{3,1,2,0:T(4,128)S(1)}, f32[3,4,34,1]{3,1,2,0:T(4,128)S(1)}, u32[]{:S(2)}, u32[]{:S(2)}) collective-permute-start(f32[3,4,34,1]{3,1,2,0:T(4,128)S(1)} %get-tuple-element.107), channel_id=1, source_target_pairs={{0,8},{8,16},{16,24},{24,32},{32,40},{40,48},{48,56},{1,9},{9,17},... | collective-permute-start | bytes 4904 | tf_op jit(solution)/shard_map/ppermute | solution.py:20
  398.3 47.3 %collective-permute-start.5 = (bf16[1,1,34,258]{3,2,1,0:T(8,128)(2,1)S(1)}, bf16[1,1,34,258]{3,2,1,0:T(8,128)(2,1)S(1)}, u32[]{:S(2)}, u32[]{:S(2)}) collective-permute-start(bf16[1,1,34,258]{3,2,1,0:T(8,128)(2,1)S(1)} %copy.554), channel_id=1, source_target_pairs={{1,0},{2,1},{3,2},{4,3},{5,4},{6,5},{7,6},{9,8},{10,9},{11,10},{12... | collective-permute-start | bytes 52640 | tf_op jit(solution)/shard_map/ppermute | solution.py:21
  400.2 45.4 %collective-permute-start.4 = (bf16[1,1,34,258]{3,2,1,0:T(8,128)(2,1)S(1)}, bf16[1,1,34,258]{3,2,1,0:T(8,128)(2,1)S(1)}, u32[]{:S(2)}, u32[]{:S(2)}) collective-permute-start(bf16[1,1,34,258]{3,2,1,0:T(8,128)(2,1)S(1)} %copy.555), channel_id=1, source_target_pairs={{0,1},{1,2},{2,3},{3,4},{4,5},{5,6},{6,7},{8,9},{9,10},{10,11},{11... | collective-permute-start | bytes 52640 | tf_op jit(solution)/shard_map/ppermute | solution.py:20
  428.1 25.5 %collective-permute-start.11 = (f32[3,1,34,258]{3,2,1,0:T(8,128)}, f32[3,1,34,258]{3,2,1,0:T(8,128)}, u32[]{:S(2)}, u32[]{:S(2)}) collective-permute-start(f32[3,1,34,258]{3,2,1,0:T(8,128)} %get-tuple-element.96), channel_id=1, source_target_pairs={{1,0},{2,1},{3,2},{4,3},{5,4},{6,5},{7,6},{9,8},{10,9},{11,10},{12... | collective-permute-start | bytes 315800 | tf_op jit(solution)/shard_map/ppermute | solution.py:21
  442.2 11.4 %collective-permute-start.10 = (f32[3,1,34,258]{3,2,1,0:T(8,128)}, f32[3,1,34,258]{3,2,1,0:T(8,128)}, u32[]{:S(2)}, u32[]{:S(2)}) collective-permute-start(f32[3,1,34,258]{3,2,1,0:T(8,128)} %get-tuple-element.95), channel_id=1, source_target_pairs={{0,1},{1,2},{2,3},{3,4},{4,5},{5,6},{6,7},{8,9},{9,10},{10,11},{11... | collective-permute-start | bytes 315800 | tf_op jit(solution)/shard_map/ppermute | solution.py:20
  449.6 0.6 copy-start.5
  456.0 5.8 %collective-permute-start.12 = (f32[3,4,1,256]{3,1,2,0:T(4,128)S(1)}, f32[3,4,1,256]{3,1,2,0:T(4,128)S(1)}, u32[]{:S(2)}, u32[]{:S(2)}) collective-permute-start(f32[3,4,1,256]{3,1,2,0:T(4,128)S(1)} %copy.454), channel_id=1, source_target_pairs={{0,64},{64,128},{128,192},{192,256},{256,320},{320,384},{384,448},... | collective-permute-start | bytes 36872 | tf_op jit(solution)/shard_map/ppermute | solution.py:20
  458.0 5.0 collective-permute-start.13
  463.2 9.9 %collective-permute-start.15 = (f32[3,4,34,1]{3,1,2,0:T(4,128)S(1)}, f32[3,4,34,1]{3,1,2,0:T(4,128)S(1)}, u32[]{:S(2)}, u32[]{:S(2)}) collective-permute-start(f32[3,4,34,1]{3,1,2,0:T(4,128)S(1)} %get-tuple-element.104), channel_id=1, source_target_pairs={{8,0},{16,8},{24,16},{32,24},{40,32},{48,40},{56,48},{9,1},{17,9},... | collective-permute-start | bytes 4904 | tf_op jit(solution)/shard_map/ppermute | solution.py:21
  465.5 20.2 %collective-permute-start.14 = (f32[3,4,34,1]{3,1,2,0:T(4,128)S(1)}, f32[3,4,34,1]{3,1,2,0:T(4,128)S(1)}, u32[]{:S(2)}, u32[]{:S(2)}) collective-permute-start(f32[3,4,34,1]{3,1,2,0:T(4,128)S(1)} %get-tuple-element.103), channel_id=1, source_target_pairs={{0,8},{8,16},{16,24},{24,32},{32,40},{40,48},{48,56},{1,9},{9,17},... | collective-permute-start | bytes 4904 | tf_op jit(solution)/shard_map/ppermute | solution.py:20
  486.2 24.9 %copy-start.1 = (f32[4,32,256]{2,1,0:T(8,128)S(1)}, f32[4,32,256]{2,1,0:T(8,128)}, u32[]{:S(2)}) copy-start(f32[4,32,256]{2,1,0:T(8,128)} %get-tuple-element.118) | copy-start | bytes 393220
  486.2 24.9 %copy-start.2 = (f32[4,32,256]{2,1,0:T(8,128)S(1)}, f32[4,32,256]{2,1,0:T(8,128)}, u32[]{:S(2)}) copy-start(f32[4,32,256]{2,1,0:T(8,128)} %get-tuple-element.119) | copy-start | bytes 393220
  486.2 24.8 %copy-start.3 = (f32[4,32,256]{2,1,0:T(8,128)S(1)}, f32[4,32,256]{2,1,0:T(8,128)}, u32[]{:S(2)}) copy-start(f32[4,32,256]{2,1,0:T(8,128)} %get-tuple-element.120) | copy-start | bytes 393220
  486.2 24.8 %copy-start.4 = (f32[4,32,256]{2,1,0:T(8,128)S(1)}, f32[4,32,256]{2,1,0:T(8,128)}, u32[]{:S(2)}) copy-start(f32[4,32,256]{2,1,0:T(8,128)} %get-tuple-element.127) | copy-start | bytes 393220
  486.4 20.6 %collective-permute-start.17 = (f32[3,1,34,258]{3,2,1,0:T(8,128)S(1)}, f32[3,1,34,258]{3,2,1,0:T(8,128)S(1)}, u32[]{:S(2)}, u32[]{:S(2)}) collective-permute-start(f32[3,1,34,258]{3,2,1,0:T(8,128)S(1)} %get-tuple-element.94), channel_id=1, source_target_pairs={{1,0},{2,1},{3,2},{4,3},{5,4},{6,5},{7,6},{9,8},{10,9},{11,10},{12... | collective-permute-start | bytes 315800 | tf_op jit(solution)/shard_map/ppermute | solution.py:21
  502.9 8.2 %collective-permute-start.16 = (f32[3,1,34,258]{3,2,1,0:T(8,128)S(1)}, f32[3,1,34,258]{3,2,1,0:T(8,128)S(1)}, u32[]{:S(2)}, u32[]{:S(2)}) collective-permute-start(f32[3,1,34,258]{3,2,1,0:T(8,128)S(1)} %get-tuple-element.93), channel_id=1, source_target_pairs={{0,1},{1,2},{2,3},{3,4},{4,5},{5,6},{6,7},{8,9},{9,10},{10,11},{11... | collective-permute-start | bytes 315800 | tf_op jit(solution)/shard_map/ppermute | solution.py:20
  511.9 13.3 %copy-start.6 = (f32[2,3,16,128,1,1]{3,1,5,4,2,0:T(4,128)S(1)}, f32[2,3,16,128,1,1]{3,1,5,4,2,0:T(4,128)}, u32[]{:S(2)}) copy-start(f32[2,3,16,128,1,1]{3,1,5,4,2,0:T(4,128)} %copy-done.5) | copy-start | bytes 147460
  512.2 5.6 collective-permute-start.18
  514.1 5.0 collective-permute-start.19
  519.3 10.6 %collective-permute-start.21 = (f32[3,4,34,1]{3,1,2,0:T(4,128)S(1)}, f32[3,4,34,1]{3,1,2,0:T(4,128)S(1)}, u32[]{:S(2)}, u32[]{:S(2)}) collective-permute-start(f32[3,4,34,1]{3,1,2,0:T(4,128)S(1)} %get-tuple-element.100), channel_id=1, source_target_pairs={{8,0},{16,8},{24,16},{32,24},{40,32},{48,40},{56,48},{9,1},{17,9},... | collective-permute-start | bytes 4904 | tf_op jit(solution)/shard_map/ppermute | solution.py:21
  521.3 24.0 %collective-permute-start.20 = (f32[3,4,34,1]{3,1,2,0:T(4,128)S(1)}, f32[3,4,34,1]{3,1,2,0:T(4,128)S(1)}, u32[]{:S(2)}, u32[]{:S(2)}) collective-permute-start(f32[3,4,34,1]{3,1,2,0:T(4,128)S(1)} %get-tuple-element.99), channel_id=1, source_target_pairs={{0,8},{8,16},{16,24},{24,32},{32,40},{40,48},{48,56},{1,9},{9,17},... | collective-permute-start | bytes 4904 | tf_op jit(solution)/shard_map/ppermute | solution.py:20
  545.9 14.3 %collective-permute-start.23 = (f32[3,1,34,258]{3,2,1,0:T(8,128)S(1)}, f32[3,1,34,258]{3,2,1,0:T(8,128)S(1)}, u32[]{:S(2)}, u32[]{:S(2)}) collective-permute-start(f32[3,1,34,258]{3,2,1,0:T(8,128)S(1)} %get-tuple-element.92), channel_id=1, source_target_pairs={{1,0},{2,1},{3,2},{4,3},{5,4},{6,5},{7,6},{9,8},{10,9},{11,10},{12... | collective-permute-start | bytes 315800 | tf_op jit(solution)/shard_map/ppermute | solution.py:21
  556.0 8.3 %collective-permute-start.22 = (f32[3,1,34,258]{3,2,1,0:T(8,128)S(1)}, f32[3,1,34,258]{3,2,1,0:T(8,128)S(1)}, u32[]{:S(2)}, u32[]{:S(2)}) collective-permute-start(f32[3,1,34,258]{3,2,1,0:T(8,128)S(1)} %get-tuple-element.91), channel_id=1, source_target_pairs={{0,1},{1,2},{2,3},{3,4},{4,5},{5,6},{6,7},{8,9},{9,10},{10,11},{11... | collective-permute-start | bytes 315800 | tf_op jit(solution)/shard_map/ppermute | solution.py:20
Sparse Core Ops, SparseCore 0:
  81.3 92.6 all-gather.2
  371.6 70.0 all-gather.4
where the time goes:
time: 576 us; the launch traced here: 573 us
  local copies, waits for them, and re-layouts  331 us (57%)
  starting transfers between devices  97.2 us (17%)
  waiting for transfers between devices  86.1 us (15%)
  other arithmetic  22.3 us (4%)
  between operations  14.9 us (3%)
  blocking collectives  12.8 us (2%)
  matrix products  7.96 us (1%)
    gather x480, local copies, waits for them, and re-layouts  296 us
    ppermute x12, waiting for transfers between devices, with_halo(): before = lax.ppermute(last, axis, up)  65.1 us
    ppermute x12, starting transfers between devices, with_halo(): after = lax.ppermute(leading, axis, down)  64.3 us
    ppermute x12, starting transfers between devices, with_halo(): before = lax.ppermute(last, axis, up)  32.8 us
    reshape x1, local copies, waits for them, and re-layouts, coarsen(): weighted.reshape(comps, depth // 2, 2, width // 2, 2, height // 2, 2)  26.6 us
    ppermute x12, waiting for transfers between devices, with_halo(): after = lax.ppermute(leading, axis, down)  20.9 us
    all_gather x1, blocking collectives, local(): lax.all_gather(coarse, 'gx', axis=2, tiled=True)  12.8 us
  transfers between devices with their start and end apart: 26, of which 13 were waited for; matrix products, arithmetic and copies ran while one was open for 51% of the time, Pallas kernels for 0%

commit v1 on v0

v1 whole, which is shorter than its diff:
```python
import functools

import jax
import jax.numpy as jnp
from jax import lax
from jax.experimental import pallas as pl
from jax.experimental.pallas import tpu as pltpu
from jax.sharding import PartitionSpec as P

f32, bf16, i32 = jnp.float32, jnp.bfloat16, jnp.int32
VM = pl.BlockSpec(memory_space=pltpu.VMEM)
SM = pl.BlockSpec(memory_space=pltpu.SMEM)
TIME_STEP = 0.02
DAMPING = 0.3


def iota(shape, dim):
    return lax.broadcasted_iota(i32, shape, dim)


def one_hot(condition):
    return jnp.where(condition, 1.0, 0.0).astype(bf16)


def dot(a, b, dims=((1,), (0,))):
    return lax.dot_general(a, b, (dims, ((), ())), preferred_element_type=f32)


def lookup(ids, table):
    bits = [(ids & (1 << k)) != 0 for k in range(4)]
    level = [table[k] for k in range(16)]
    for bit in bits:
        level = [jnp.where(bit, level[2 * k + 1], level[2 * k]) for k in range(len(level) // 2)]
    return level[0]


def call(body, out_shape, in_specs, scratch=(), flops=0, nbytes=0):
    outs = out_shape if isinstance(out_shape, list) else [out_shape]
    result = pl.pallas_call(
        body,
        out_shape=outs,
        in_specs=in_specs,
        out_specs=[VM] * len(outs),
        scratch_shapes=list(scratch),
        cost_estimate=pl.CostEstimate(flops=flops, bytes_accessed=nbytes, transcendentals=0),
    )
    return result


def coarse_kernel(mag, grains, sat, out, scr):
    for a in range(2):
        s0 = lookup(grains[2 * a], sat)
        s1 = lookup(grains[2 * a + 1], sat)
        for j in range(3):
            scr[j * 2 + a] = s0 * mag[j, 2 * a] + s1 * mag[j, 2 * a + 1]
    pick = one_hot(iota((256, 128), 0) == 2 * iota((256, 128), 1))
    rows = []
    for p in range(6):
        s = scr[p].reshape(16, 2, 256)
        s = s[:, 0, :] + s[:, 1, :]
        s = s + pltpu.roll(s, 255, 1)
        rows.append((s * 0.125).astype(bf16))
    out[0:96, :] = dot(jnp.concatenate(rows, axis=0), pick).astype(bf16)
    cells = [mag[j].reshape(128, 256).astype(bf16) for j in range(3)]
    cells.append(grains[...].reshape(128, 256).astype(f32).astype(bf16))
    cells = jnp.concatenate(cells, axis=0)
    k, lane = iota((16, 256), 0), iota((16, 256), 1)
    edge = one_hot(((k < 3) & (lane == k)) | ((k >= 8) & (k < 11) & (lane == 245 + k)))
    faces = dot(edge, cells, ((1,), (1,))).astype(bf16)
    for q in range(4):
        out[96 + 16 * q : 112 + 16 * q, :] = faces[:, 128 * q : 128 * (q + 1)]


def toeplitz_kernel(kyp, kxr, strip, kx_out):
    gx = lax.axis_index("gx")

    def one(r, carry):
        row = jnp.broadcast_to(kyp[pl.ds(r, 1), :], (128, 2176))
        strip[pl.ds(r, 1)] = pltpu.roll(row, 0, 1, stride=1, stride_axis=0).astype(bf16)[None]
        return carry

    lax.fori_loop(0, 8, one, 0)
    lane = iota((24, 256), 1)
    for r in range(8):
        row = pltpu.roll(jnp.broadcast_to(kxr[r : r + 1, :], (24, 256)), 0, 1, stride=1, stride_axis=0)
        total = jnp.zeros((24, 256), f32)
        for l in range(8):
            shift = (16 * l + 16 * (gx - (gx ^ l)) + 128 + 512) & 255
            total = jnp.where(lane // 16 == l, pltpu.roll(row, shift, 1), total)
        kx_out[r * 24 : (r + 1) * 24, :] = total[:, :128]


def faces_kernel(own, p7, r1, r2, r3, mag, grains, pay, face_a, rim, scr_a, scr_b):
    gx, gy = lax.axis_index("gx"), lax.axis_index("gy")
    blocks = [own[0:96], r1[0:96], r2[0:96], r3[0:96], r3[96:192], r2[96:192], r1[96:192], p7[0:96]]
    for k in range(8):
        pay[k * 96 : (k + 1) * 96, :] = blocks[k]

    def faces(ref, base):
        return jnp.concatenate([ref[base + 16 * q : base + 16 * (q + 1), :].astype(f32) for q in range(4)], axis=1)

    f1, f3, f7 = faces(r1, 192), faces(r3, 192), faces(p7, 96)
    even = (gy & 1) == 0
    fb = jnp.where((gy == 3) | (gy == 4), f7, f3)
    right, left = jnp.where(even, f1, fb), jnp.where(even, fb, f1)
    sel = jnp.concatenate([right[0:8], left[8:16]], axis=0)
    k, lane = iota((16, 128), 0), iota((16, 128), 1)
    put = one_hot(((k < 3) & (lane == k)) | ((k >= 8) & (k < 11) & (lane == 117 + k)))
    unpacked = dot(sel.astype(bf16), put, ((0,), (0,)))
    rim[...] = unpacked.astype(bf16)
    odd = (gx & 1) == 1
    for c in range(4):
        for z in range(4):
            plane = (c * 4 + z) * 32
            low = mag[c, z, 0:8, :] if c < 3 else grains[z, 0:8, :].astype(f32)
            high = mag[c, z, 24:32, :] if c < 3 else grains[z, 24:32, :].astype(f32)
            low = jnp.concatenate([low, unpacked[plane : plane + 8]], axis=1)[0:3]
            high = jnp.concatenate([high, unpacked[plane + 24 : plane + 32]], axis=1)[5:8]
            to_b, to_a = jnp.where(odd, high, low), jnp.where(odd, low, high)
            for q in range(3):
                at = q * 48 + (c * 4 + z) * 3
                scr_b[at : at + 3, :] = to_b[:, q * 128 : (q + 1) * 128]
                scr_a[at : at + 3, :] = to_a[:, q * 128 : (q + 1) * 128]
    pay[768:912, :] = scr_b[...].astype(bf16)
    face_a[...] = scr_a[...].astype(bf16)


def rims_kernel(mag, grains, rim, rc, r3, r7, low_out, high_out, scr, fa, fb):
    gx = lax.axis_index("gx")
    even = (gx & 1) == 0
    a = rc[3072:3216, :].astype(f32)
    b = jnp.where((gx == 3) | (gx == 4), r7[768:912, :].astype(f32), r3[768:912, :].astype(f32))
    fa[...] = jnp.where(even, a, b)
    fb[...] = jnp.where(even, b, a)
    for z in range(4):
        for c in range(4):
            plane = (c * 4 + z) * 32
            scr[0:32, 0:256] = mag[c, z] if c < 3 else grains[z].astype(f32)
            scr[0:32, 256:384] = rim[plane : plane + 32, :].astype(f32)
            scr[32:40, :] = jnp.zeros((8, 384), f32)
            for q in range(3):
                at = q * 48 + (c * 4 + z) * 3
                scr[32:35, q * 128 : (q + 1) * 128] = fa[at : at + 3, :]
                scr[37:40, q * 128 : (q + 1) * 128] = fb[at : at + 3, :]
            whole = scr[...].astype(bf16)
            if z < 3:
                low_out[z * 4 + c] = whole
            if z > 0:
                high_out[(z - 1) * 4 + c] = whole


def stages_kernel(own, r3, r4, r7, rc, kx, strip, wz, out, ax, ay):
    gy = lax.axis_index("gy")
    kxm = kx[...].astype(bf16)

    def x_stage(n, carry):
        kp, jz = n // 6, n % 6
        halves = []
        for half in range(2):
            at = pl.multiple_of(((2 * kp + half) * 6 + jz) * 16, 16)
            base = lambda g: pl.ds(pl.multiple_of(at + 768 * g, 16), 16)
            parts = [own[base(0)], rc[base(0)], rc[base(1)], r3[base(0)], r4[base(0)], rc[base(2)], rc[base(3)], r7[base(0)]]
            halves.append(jnp.concatenate(parts, axis=0))
        res = dot(kxm, jnp.concatenate(halves, axis=1))
        for r in range(8):
            ax[r, pl.ds(pl.multiple_of(jz * 24, 8), 24), pl.ds(pl.multiple_of(kp * 256, 256), 256)] = res[r * 24 : (r + 1) * 24]
        return carry

    lax.fori_loop(0, 24, x_stage, 0)
    ay[...] = jnp.zeros_like(ay)

    def y_stage(r, carry):
        acc = jnp.zeros((144, 256), f32)
        for kp in range(4):
            tiles = []
            for k in (2 * kp, 2 * kp + 1):
                at = pl.multiple_of(128 * (8 + gy - (gy ^ k)), 128)
                tiles.append(strip[r, :, pl.ds(at, 256)])
            acc = acc + dot(ax[r, :, kp * 256 : (kp + 1) * 256].astype(bf16), jnp.concatenate(tiles, axis=0))
        acc = acc.astype(bf16).astype(f32)
        for jz in range(6):
            for a in range(18):
                ay[a, pl.ds(r * 8 + jz, 1), :] = acc[jz * 24 + a : jz * 24 + a + 1, :]
        return carry

    lax.fori_loop(0, 8, y_stage, 0)
    w = wz[...]
    lane = iota((64, 128), 1)
    rims = jnp.zeros((64, 128), f32)
    for a in range(18):
        o3 = dot(w, ay[a].astype(bf16))
        o = pltpu.roll(o3[0:64] + o3[64:128] + o3[128:192], 192, 1)
        rims = jnp.where(lane // 2 == a, pltpu.roll(o[:, 128:], 2 * a + 1, 1), rims)
        for d in range(8):
            out[d, a * 6 : a * 6 + 6, :] = o[d * 8 : d * 8 + 6, :128]
    for d in range(8):
        out[d, 108:114, :] = rims[d * 8 : d * 8 + 6]
        out[d, 114:120, :] = jnp.zeros((6, 128), f32)


def substeps_kernel(
    mag, grains, own_low, own_high, z_low, z_high, d_own, d_low, d_high, stiff, two_over_sat,
    state_out, demag_out, m0, m1, aa, wx, wy, wz, ss, fz, field, rows, spread,
):
    gx, gy, gz = (lax.axis_index(n) for n in ("gx", "gy", "gz"))
    for q in range(6):
        demag_out[q // 3, q % 3] = d_own[pl.ds(6 + q, 16, stride=6), :]
    lane24 = iota((24, 128), 1)
    row24 = iota((24, 128), 0)
    sources = [(d_low, 3), (d_own, 0), (d_own, 3), (d_high, 0)]
    rows[...] = jnp.zeros_like(rows)
    for level in range(4):
        ref, first = sources[level]
        for i in range(3):
            g = level * 3 + i
            q = first + i
            rows[g * 24 : g * 24 + 18, 0:128] = ref[pl.ds(q, 18, stride=6), :]
            rim = jnp.broadcast_to(ref[108 + q : 109 + q, :], (24, 128))
            rows[g * 24 : g * 24 + 24, 128:256] = jnp.where(lane24 // 2 == row24, rim, 0.0)
    x = rows[...]
    hi = x.astype(bf16)
    lo = (x - hi.astype(f32)).astype(bf16)
    a, b = iota((128, 256), 0), iota((128, 256), 1)
    wide = one_hot(b // 2 == a)
    a, b = iota((128, 128), 0), iota((128, 128), 1)
    ends = one_hot(((a % 2 == 1) & (b < 2)) | ((a % 2 == 0) & (b >= 126)))
    spread[:, 0:256] = dot(hi[:, :128], wide) + dot(lo[:, :128], wide)
    spread[:, 256:384] = dot(hi[:, 128:], ends) + dot(lo[:, 128:], ends)
    r40, c24 = iota((40, 24), 0), iota((40, 24), 1)
    tall = one_hot(((r40 < 32) & (c24 == 1 + r40 // 2)) | ((r40 >= 32) & (r40 < 34) & (c24 == 17)) | ((r40 >= 38) & (c24 == 0)))
    for g in range(12):
        v = spread[g * 24 : (g + 1) * 24, :]
        hi = v.astype(bf16)
        lo = (v - hi.astype(f32)).astype(bf16)
        field[g] = dot(tall, hi) + dot(tall, lo)
    row, col = iota((40, 384), 0), iota((40, 384), 1)
    inside = ((row < 32) | ((row < 36) & (gx < 7)) | ((row >= 36) & (gx > 0))) & (
        (col < 256) | ((col < 320) & (gy < 7)) | ((col >= 320) & (gy > 0))
    )
    for p in range(10):
        z = p - 3
        if z < 0:
            whole = [z_low[p * 4 + c].astype(f32) for c in range(4)]
            ok = gz > 0
        elif z > 3:
            whole = [z_high[(z - 4) * 4 + c].astype(f32) for c in range(4)]
            ok = gz < 7
        else:
            ref, at = (own_low, z * 4) if z < 3 else (own_high, 8)
            whole = [ref[at + c].astype(f32) for c in range(4)]
            ok = gz >= 0
        for c in range(3):
            m0[c, p] = whole[c]
            if 0 <= z < 4:
                m0[c, p, 0:32, 0:256] = mag[c, z]
        ids = whole[3].astype(i32)
        aa[p] = jnp.where(inside & ok, lookup(ids, stiff), 0.0)
        ss[p] = lookup(ids, two_over_sat)

    def weight(u, v):
        den = u + v
        return 2.0 * u * v / jnp.where(den > 0.0, den, 1.0)

    for p in range(10):
        here = aa[p]
        if 1 <= p <= 8:
            wx[p] = weight(here, pltpu.roll(here, 39, 0))
            wy[p] = weight(here, pltpu.roll(here, 383, 1))
        if p < 9:
            wz[p] = weight(here, aa[p + 1])
    for step in range(3):
        src, dst = (m0, m1) if step % 2 == 0 else (m1, m0)
        first, last = step + 1, 8 - step

        def plane(p, carry):
            m = [src[c, p] for c in range(3)]
            w_up = wz[p]
            sat = ss[p]
            level = (p - 1) // 2
            h = []
            for c in range(3):
                flux = wx[p] * (pltpu.roll(m[c], 39, 0) - m[c])
                total = flux - pltpu.roll(flux, 1, 0)
                flux = wy[p] * (pltpu.roll(m[c], 383, 1) - m[c])
                total = total + (flux - pltpu.roll(flux, 1, 1))
                up = w_up * (src[c, p + 1] - m[c])
                total = total + (up - fz[c])
                fz[c] = up
                h.append(total * sat + field[level * 3 + c])
            t = [m[1] * h[2] - m[2] * h[1], m[2] * h[0] - m[0] * h[2], m[0] * h[1] - m[1] * h[0]]
            u = [m[1] * t[2] - m[2] * t[1], m[2] * t[0] - m[0] * t[2], m[0] * t[1] - m[1] * t[0]]
            raw = [m[c] - TIME_STEP * (t[c] + DAMPING * u[c]) for c in range(3)]
            scale = lax.rsqrt(jnp.maximum(raw[0] * raw[0] + raw[1] * raw[1] + raw[2] * raw[2], 1e-30))
            for c in range(3):
                if step < 2:
                    dst[c, p] = raw[c] * scale
                else:
                    state_out[c, p - 3] = (raw[c] * scale)[0:32, 0:256]
            return carry

        for c in range(3):
            fz[c] = wz[first - 1] * (src[c, first] - src[c, first - 1])
        lax.fori_loop(first, last + 1, plane, 0)


def swap(value, axis, bit):
    return lax.ppermute(value, axis, [(i, i ^ bit) for i in range(8)])


def z_weights(kernel_z, mixing):
    gz = lax.axis_index("gz")
    kz = kernel_z.astype(f32)
    own = jnp.stack([lax.dynamic_slice_in_dim(kz, 16 - 2 * gz - zl, 16, 1) for zl in range(2)])
    own = own.reshape(2, 8, 8, 2)
    w = jnp.einsum("rij,zrda->dairjz", mixing, own, precision=lax.Precision.HIGHEST).reshape(8, 6, 8, 6)
    w = jnp.pad(w, ((0, 0), (0, 2), (0, 0), (0, 2))).reshape(64, 64)
    hi = lax.reduce_precision(w, 8, 7)
    mid = lax.reduce_precision(w - hi, 8, 7)
    return jnp.concatenate([hi, mid, w - hi - mid], axis=0).astype(bf16)


def local(magnet, grains, stiffness_table, saturation_table, kernel_x, kernel_y, kernel_z, mixing):
    shape = jax.ShapeDtypeStruct
    (pay0,) = call(
        coarse_kernel, shape((160, 128), bf16), [VM, VM, SM], [pltpu.VMEM((6, 32, 256), f32)], 20_000_000, 600_000
    )(magnet, grains, saturation_table)
    kyp = jnp.pad(kernel_y.astype(f32), ((0, 0), (64, 64)))
    strip, kx = call(
        toeplitz_kernel, [shape((8, 128, 2176), bf16), shape((192, 128), f32)], [VM, VM], (), 20_000_000, 5_000_000
    )(kyp, kernel_x[:, ::-1].astype(f32))
    wz = z_weights(kernel_z, mixing)
    p7 = swap(pay0, "gy", 7)
    pay_y = jnp.concatenate([pay0[:96], p7[:96], pay0[96:]], axis=0)
    r1, r2, r3 = (swap(pay_y, "gy", k) for k in (1, 2, 3))
    pay_x, face_a, rim = call(
        faces_kernel,
        [shape((912, 128), bf16), shape((144, 128), bf16), shape((512, 128), bf16)],
        [VM] * 7,
        [pltpu.VMEM((144, 128), f32)] * 2,
        1_000_000,
        1_000_000,
    )(pay0, p7, r1, r2, r3, magnet, grains)
    x3, x4, x7 = (swap(pay_x, "gx", k) for k in (3, 4, 7))
    pay_c = jnp.concatenate([pay_x[:768], x3[:768], x4[:768], x7[:768], face_a], axis=0)
    rc = swap(pay_c, "gx", 1)
    own_low, own_high = call(
        rims_kernel,
        [shape((12, 40, 384), bf16)] * 2,
        [VM] * 6,
        [pltpu.VMEM((40, 384), f32), pltpu.VMEM((144, 128), f32), pltpu.VMEM((144, 128), f32)],
        1_000_000,
        2_000_000,
    )(magnet, grains, rim, rc, x3, x7)
    up = [(i, i + 1) for i in range(7)]
    down = [(i + 1, i) for i in range(7)]
    z_low = lax.ppermute(own_high, "gz", up)
    z_high = lax.ppermute(own_low, "gz", down)
    (parts,) = call(
        stages_kernel,
        shape((8, 120, 128), f32),
        [VM] * 8,
        [pltpu.VMEM((8, 144, 1024), f32), pltpu.VMEM((18, 64, 256), f32)],
        2_000_000_000,
        10_000_000,
    )(pay_x, x3, x4, x7, rc, kx, strip, wz)
    d_own = jnp.sum(lax.all_to_all(parts, "gz", 0, 0, tiled=True), axis=0)
    d_low = lax.ppermute(d_own, "gz", up)
    d_high = lax.ppermute(d_own, "gz", down)
    big = (10, 40, 384)
    state, demag = call(
        substeps_kernel,
        [shape((3, 4, 32, 256), f32), shape((2, 3, 16, 128), f32)],
        [VM] * 9 + [SM] * 2,
        [pltpu.VMEM((3,) + big, f32)] * 2
        + [pltpu.VMEM(big, f32)] * 5
        + [pltpu.VMEM((3, 40, 384), f32), pltpu.VMEM((12, 40, 384), f32)]
        + [pltpu.VMEM((288, 256), f32), pltpu.VMEM((288, 384), f32)],
        50_000_000,
        5_000_000,
    )(magnet, grains, own_low, own_high, z_low, z_high, d_own, d_low, d_high, stiffness_table, 2.0 / saturation_table)
    return (state, demag)


def solution(mesh):
    in_specs = (P(None, "gz", "gx", "gy"), P("gz", "gx", "gy"), P(), P(), P(), P(), P(), P())
    out_specs = (P(None, "gz", "gx", "gy"), P("gz", None, "gx", "gy"))
    return jax.shard_map(local, mesh=mesh, in_specs=in_specs, out_specs=out_specs, check_vma=False)
```

time: 576 us -> 143 us (0.25)
  the two profiles are of different devices: /device:TPU:322 before, /device:TPU:2 now
where the time goes in v1:
time: 143 us; the launch traced here: 142 us
  starting transfers between devices  59.6 us (42%)
  waiting for transfers between devices  38.5 us (27%)
  Pallas kernels  33 us (23%)
  local copies, waits for them, and re-layouts  6.97 us (5%)
  other arithmetic  3.31 us (2%)
    ppermute x8, starting transfers between devices, swap(): return lax.ppermute(value, axis, [(i, i ^ bit) for i in range(8)])  39.2 us
    all_to_all x1, waiting for transfers between devices, local(): d_own = jnp.sum(lax.all_to_all(parts, 'gz', 0, 0, tiled=True), axis=0)  21 us
    ppermute x8, waiting for transfers between devices, swap(): return lax.ppermute(value, axis, [(i, i ^ bit) for i in range(8)])  13.4 us
    all_to_all x1, starting transfers between devices, local(): d_own = jnp.sum(lax.all_to_all(parts, 'gz', 0, 0, tiled=True), axis=0)  11.8 us
    pallas_call x1, Pallas kernels, local(): call(stages_kernel, shape((8, 120, 128), f32), [VM] * 8, [pltpu.VMEM((8,...  10.8 us
    pallas_call x1, Pallas kernels, local(): call(substeps_kernel, [shape((3, 4, 32, 256), f32), shape((2, 3, 16, 128)...  9.86 us
    pallas_call x1, Pallas kernels, local(): call(toeplitz_kernel, [shape((8, 128, 2176), bf16), shape((192, 128), f32...  5.56 us
    unnamed x38, local copies, waits for them, and re-layouts  4.36 us
  transfers between devices with their start and end apart: 13, of which 5 were waited for; matrix products, arithmetic and copies ran while one was open for 5% of the time, Pallas kernels for 6%

profile of v1, /device:TPU:2, one launch (start us, length us, event | category | flops | bytes accessed | tf_op | source)
XLA Modules:
  0.0 142.4 jit_solution(14216348859022501656)
XLA Ops:
  0.6 2.1 %shard_map.95.own = bf16[160,128]{1,0:T(8,128)(2,1)} custom-call(f32[3,4,32,256]{3,2,1,0:T(8,128)} %mag.7, s32[4,32,256]{2,1,0:T(8,128)} %grains.7, f32[16]{0:T(128)} %sat.1), custom_call_target="tpu_custom_call" | custom-call | flops 20000000 | bytes 600000 | tf_op jit(solution)/shard_map/pallas_call | solution.py:324
  2.7 18.2 %collective-permute-start = (bf16[160,128]{1,0:T(8,128)(2,1)}, bf16[160,128]{1,0:T(8,128)(2,1)S(1)}, u32[]{:S(2)}, u32[]{:S(2)}) collective-permute-start(bf16[160,128]{1,0:T(8,128)(2,1)} %shard_map.95.own), channel_id=1, source_target_pairs={{0,56},{8,48},{16,40},{24,32},{32,24},{40,16},{48,8},{56,0},{1,57}... | collective-permute-start | bytes 122888 | tf_op jit(solution)/shard_map/ppermute | solution.py:307
  20.9 0.8 copy.13
  21.7 0.7 slice.28
  22.4 0.7 slice.30
  23.2 0.0 collective-permute-done.p7
  23.2 2.1 %collective-permute-start.1 = (bf16[256,128]{1,0:T(8,128)(2,1)S(1)}, bf16[256,128]{1,0:T(8,128)(2,1)S(1)}, u32[]{:S(2)}, u32[]{:S(2)}) collective-permute-start(bf16[256,128]{1,0:T(8,128)(2,1)S(1)} %pad_maximum_fusion), channel_id=1, source_target_pairs={{0,8},{8,0},{16,24},{24,16},{32,40},{40,32},{48,56},{56,48},{1,9},... | collective-permute-start | bytes 196616 | tf_op jit(solution)/shard_map/ppermute | solution.py:307
  25.3 3.4 %collective-permute-start.2 = (bf16[256,128]{1,0:T(8,128)(2,1)S(1)}, bf16[256,128]{1,0:T(8,128)(2,1)S(1)}, u32[]{:S(2)}, u32[]{:S(2)}) collective-permute-start(bf16[256,128]{1,0:T(8,128)(2,1)S(1)} %pad_maximum_fusion), channel_id=1, source_target_pairs={{0,16},{8,24},{16,0},{24,8},{32,48},{40,56},{48,32},{56,40},{1,17}... | collective-permute-start | bytes 196616 | tf_op jit(solution)/shard_map/ppermute | solution.py:307
  28.7 4.9 %collective-permute-start.3 = (bf16[256,128]{1,0:T(8,128)(2,1)S(1)}, bf16[256,128]{1,0:T(8,128)(2,1)S(1)}, u32[]{:S(2)}, u32[]{:S(2)}) collective-permute-start(bf16[256,128]{1,0:T(8,128)(2,1)S(1)} %pad_maximum_fusion), channel_id=1, source_target_pairs={{0,24},{8,16},{16,8},{24,0},{32,56},{40,48},{48,40},{56,32},{1,25}... | collective-permute-start | bytes 196616 | tf_op jit(solution)/shard_map/ppermute | solution.py:307
  33.7 0.0 collective-permute-done.1.r1
  33.7 0.0 collective-permute-done.2.r2
  33.7 2.4 %collective-permute-done.3.r3 = bf16[256,128]{1,0:T(8,128)(2,1)S(1)} collective-permute-done((bf16[256,128]{1,0:T(8,128)(2,1)S(1)}, bf16[256,128]{1,0:T(8,128)(2,1)S(1)}, u32[]{:S(2)}, u32[]{:S(2)}) %collective-permute-start.3) | collective-permute-done | bytes 65568 | tf_op jit(solution)/shard_map/ppermute | solution.py:307
  36.1 0.6 copy-done.10
  36.7 2.1 %shard_map.96 = (bf16[912,128]{1,0:T(8,128)(2,1)}, bf16[144,128]{1,0:T(8,128)(2,1)}, bf16[512,128]{1,0:T(8,128)(2,1)}) custom-call(bf16[160,128]{1,0:T(8,128)(2,1)} %shard_map.95.own, bf16[160,128]{1,0:T(8,128)(2,1)} %copy-done.7, bf16[256,128]{1,0:T(8,128)(2,1)} %copy-done.8, bf16[256,128]{1,0:T(8,128)(2,1)} %copy-done.9, bf16[256,128]{1,0:T(8,128)(2,1)} %copy-done.10, ...), custom_call_target="tpu_custom_call" | custom-call | flops 1000000 | bytes 1000000 | tf_op jit(solution)/shard_map/pallas_call | solution.py:335
  38.8 1.9 %collective-permute-start.4 = (bf16[912,128]{1,0:T(8,128)(2,1)}, bf16[912,128]{1,0:T(8,128)(2,1)S(1)}, u32[]{:S(2)}, u32[]{:S(2)}) collective-permute-start(bf16[912,128]{1,0:T(8,128)(2,1)} %get-tuple-element.10.own), channel_id=1, source_target_pairs={{0,192},{64,128},{128,64},{192,0},{256,448},{320,384},{384,320},{4... | collective-permute-start | bytes 700424 | tf_op jit(solution)/shard_map/ppermute | solution.py:307
  40.7 4.0 %collective-permute-start.5 = (bf16[912,128]{1,0:T(8,128)(2,1)}, bf16[912,128]{1,0:T(8,128)(2,1)S(1)}, u32[]{:S(2)}, u32[]{:S(2)}) collective-permute-start(bf16[912,128]{1,0:T(8,128)(2,1)} %get-tuple-element.10.own), channel_id=1, source_target_pairs={{0,256},{64,320},{128,384},{192,448},{256,0},{320,64},{384,128},{4... | collective-permute-start | bytes 700424 | tf_op jit(solution)/shard_map/ppermute | solution.py:307
  44.8 2.7 %collective-permute-start.6 = (bf16[912,128]{1,0:T(8,128)(2,1)}, bf16[912,128]{1,0:T(8,128)(2,1)S(1)}, u32[]{:S(2)}, u32[]{:S(2)}) collective-permute-start(bf16[912,128]{1,0:T(8,128)(2,1)} %get-tuple-element.10.own), channel_id=1, source_target_pairs={{0,448},{64,384},{128,320},{192,256},{256,192},{320,128},{384,64},... | collective-permute-start | bytes 700424 | tf_op jit(solution)/shard_map/ppermute | solution.py:307
  47.5 1.0 slice_dynamic-update-slice_fusion.3
  48.4 0.0 collective-permute-done.4.r3
  48.5 6.0 %collective-permute-done.5.r4 = bf16[912,128]{1,0:T(8,128)(2,1)S(1)} collective-permute-done((bf16[912,128]{1,0:T(8,128)(2,1)}, bf16[912,128]{1,0:T(8,128)(2,1)S(1)}, u32[]{:S(2)}, u32[]{:S(2)}) %collective-permute-start.5) | collective-permute-done | bytes 233504 | tf_op jit(solution)/shard_map/ppermute | solution.py:307
  54.5 5.0 %collective-permute-done.6.r7 = bf16[912,128]{1,0:T(8,128)(2,1)S(1)} collective-permute-done((bf16[912,128]{1,0:T(8,128)(2,1)}, bf16[912,128]{1,0:T(8,128)(2,1)S(1)}, u32[]{:S(2)}, u32[]{:S(2)}) %collective-permute-start.6) | collective-permute-done | bytes 233504 | tf_op jit(solution)/shard_map/ppermute | solution.py:307
  59.5 0.8 constant_dynamic-update-slice_fusion
  60.4 2.0 %collective-permute-start.7 = (bf16[3216,128]{1,0:T(8,128)(2,1)S(1)}, bf16[3216,128]{1,0:T(8,128)(2,1)S(1)}, u32[]{:S(2)}, u32[]{:S(2)}) collective-permute-start(bf16[3216,128]{1,0:T(8,128)(2,1)S(1)} %constant_dynamic-update-slice_fusion), channel_id=1, source_target_pairs={{0,64},{64,0},{128,192},{192,128},{256,320},{320,256},{384,448},{4... | collective-permute-start | bytes 2469896 | tf_op jit(solution)/shard_map/ppermute | solution.py:307
  62.4 0.7 broadcast_multiply_fusion
  63.1 0.4 copy.16
  63.5 0.1 reshape.16
  63.6 0.2 rev.3
  63.8 0.6 convert_element_type.12.kxr
  64.4 0.7 pad_convert_fusion.kyp
  65.1 5.6 %shard_map.98 = (bf16[8,128,2176]{2,1,0:T(8,128)(2,1)}, f32[192,128]{1,0:T(8,128)}) custom-call(f32[8,2176]{1,0:T(8,128)} %pad_convert_fusion.kyp, f32[8,256]{1,0:T(8,128)} %convert_element_type.12.kxr), custom_call_target="tpu_custom_call" | custom-call | flops 20000000 | bytes 5000000 | tf_op jit(solution)/shard_map/pallas_call | solution.py:328
  70.7 0.6 pad_maximum_fusion.1.wz
  71.3 0.0 collective-permute-done.7.rc
  71.3 0.9 copy-done
  72.3 10.8 %shard_map.99 = f32[8,120,128]{2,1,0:T(8,128)} custom-call(bf16[912,128]{1,0:T(8,128)(2,1)} %get-tuple-element.10.own, bf16[912,128]{1,0:T(8,128)(2,1)} %copy-done.1, bf16[912,128]{1,0:T(8,128)(2,1)} %copy-done.6, bf16[912,128]{1,0:T(8,128)(2,1)} %copy-done.2, bf16[3216,128]{1,0:T(8,128)(2,1)} %copy-done, f32[192,128]{1,0:T(8,128)} %get-tuple-element.14.kx, ...), custom_call_target="tpu_custom_call" | custom-call | flops 2000000000 | bytes 10000000 | tf_op jit(solution)/shard_map/pallas_call | solution.py:358
  83.1 11.8 %all-to-all-start = ((f32[8,120,128]{2,1,0:T(8,128)}), f32[8,120,128]{2,1,0:T(8,128)S(1)}, u32[]{:S(2)}, u32[]{:S(2)}) async-start(f32[8,120,128]{2,1,0:T(8,128)} %shard_map.99), calls=%async_computation | async-start | bytes 983040 | tf_op jit(solution)/shard_map/all_to_all | solution.py:366
  94.9 2.5 %shard_map.97 = (bf16[12,40,384]{2,1,0:T(8,128)(2,1)}, bf16[12,40,384]{2,1,0:T(8,128)(2,1)}) custom-call(f32[3,4,32,256]{3,2,1,0:T(8,128)} %mag.7, s32[4,32,256]{2,1,0:T(8,128)} %grains.7, bf16[512,128]{1,0:T(8,128)(2,1)} %get-tuple-element.9.rim, bf16[3216,128]{1,0:T(8,128)(2,1)} %copy-done, bf16[912,128]{1,0:T(8,128)(2,1)} %copy-done.1, ...), custom_call_target="tpu_custom_call" | custom-call | flops 1000000 | bytes 2000000 | tf_op jit(solution)/shard_map/pallas_call | solution.py:346
  97.4 3.9 %collective-permute-start.8 = (bf16[12,40,384]{2,1,0:T(8,128)(2,1)}, bf16[12,40,384]{2,1,0:T(8,128)(2,1)S(1)}, u32[]{:S(2)}, u32[]{:S(2)}) collective-permute-start(bf16[12,40,384]{2,1,0:T(8,128)(2,1)} %get-tuple-element.13.own_high), channel_id=1, source_target_pairs={{0,1},{1,2},{2,3},{3,4},{4,5},{5,6},{6,7},{8,9},{9,10},{10,11},{11... | collective-permute-start | bytes 1105928 | tf_op jit(solution)/shard_map/ppermute | solution.py:356
  101.4 1.3 collective-permute-start.9
  102.7 21.0 %all-to-all-done = f32[8,120,128]{2,1,0:T(8,128)S(1)} async-done(((f32[8,120,128]{2,1,0:T(8,128)}), f32[8,120,128]{2,1,0:T(8,128)S(1)}, u32[]{:S(2)}, u32[]{:S(2)}) %all-to-all-start) | async-done | bytes 491552 | tf_op jit(solution)/shard_map/all_to_all | solution.py:366
  123.7 2.1 %collective-permute-start.10 = (f32[120,128]{1,0:T(8,128)S(1)}, f32[120,128]{1,0:T(8,128)S(1)}, u32[]{:S(2)}, u32[]{:S(2)}) collective-permute-start(f32[120,128]{1,0:T(8,128)S(1)} %reduce_sum.9.d_own), channel_id=1, source_target_pairs={{0,1},{1,2},{2,3},{3,4},{4,5},{5,6},{6,7},{8,9},{9,10},{10,11},{11... | collective-permute-start | bytes 184328 | tf_op jit(solution)/shard_map/ppermute | solution.py:367
  125.7 1.3 collective-permute-start.11
  127.1 0.6 broadcast_divide_fusion.two_over_sat
  127.6 0.0 collective-permute-done.8.z_low
  127.7 0.0 collective-permute-done.9.z_high
  127.7 0.0 collective-permute-done.10.d_low
  127.7 4.2 %collective-permute-done.11.d_high = f32[120,128]{1,0:T(8,128)S(1)} collective-permute-done((f32[120,128]{1,0:T(8,128)S(1)}, f32[120,128]{1,0:T(8,128)S(1)}, u32[]{:S(2)}, u32[]{:S(2)}) %collective-permute-start.11) | collective-permute-done | bytes 61472 | tf_op jit(solution)/shard_map/ppermute | solution.py:368
  131.9 0.6 copy-done.12
  132.5 9.9 %shard_map.100 = (f32[3,4,32,256]{3,2,1,0:T(8,128)}, f32[2,3,16,128]{3,2,1,0:T(8,128)}) custom-call(f32[3,4,32,256]{3,2,1,0:T(8,128)} %mag.7, s32[4,32,256]{2,1,0:T(8,128)} %grains.7, bf16[12,40,384]{2,1,0:T(8,128)(2,1)} %get-tuple-element.12.own_low, bf16[12,40,384]{2,1,0:T(8,128)(2,1)} %get-tuple-element.13.own_high, bf16[12,40,384]{2,1,0:T(8,128)(2,1)} %copy-done.3, ...), custom_call_target="tpu_custom_call" | custom-call | flops 50000000 | bytes 5000000 | tf_op jit(solution)/shard_map/pallas_call | solution.py:370
  (41 shorter events, 0.2 us)
Async XLA Ops:
  0.6 63.0 %copy-start.14 = (bf16[8,256]{1,0:T(8,128)(2,1)S(1)}, bf16[8,256]{1,0:T(8,128)(2,1)}, u32[]{:S(2)}) copy-start(bf16[8,256]{1,0:T(8,128)(2,1)} %param.12) | copy-start | bytes 12292
  0.6 63.8 %copy-start.13 = (bf16[8,2048]{1,0:T(8,128)(2,1)S(1)}, bf16[8,2048]{1,0:T(8,128)(2,1)}, u32[]{:S(2)}) copy-start(bf16[8,2048]{1,0:T(8,128)(2,1)} %param.13) | copy-start | bytes 98308
  2.7 20.4 %collective-permute-start = (bf16[160,128]{1,0:T(8,128)(2,1)}, bf16[160,128]{1,0:T(8,128)(2,1)S(1)}, u32[]{:S(2)}, u32[]{:S(2)}) collective-permute-start(bf16[160,128]{1,0:T(8,128)(2,1)} %shard_map.95.own), channel_id=1, source_target_pairs={{0,56},{8,48},{16,40},{24,32},{32,24},{40,16},{48,8},{56,0},{1,57}... | collective-permute-start | bytes 122888 | tf_op jit(solution)/shard_map/ppermute | solution.py:307
  23.2 12.9 %copy-start.7 = (bf16[160,128]{1,0:T(8,128)(2,1)}, bf16[160,128]{1,0:T(8,128)(2,1)S(1)}, u32[]{:S(2)}) copy-start(bf16[160,128]{1,0:T(8,128)(2,1)S(1)} %collective-permute-done.p7) | copy-start | bytes 122884
  23.2 10.5 %collective-permute-start.1 = (bf16[256,128]{1,0:T(8,128)(2,1)S(1)}, bf16[256,128]{1,0:T(8,128)(2,1)S(1)}, u32[]{:S(2)}, u32[]{:S(2)}) collective-permute-start(bf16[256,128]{1,0:T(8,128)(2,1)S(1)} %pad_maximum_fusion), channel_id=1, source_target_pairs={{0,8},{8,0},{16,24},{24,16},{32,40},{40,32},{48,56},{56,48},{1,9},... | collective-permute-start | bytes 196616 | tf_op jit(solution)/shard_map/ppermute | solution.py:307
  25.3 8.4 %collective-permute-start.2 = (bf16[256,128]{1,0:T(8,128)(2,1)S(1)}, bf16[256,128]{1,0:T(8,128)(2,1)S(1)}, u32[]{:S(2)}, u32[]{:S(2)}) collective-permute-start(bf16[256,128]{1,0:T(8,128)(2,1)S(1)} %pad_maximum_fusion), channel_id=1, source_target_pairs={{0,16},{8,24},{16,0},{24,8},{32,48},{40,56},{48,32},{56,40},{1,17}... | collective-permute-start | bytes 196616 | tf_op jit(solution)/shard_map/ppermute | solution.py:307
  28.7 7.4 %collective-permute-start.3 = (bf16[256,128]{1,0:T(8,128)(2,1)S(1)}, bf16[256,128]{1,0:T(8,128)(2,1)S(1)}, u32[]{:S(2)}, u32[]{:S(2)}) collective-permute-start(bf16[256,128]{1,0:T(8,128)(2,1)S(1)} %pad_maximum_fusion), channel_id=1, source_target_pairs={{0,24},{8,16},{16,8},{24,0},{32,56},{40,48},{48,40},{56,32},{1,25}... | collective-permute-start | bytes 196616 | tf_op jit(solution)/shard_map/ppermute | solution.py:307
  33.7 2.4 %copy-start.8 = (bf16[256,128]{1,0:T(8,128)(2,1)}, bf16[256,128]{1,0:T(8,128)(2,1)S(1)}, u32[]{:S(2)}) copy-start(bf16[256,128]{1,0:T(8,128)(2,1)S(1)} %collective-permute-done.1.r1) | copy-start | bytes 196612
  33.7 2.4 %copy-start.9 = (bf16[256,128]{1,0:T(8,128)(2,1)}, bf16[256,128]{1,0:T(8,128)(2,1)S(1)}, u32[]{:S(2)}) copy-start(bf16[256,128]{1,0:T(8,128)(2,1)S(1)} %collective-permute-done.2.r2) | copy-start | bytes 196612
  36.1 0.6 copy-start.10
  38.8 9.6 %collective-permute-start.4 = (bf16[912,128]{1,0:T(8,128)(2,1)}, bf16[912,128]{1,0:T(8,128)(2,1)S(1)}, u32[]{:S(2)}, u32[]{:S(2)}) collective-permute-start(bf16[912,128]{1,0:T(8,128)(2,1)} %get-tuple-element.10.own), channel_id=1, source_target_pairs={{0,192},{64,128},{128,64},{192,0},{256,448},{320,384},{384,320},{4... | collective-permute-start | bytes 700424 | tf_op jit(solution)/shard_map/ppermute | solution.py:307
  40.7 13.7 %collective-permute-start.5 = (bf16[912,128]{1,0:T(8,128)(2,1)}, bf16[912,128]{1,0:T(8,128)(2,1)S(1)}, u32[]{:S(2)}, u32[]{:S(2)}) collective-permute-start(bf16[912,128]{1,0:T(8,128)(2,1)} %get-tuple-element.10.own), channel_id=1, source_target_pairs={{0,256},{64,320},{128,384},{192,448},{256,0},{320,64},{384,128},{4... | collective-permute-start | bytes 700424 | tf_op jit(solution)/shard_map/ppermute | solution.py:307
  44.8 14.7 %collective-permute-start.6 = (bf16[912,128]{1,0:T(8,128)(2,1)}, bf16[912,128]{1,0:T(8,128)(2,1)S(1)}, u32[]{:S(2)}, u32[]{:S(2)}) collective-permute-start(bf16[912,128]{1,0:T(8,128)(2,1)} %get-tuple-element.10.own), channel_id=1, source_target_pairs={{0,448},{64,384},{128,320},{192,256},{256,192},{320,128},{384,64},... | collective-permute-start | bytes 700424 | tf_op jit(solution)/shard_map/ppermute | solution.py:307
  48.4 22.9 %copy-start.1 = (bf16[912,128]{1,0:T(8,128)(2,1)}, bf16[912,128]{1,0:T(8,128)(2,1)S(1)}, u32[]{:S(2)}) copy-start(bf16[912,128]{1,0:T(8,128)(2,1)S(1)} %collective-permute-done.4.r3) | copy-start | bytes 700420
  54.4 16.9 %copy-start.6 = (bf16[912,128]{1,0:T(8,128)(2,1)}, bf16[912,128]{1,0:T(8,128)(2,1)S(1)}, u32[]{:S(2)}) copy-start(bf16[912,128]{1,0:T(8,128)(2,1)S(1)} %collective-permute-done.5.r4) | copy-start | bytes 700420
  59.5 11.8 %copy-start.2 = (bf16[912,128]{1,0:T(8,128)(2,1)}, bf16[912,128]{1,0:T(8,128)(2,1)S(1)}, u32[]{:S(2)}) copy-start(bf16[912,128]{1,0:T(8,128)(2,1)S(1)} %collective-permute-done.6.r7) | copy-start | bytes 700420
  60.4 11.0 %collective-permute-start.7 = (bf16[3216,128]{1,0:T(8,128)(2,1)S(1)}, bf16[3216,128]{1,0:T(8,128)(2,1)S(1)}, u32[]{:S(2)}, u32[]{:S(2)}) collective-permute-start(bf16[3216,128]{1,0:T(8,128)(2,1)S(1)} %constant_dynamic-update-slice_fusion), channel_id=1, source_target_pairs={{0,64},{64,0},{128,192},{192,128},{256,320},{320,256},{384,448},{4... | collective-permute-start | bytes 2469896 | tf_op jit(solution)/shard_map/ppermute | solution.py:307
  71.3 0.9 copy-start
  72.3 54.8 %copy-start.15 = (f32[16]{0:T(128)S(1)}, f32[16]{0:T(128)}, u32[]{:S(2)}) copy-start(f32[16]{0:T(128)} %sat.1) | copy-start | bytes 196
  83.1 40.5 %all-to-all-start = ((f32[8,120,128]{2,1,0:T(8,128)}), f32[8,120,128]{2,1,0:T(8,128)S(1)}, u32[]{:S(2)}, u32[]{:S(2)}) async-start(f32[8,120,128]{2,1,0:T(8,128)} %shard_map.99), calls=%async_computation | async-start | bytes 983040 | tf_op jit(solution)/shard_map/all_to_all | solution.py:366
  97.4 30.2 %collective-permute-start.8 = (bf16[12,40,384]{2,1,0:T(8,128)(2,1)}, bf16[12,40,384]{2,1,0:T(8,128)(2,1)S(1)}, u32[]{:S(2)}, u32[]{:S(2)}) collective-permute-start(bf16[12,40,384]{2,1,0:T(8,128)(2,1)} %get-tuple-element.13.own_high), channel_id=1, source_target_pairs={{0,1},{1,2},{2,3},{3,4},{4,5},{5,6},{6,7},{8,9},{9,10},{10,11},{11... | collective-permute-start | bytes 1105928 | tf_op jit(solution)/shard_map/ppermute | solution.py:356
  101.4 26.3 %collective-permute-start.9 = (bf16[12,40,384]{2,1,0:T(8,128)(2,1)}, bf16[12,40,384]{2,1,0:T(8,128)(2,1)S(1)}, u32[]{:S(2)}, u32[]{:S(2)}) collective-permute-start(bf16[12,40,384]{2,1,0:T(8,128)(2,1)} %get-tuple-element.12.own_low), channel_id=1, source_target_pairs={{1,0},{2,1},{3,2},{4,3},{5,4},{6,5},{7,6},{9,8},{10,9},{11,10},{12... | collective-permute-start | bytes 1105928 | tf_op jit(solution)/shard_map/ppermute | solution.py:357
  123.7 8.2 %copy-start.5 = (f32[120,128]{1,0:T(8,128)}, f32[120,128]{1,0:T(8,128)S(1)}, u32[]{:S(2)}) copy-start(f32[120,128]{1,0:T(8,128)S(1)} %reduce_sum.9.d_own) | copy-start | bytes 184324
  123.7 4.0 %collective-permute-start.10 = (f32[120,128]{1,0:T(8,128)S(1)}, f32[120,128]{1,0:T(8,128)S(1)}, u32[]{:S(2)}, u32[]{:S(2)}) collective-permute-start(f32[120,128]{1,0:T(8,128)S(1)} %reduce_sum.9.d_own), channel_id=1, source_target_pairs={{0,1},{1,2},{2,3},{3,4},{4,5},{5,6},{6,7},{8,9},{9,10},{10,11},{11... | collective-permute-start | bytes 184328 | tf_op jit(solution)/shard_map/ppermute | solution.py:367
  125.7 6.1 %collective-permute-start.11 = (f32[120,128]{1,0:T(8,128)S(1)}, f32[120,128]{1,0:T(8,128)S(1)}, u32[]{:S(2)}, u32[]{:S(2)}) collective-permute-start(f32[120,128]{1,0:T(8,128)S(1)} %reduce_sum.9.d_own), channel_id=1, source_target_pairs={{1,0},{2,1},{3,2},{4,3},{5,4},{6,5},{7,6},{9,8},{10,9},{11,10},{12... | collective-permute-start | bytes 184328 | tf_op jit(solution)/shard_map/ppermute | solution.py:368
  127.6 4.2 %copy-start.3 = (bf16[12,40,384]{2,1,0:T(8,128)(2,1)}, bf16[12,40,384]{2,1,0:T(8,128)(2,1)S(1)}, u32[]{:S(2)}) copy-start(bf16[12,40,384]{2,1,0:T(8,128)(2,1)S(1)} %collective-permute-done.8.z_low) | copy-start | bytes 1105924
  127.7 4.2 %copy-start.4 = (bf16[12,40,384]{2,1,0:T(8,128)(2,1)}, bf16[12,40,384]{2,1,0:T(8,128)(2,1)S(1)}, u32[]{:S(2)}) copy-start(bf16[12,40,384]{2,1,0:T(8,128)(2,1)S(1)} %collective-permute-done.9.z_high) | copy-start | bytes 1105924
  127.7 4.2 %copy-start.11 = (f32[120,128]{1,0:T(8,128)}, f32[120,128]{1,0:T(8,128)S(1)}, u32[]{:S(2)}) copy-start(f32[120,128]{1,0:T(8,128)S(1)} %collective-permute-done.10.d_low) | copy-start | bytes 184324
  131.9 0.6 copy-start.12

commit v2 on v1

--- a/solution.py
+++ b/solution.py
@@ -1,5 +1,3 @@
-import functools
-
 import jax
 import jax.numpy as jnp
 from jax import lax
@@ -7,11 +5,13 @@
 from jax.experimental.pallas import tpu as pltpu
 from jax.sharding import PartitionSpec as P
 
+
 f32, bf16, i32 = jnp.float32, jnp.bfloat16, jnp.int32
 VM = pl.BlockSpec(memory_space=pltpu.VMEM)
 SM = pl.BlockSpec(memory_space=pltpu.SMEM)
 TIME_STEP = 0.02
 DAMPING = 0.3
+SCALE = 32000.0
 
 
 def iota(shape, dim):
@@ -34,7 +34,7 @@
     return level[0]
 
 
-def call(body, out_shape, in_specs, scratch=(), flops=0, nbytes=0):
+def call(body, out_shape, in_specs, scratch=(), flops=0, nbytes=0, vmem=24):
     outs = out_shape if isinstance(out_shape, list) else [out_shape]
     result = pl.pallas_call(
         body,
@@ -42,6 +42,7 @@
         in_specs=in_specs,
         out_specs=[VM] * len(outs),
         scratch_shapes=list(scratch),
+        compiler_params=pltpu.CompilerParams(vmem_limit_bytes=vmem << 20),
         cost_estimate=pl.CostEstimate(flops=flops, bytes_accessed=nbytes, transcendentals=0),
     )
     return result
@@ -60,19 +61,50 @@
         s = s[:, 0, :] + s[:, 1, :]
         s = s + pltpu.roll(s, 255, 1)
         rows.append((s * 0.125).astype(bf16))
-    out[0:96, :] = dot(jnp.concatenate(rows, axis=0), pick).astype(bf16)
+    coarse = dot(jnp.concatenate(rows, axis=0), pick).astype(bf16)
     cells = [mag[j].reshape(128, 256).astype(bf16) for j in range(3)]
     cells.append(grains[...].reshape(128, 256).astype(f32).astype(bf16))
     cells = jnp.concatenate(cells, axis=0)
-    k, lane = iota((16, 256), 0), iota((16, 256), 1)
-    edge = one_hot(((k < 3) & (lane == k)) | ((k >= 8) & (k < 11) & (lane == 245 + k)))
-    faces = dot(edge, cells, ((1,), (1,))).astype(bf16)
-    for q in range(4):
-        out[96 + 16 * q : 112 + 16 * q, :] = faces[:, 128 * q : 128 * (q + 1)]
-
-
-def toeplitz_kernel(kyp, kxr, strip, kx_out):
-    gx = lax.axis_index("gx")
+    k, lane = iota((8, 256), 0), iota((8, 256), 1)
+    edge = one_hot(((k < 3) & (lane == k)) | ((k >= 4) & (k < 7) & (lane == 249 + k)))
+    faces = dot(edge, cells, ((1,), (1,)))
+    faces = jnp.concatenate([faces[:, 128 * q : 128 * (q + 1)] for q in range(4)], axis=0).astype(bf16)
+    for d in range(8):
+        out[d, 0:96, :] = coarse
+        out[d, 96:128, :] = faces
+
+
+def toeplitz_kernel(kernel_x, kernel_y, kernel_z, mixing, strip, kx_out, wz_out, kyp):
+    gx, gz = lax.axis_index("gx"), lax.axis_index("gz")
+    kyp[...] = jnp.zeros_like(kyp)
+    kyp[:, 0:2048] = kernel_y[...].astype(f32)
+    kyp[...] = pltpu.roll(kyp[...], 64, 1)
+    mirror = one_hot(iota((256, 256), 0) + iota((256, 256), 1) == 255)
+    kxr = dot(kernel_x[...], mirror)
+    row, col = iota((64, 32), 0), iota((64, 32), 1)
+    level = 2 * (row // 8) + jnp.where(row % 8 >= 3, 1, 0) + 16 - 2 * gz
+    row, col8 = iota((8, 64), 0), iota((8, 64), 1)
+    total = jnp.zeros((64, 64), f32)
+    for zl in range(2):
+        per_rank = dot(one_hot(col == level - zl), kernel_z[...], ((1,), (1,)))
+        total = total + dot(per_rank.astype(bf16), one_hot((col8 // 8 == row) & (col8 % 8 < 6) & (col8 % 2 == zl)))
+    row, col = iota((64, 64), 0), iota((64, 64), 1)
+    i_of = jnp.where(row % 8 < 6, row % 8 % 3, 3)
+    rj_of = col // 2
+    mix = jnp.zeros((64, 64), f32)
+    for i in range(3):
+        line = jnp.zeros((1, 64), f32)
+        for r in range(8):
+            for j in range(3):
+                line = jnp.where(rj_of[0:1] == r * 4 + j, mixing[r, i * 3 + j], line)
+        mix = jnp.where(i_of == i, line, mix)
+    w = mix * total
+    hi = w.astype(bf16)
+    rest = w - hi.astype(f32)
+    mid = rest.astype(bf16)
+    wz_out[0:64] = hi
+    wz_out[64:128] = mid
+    wz_out[128:192] = (rest - mid.astype(f32)).astype(bf16)
 
     def one(r, carry):
         row = jnp.broadcast_to(kyp[pl.ds(r, 1), :], (128, 2176))
@@ -90,22 +122,19 @@
         kx_out[r * 24 : (r + 1) * 24, :] = total[:, :128]
 
 
-def faces_kernel(own, p7, r1, r2, r3, mag, grains, pay, face_a, rim, scr_a, scr_b):
+def faces_kernel(gathered, mag, grains, pay, face_a, rim, scr_a, scr_b):
     gx, gy = lax.axis_index("gx"), lax.axis_index("gy")
-    blocks = [own[0:96], r1[0:96], r2[0:96], r3[0:96], r3[96:192], r2[96:192], r1[96:192], p7[0:96]]
     for k in range(8):
-        pay[k * 96 : (k + 1) * 96, :] = blocks[k]
-
-    def faces(ref, base):
-        return jnp.concatenate([ref[base + 16 * q : base + 16 * (q + 1), :].astype(f32) for q in range(4)], axis=1)
-
-    f1, f3, f7 = faces(r1, 192), faces(r3, 192), faces(p7, 96)
-    even = (gy & 1) == 0
-    fb = jnp.where((gy == 3) | (gy == 4), f7, f3)
-    right, left = jnp.where(even, f1, fb), jnp.where(even, fb, f1)
-    sel = jnp.concatenate([right[0:8], left[8:16]], axis=0)
-    k, lane = iota((16, 128), 0), iota((16, 128), 1)
-    put = one_hot(((k < 3) & (lane == k)) | ((k >= 8) & (k < 11) & (lane == 117 + k)))
+        pay[k * 96 : (k + 1) * 96, :] = gathered[k, 0:96, :]
+
+    def faces(q):
+        rows = gathered[q, 96:128, :].astype(f32)
+        return jnp.concatenate([rows[8 * n : 8 * (n + 1)] for n in range(4)], axis=1)
+
+    right, left = faces(jnp.minimum(gy + 1, 7)), faces(jnp.maximum(gy - 1, 0))
+    sel = jnp.where(iota((8, 512), 0) < 4, right, left)
+    k, lane = iota((8, 128), 0), iota((8, 128), 1)
+    put = one_hot(((k < 3) & (lane == k)) | ((k >= 4) & (k < 7) & (lane == 121 + k)))
     unpacked = dot(sel.astype(bf16), put, ((0,), (0,)))
     rim[...] = unpacked.astype(bf16)
     odd = (gx & 1) == 1
@@ -149,7 +178,7 @@
                 high_out[(z - 1) * 4 + c] = whole
 
 
-def stages_kernel(own, r3, r4, r7, rc, kx, strip, wz, out, ax, ay):
+def stages_kernel(own, r3, r4, r7, rc, kx, strip, wz, packed, ax, ay, out):
     gy = lax.axis_index("gy")
     kxm = kx[...].astype(bf16)
 
@@ -174,7 +203,7 @@
         for kp in range(4):
             tiles = []
             for k in (2 * kp, 2 * kp + 1):
-                at = pl.multiple_of(128 * (8 + gy - (gy ^ k)), 128)
+                at = pl.multiple_of(128 * (8 + gy - k), 128)
                 tiles.append(strip[r, :, pl.ds(at, 256)])
             acc = acc + dot(ax[r, :, kp * 256 : (kp + 1) * 256].astype(bf16), jnp.concatenate(tiles, axis=0))
         acc = acc.astype(bf16).astype(f32)
@@ -195,14 +224,81 @@
             out[d, a * 6 : a * 6 + 6, :] = o[d * 8 : d * 8 + 6, :128]
     for d in range(8):
         out[d, 108:114, :] = rims[d * 8 : d * 8 + 6]
-        out[d, 114:120, :] = jnp.zeros((6, 128), f32)
+        values = out[d, 0:114, :]
+        peak = jnp.max(jnp.abs(values), axis=0, keepdims=True)
+        code = jnp.ceil(16.0 * jnp.log2(jnp.maximum(peak, 1e-30)))
+        scaled = values * (SCALE * jnp.exp2(code * -0.0625))
+        scaled = jnp.concatenate([scaled, jnp.broadcast_to(code, (6, 128))], axis=0)
+        packed[d] = jnp.round(scaled).astype(i32).astype(jnp.int16)
+
+
+def sum_kernel(parts, out):
+    total = jnp.zeros((114, 128), f32)
+    for d in range(8):
+        values = parts[d].astype(i32).astype(f32)
+        total = total + values[0:114] * (jnp.exp2(values[114:115] * 0.0625) * (1.0 / SCALE))
+    out[0:114] = total
+    out[114:120] = jnp.zeros((6, 128), f32)
+
+
+def weights_kernel(mag, grains, own_low, own_high, z_low, z_high, stiff, sat, m0, hh, wx, wy, wz, ss, aa):
+    gx, gy, gz = (lax.axis_index(n) for n in ("gx", "gy", "gz"))
+    row, col = iota((40, 384), 0), iota((40, 384), 1)
+    inside = ((row < 32) | ((row < 36) & (gx < 7)) | ((row >= 36) & (gx > 0))) & (
+        (col < 256) | ((col < 320) & (gy < 7)) | ((col >= 320) & (gy > 0))
+    )
+    for p in range(10):
+        z = p - 3
+        if z < 0:
+            whole = [z_low[p * 4 + c].astype(f32) for c in range(4)]
+            ok = gz > 0
+        elif z > 3:
+            whole = [z_high[(z - 4) * 4 + c].astype(f32) for c in range(4)]
+            ok = gz < 7
+        else:
+            ref, at = (own_low, z * 4) if z < 3 else (own_high, 8)
+            whole = [ref[at + c].astype(f32) for c in range(4)]
+            ok = gz >= 0
+        for c in range(3):
+            m0[c, p] = whole[c]
+            if 0 <= z < 4:
+                m0[c, p, 0:32, 0:256] = mag[c, z]
+        ids = whole[3].astype(i32)
+        aa[p] = jnp.where(inside & ok, lookup(ids, stiff), 0.0)
+        ss[p] = 2.0 / lookup(ids, sat)
+
+    def weight(u, v):
+        den = u + v
+        return 2.0 * u * v / jnp.where(den > 0.0, den, 1.0)
+
+    for p in range(10):
+        here = aa[p]
+        if 1 <= p <= 8:
+            wx[p] = weight(here, pltpu.roll(here, 39, 0))
+            wy[p] = weight(here, pltpu.roll(here, 383, 1))
+        if p < 9:
+            wz[p] = weight(here, aa[p + 1])
+
+    fz = [wz[0] * (m0[c, 1] - m0[c, 0]) for c in range(3)]
+    for p in range(1, 9):
+        for c in range(3):
+            total, fz[c] = exchange(m0, wx, wy, wz, c, p, fz[c])
+            hh[c, p - 1] = total * ss[p]
+
+
+def exchange(src, wx, wy, wz, c, p, below):
+    m = src[c, p]
+    flux = wx[p] * (pltpu.roll(m, 39, 0) - m)
+    total = flux - pltpu.roll(flux, 1, 0)
+    flux = wy[p] * (pltpu.roll(m, 383, 1) - m)
+    total = total + (flux - pltpu.roll(flux, 1, 1))
+    up = wz[p] * (src[c, p + 1] - m)
+    return total + (up - below), up
 
 
 def substeps_kernel(
-    mag, grains, own_low, own_high, z_low, z_high, d_own, d_low, d_high, stiff, two_over_sat,
-    state_out, demag_out, m0, m1, aa, wx, wy, wz, ss, fz, field, rows, spread,
+    m0, hh, wx, wy, wz, ss, d_own, d_low, d_high, state_out, demag_out, m1, m2, fz, field, rows, spread
 ):
-    gx, gy, gz = (lax.axis_index(n) for n in ("gx", "gy", "gz"))
     for q in range(6):
         demag_out[q // 3, q % 3] = d_own[pl.ds(6 + q, 16, stride=6), :]
     lane24 = iota((24, 128), 1)
@@ -233,60 +329,22 @@
         hi = v.astype(bf16)
         lo = (v - hi.astype(f32)).astype(bf16)
         field[g] = dot(tall, hi) + dot(tall, lo)
-    row, col = iota((40, 384), 0), iota((40, 384), 1)
-    inside = ((row < 32) | ((row < 36) & (gx < 7)) | ((row >= 36) & (gx > 0))) & (
-        (col < 256) | ((col < 320) & (gy < 7)) | ((col >= 320) & (gy > 0))
-    )
-    for p in range(10):
-        z = p - 3
-        if z < 0:
-            whole = [z_low[p * 4 + c].astype(f32) for c in range(4)]
-            ok = gz > 0
-        elif z > 3:
-            whole = [z_high[(z - 4) * 4 + c].astype(f32) for c in range(4)]
-            ok = gz < 7
-        else:
-            ref, at = (own_low, z * 4) if z < 3 else (own_high, 8)
-            whole = [ref[at + c].astype(f32) for c in range(4)]
-            ok = gz >= 0
-        for c in range(3):
-            m0[c, p] = whole[c]
-            if 0 <= z < 4:
-                m0[c, p, 0:32, 0:256] = mag[c, z]
-        ids = whole[3].astype(i32)
-        aa[p] = jnp.where(inside & ok, lookup(ids, stiff), 0.0)
-        ss[p] = lookup(ids, two_over_sat)
-
-    def weight(u, v):
-        den = u + v
-        return 2.0 * u * v / jnp.where(den > 0.0, den, 1.0)
-
-    for p in range(10):
-        here = aa[p]
-        if 1 <= p <= 8:
-            wx[p] = weight(here, pltpu.roll(here, 39, 0))
-            wy[p] = weight(here, pltpu.roll(here, 383, 1))
-        if p < 9:
-            wz[p] = weight(here, aa[p + 1])
     for step in range(3):
-        src, dst = (m0, m1) if step % 2 == 0 else (m1, m0)
+        src, dst = ((m0, m1), (m1, m2), (m2, None))[step]
         first, last = step + 1, 8 - step
 
         def plane(p, carry):
             m = [src[c, p] for c in range(3)]
-            w_up = wz[p]
-            sat = ss[p]
             level = (p - 1) // 2
             h = []
             for c in range(3):
-                flux = wx[p] * (pltpu.roll(m[c], 39, 0) - m[c])
-                total = flux - pltpu.roll(flux, 1, 0)
-                flux = wy[p] * (pltpu.roll(m[c], 383, 1) - m[c])
-                total = total + (flux - pltpu.roll(flux, 1, 1))
-                up = w_up * (src[c, p + 1] - m[c])
-                total = total + (up - fz[c])
-                fz[c] = up
-                h.append(total * sat + field[level * 3 + c])
+                if step == 0:
+                    total = hh[c, p - 1]
+                else:
+                    total, up = exchange(src, wx, wy, wz, c, p, fz[c])
+                    fz[c] = up
+                    total = total * ss[p]
+                h.append(total + field[level * 3 + c])
             t = [m[1] * h[2] - m[2] * h[1], m[2] * h[0] - m[0] * h[2], m[0] * h[1] - m[1] * h[0]]
             u = [m[1] * t[2] - m[2] * t[1], m[2] * t[0] - m[0] * t[2], m[0] * t[1] - m[1] * t[0]]
             raw = [m[c] - TIME_STEP * (t[c] + DAMPING * u[c]) for c in range(3)]
@@ -298,8 +356,9 @@
                     state_out[c, p - 3] = (raw[c] * scale)[0:32, 0:256]
             return carry
 
-        for c in range(3):
-            fz[c] = wz[first - 1] * (src[c, first] - src[c, first - 1])
+        if step:
+            for c in range(3):
+                fz[c] = wz[first - 1] * (src[c, first] - src[c, first - 1])
         lax.fori_loop(first, last + 1, plane, 0)
 
 
@@ -307,39 +366,28 @@
     return lax.ppermute(value, axis, [(i, i ^ bit) for i in range(8)])
 
 
-def z_weights(kernel_z, mixing):
-    gz = lax.axis_index("gz")
-    kz = kernel_z.astype(f32)
-    own = jnp.stack([lax.dynamic_slice_in_dim(kz, 16 - 2 * gz - zl, 16, 1) for zl in range(2)])
-    own = own.reshape(2, 8, 8, 2)
-    w = jnp.einsum("rij,zrda->dairjz", mixing, own, precision=lax.Precision.HIGHEST).reshape(8, 6, 8, 6)
-    w = jnp.pad(w, ((0, 0), (0, 2), (0, 0), (0, 2))).reshape(64, 64)
-    hi = lax.reduce_precision(w, 8, 7)
-    mid = lax.reduce_precision(w - hi, 8, 7)
-    return jnp.concatenate([hi, mid, w - hi - mid], axis=0).astype(bf16)
-
-
 def local(magnet, grains, stiffness_table, saturation_table, kernel_x, kernel_y, kernel_z, mixing):
     shape = jax.ShapeDtypeStruct
-    (pay0,) = call(
-        coarse_kernel, shape((160, 128), bf16), [VM, VM, SM], [pltpu.VMEM((6, 32, 256), f32)], 20_000_000, 600_000
+    (pay_y,) = call(
+        coarse_kernel, shape((8, 128, 128), bf16), [VM, VM, SM], [pltpu.VMEM((6, 32, 256), f32)], 20_000_000, 600_000
     )(magnet, grains, saturation_table)
-    kyp = jnp.pad(kernel_y.astype(f32), ((0, 0), (64, 64)))
-    strip, kx = call(
-        toeplitz_kernel, [shape((8, 128, 2176), bf16), shape((192, 128), f32)], [VM, VM], (), 20_000_000, 5_000_000
-    )(kyp, kernel_x[:, ::-1].astype(f32))
-    wz = z_weights(kernel_z, mixing)
-    p7 = swap(pay0, "gy", 7)
-    pay_y = jnp.concatenate([pay0[:96], p7[:96], pay0[96:]], axis=0)
-    r1, r2, r3 = (swap(pay_y, "gy", k) for k in (1, 2, 3))
+    gathered = lax.all_to_all(pay_y, "gy", 0, 0, tiled=True)
+    strip, kx, wz = call(
+        toeplitz_kernel,
+        [shape((8, 128, 2176), bf16), shape((192, 128), f32), shape((192, 64), bf16)],
+        [VM, VM, VM, SM],
+        [pltpu.VMEM((8, 2176), f32)],
+        20_000_000,
+        5_000_000,
+    )(kernel_x, kernel_y, kernel_z, mixing.reshape(8, 9))
     pay_x, face_a, rim = call(
         faces_kernel,
         [shape((912, 128), bf16), shape((144, 128), bf16), shape((512, 128), bf16)],
-        [VM] * 7,
+        [VM] * 3,
         [pltpu.VMEM((144, 128), f32)] * 2,
         1_000_000,
         1_000_000,
-    )(pay0, p7, r1, r2, r3, magnet, grains)
+    )(gathered, magnet, grains)
     x3, x4, x7 = (swap(pay_x, "gx", k) for k in (3, 4, 7))
     pay_c = jnp.concatenate([pay_x[:768], x3[:768], x4[:768], x7[:768], face_a], axis=0)
     rc = swap(pay_c, "gx", 1)
@@ -357,27 +405,35 @@
     z_high = lax.ppermute(own_low, "gz", down)
     (parts,) = call(
         stages_kernel,
-        shape((8, 120, 128), f32),
+        shape((8, 120, 128), jnp.int16),
         [VM] * 8,
-        [pltpu.VMEM((8, 144, 1024), f32), pltpu.VMEM((18, 64, 256), f32)],
+        [pltpu.VMEM((8, 144, 1024), f32), pltpu.VMEM((18, 64, 256), f32), pltpu.VMEM((8, 120, 128), f32)],
         2_000_000_000,
         10_000_000,
     )(pay_x, x3, x4, x7, rc, kx, strip, wz)
-    d_own = jnp.sum(lax.all_to_all(parts, "gz", 0, 0, tiled=True), axis=0)
+    parts = lax.all_to_all(parts, "gz", 0, 0, tiled=True)
+    big = (10, 40, 384)
+    m0, hh, wx, wy, wz, ss = call(
+        weights_kernel,
+        [shape((3,) + big, f32), shape((3, 8, 40, 384), f32)] + [shape(big, f32)] * 4,
+        [VM] * 6 + [SM] * 2,
+        [pltpu.VMEM(big, f32)],
+        20_000_000,
+        5_000_000,
+    )(magnet, grains, own_low, own_high, z_low, z_high, stiffness_table, saturation_table)
+    (d_own,) = call(sum_kernel, shape((120, 128), f32), [VM], (), 100_000, 300_000)(parts)
     d_low = lax.ppermute(d_own, "gz", up)
     d_high = lax.ppermute(d_own, "gz", down)
-    big = (10, 40, 384)
     state, demag = call(
         substeps_kernel,
         [shape((3, 4, 32, 256), f32), shape((2, 3, 16, 128), f32)],
-        [VM] * 9 + [SM] * 2,
+        [VM] * 9,
         [pltpu.VMEM((3,) + big, f32)] * 2
-        + [pltpu.VMEM(big, f32)] * 5
         + [pltpu.VMEM((3, 40, 384), f32), pltpu.VMEM((12, 40, 384), f32)]
         + [pltpu.VMEM((288, 256), f32), pltpu.VMEM((288, 384), f32)],
         50_000_000,
         5_000_000,
-    )(magnet, grains, own_low, own_high, z_low, z_high, d_own, d_low, d_high, stiffness_table, 2.0 / saturation_table)
+    )(m0, hh, wx, wy, wz, ss, d_own, d_low, d_high)
     return (state, demag)
 
 

time: 143 us -> 120 us (0.84)
  the two profiles are of different devices: /device:TPU:2 before, /device:TPU:32 now
where the time goes in v2:
time: 120 us
  blocking collectives  41 us (34%)
  starting transfers between devices  29.3 us (24%)
  Pallas kernels  22.5 us (19%)
  waiting for transfers between devices  20.4 us (17%)
  local copies, waits for them, and re-layouts  6.04 us (5%)
    all_to_all x1, blocking collectives, local(): gathered = lax.all_to_all(pay_y, 'gy', 0, 0, tiled=True)  41 us
    ppermute x4, starting transfers between devices, swap(): return lax.ppermute(value, axis, [(i, i ^ bit) for i in range(8)])  11.9 us
    all_to_all x1, waiting for transfers between devices, local(): parts = lax.all_to_all(parts, 'gz', 0, 0, tiled=True)  10.9 us
    ppermute x4, waiting for transfers between devices, swap(): return lax.ppermute(value, axis, [(i, i ^ bit) for i in range(8)])  9.43 us
    pallas_call x1, Pallas kernels, local(): call(stages_kernel, shape((8, 120, 128), jnp.int16), [VM] * 8, [pltpu.VME...  7.91 us
    all_to_all x1, starting transfers between devices, local(): parts = lax.all_to_all(parts, 'gz', 0, 0, tiled=True)  5.69 us
    pallas_call x1, Pallas kernels, local(): call(substeps_kernel, [shape((3, 4, 32, 256), f32), shape((2, 3, 16, 128)...  5.49 us
    unnamed x26, local copies, waits for them, and re-layouts  5.34 us
  transfers between devices with their start and end apart: 9, of which 3 were waited for; matrix products, arithmetic and copies ran while one was open for 2% of the time, Pallas kernels for 7%

profile of v2, /device:TPU:32, one launch (start us, length us, event | category | flops | bytes accessed | tf_op | source)
XLA Modules:
  0.0 119.9 jit_solution(14754373358497843167)
XLA Ops:
  0.6 0.0 copy-start
  0.6 1.0 copy-done
  1.6 0.0 copy-start.2
  1.6 0.9 copy-done.2
  2.5 0.7 copy-done.4
  3.2 1.0 shard_map.95
  4.2 41.0 %all_to_all.10.gathered = bf16[8,128,128]{2,1,0:T(8,128)(2,1)S(1)} all-to-all(bf16[8,128,128]{2,1,0:T(8,128)(2,1)S(1)} %shard_map.95), channel_id=1, replica_groups=mesh['gx'=8,'gy'=8,'gz'=8] {'gy'}, dimensions={0} | all-to-all | bytes 524288 | tf_op jit(solution)/shard_map/all_to_all | solution.py:374
  45.1 0.2 shard_map.96
  45.4 1.9 %collective-permute-start = (bf16[912,128]{1,0:T(8,128)(2,1)S(1)}, bf16[912,128]{1,0:T(8,128)(2,1)S(1)}, u32[]{:S(2)}, u32[]{:S(2)}) collective-permute-start(bf16[912,128]{1,0:T(8,128)(2,1)S(1)} %get-tuple-element.17.own), channel_id=1, source_target_pairs={{0,192},{64,128},{128,64},{192,0},{256,448},{320,384},{384,320},{4... | collective-permute-start | bytes 700424 | tf_op jit(solution)/shard_map/ppermute | solution.py:366
  47.3 4.9 %collective-permute-start.1 = (bf16[912,128]{1,0:T(8,128)(2,1)S(1)}, bf16[912,128]{1,0:T(8,128)(2,1)S(1)}, u32[]{:S(2)}, u32[]{:S(2)}) collective-permute-start(bf16[912,128]{1,0:T(8,128)(2,1)S(1)} %get-tuple-element.17.own), channel_id=1, source_target_pairs={{0,256},{64,320},{128,384},{192,448},{256,0},{320,64},{384,128},{4... | collective-permute-start | bytes 700424 | tf_op jit(solution)/shard_map/ppermute | solution.py:366
  52.3 3.0 %collective-permute-start.2 = (bf16[912,128]{1,0:T(8,128)(2,1)S(1)}, bf16[912,128]{1,0:T(8,128)(2,1)S(1)}, u32[]{:S(2)}, u32[]{:S(2)}) collective-permute-start(bf16[912,128]{1,0:T(8,128)(2,1)S(1)} %get-tuple-element.17.own), channel_id=1, source_target_pairs={{0,448},{64,384},{128,320},{192,256},{256,192},{320,128},{384,64},... | collective-permute-start | bytes 700424 | tf_op jit(solution)/shard_map/ppermute | solution.py:366
  55.3 0.7 slice_dynamic-update-slice_fusion.3
  56.0 0.0 collective-permute-done.r3
  56.0 0.7 slice_dynamic-update-slice_fusion.2
  56.7 4.7 %collective-permute-done.1.r4 = bf16[912,128]{1,0:T(8,128)(2,1)S(1)} collective-permute-done((bf16[912,128]{1,0:T(8,128)(2,1)S(1)}, bf16[912,128]{1,0:T(8,128)(2,1)S(1)}, u32[]{:S(2)}, u32[]{:S(2)}) %collective-permute-start.1) | collective-permute-done | bytes 233504 | tf_op jit(solution)/shard_map/ppermute | solution.py:366
  61.3 0.7 slice_dynamic-update-slice_fusion.1
  62.0 4.7 %collective-permute-done.2.r7 = bf16[912,128]{1,0:T(8,128)(2,1)S(1)} collective-permute-done((bf16[912,128]{1,0:T(8,128)(2,1)S(1)}, bf16[912,128]{1,0:T(8,128)(2,1)S(1)}, u32[]{:S(2)}, u32[]{:S(2)}) %collective-permute-start.2) | collective-permute-done | bytes 233504 | tf_op jit(solution)/shard_map/ppermute | solution.py:366
  66.8 0.7 slice_dynamic-update-slice_fusion
  67.5 0.6 constant_dynamic-update-slice_fusion
  68.1 2.0 %collective-permute-start.3 = (bf16[3216,128]{1,0:T(8,128)(2,1)}, bf16[3216,128]{1,0:T(8,128)(2,1)S(1)}, u32[]{:S(2)}, u32[]{:S(2)}) collective-permute-start(bf16[3216,128]{1,0:T(8,128)(2,1)} %constant_dynamic-update-slice_fusion), channel_id=1, source_target_pairs={{0,64},{64,0},{128,192},{192,128},{256,320},{320,256},{384,448},{4... | collective-permute-start | bytes 2469896 | tf_op jit(solution)/shard_map/ppermute | solution.py:366
  70.1 0.0 copy-done.10
  70.1 0.1 copy.11.mixing
  70.2 0.0 copy-done.7
  70.2 0.0 copy-done.8
  70.2 0.0 copy-done.9
  70.2 3.6 %shard_map.99 = (bf16[8,128,2176]{2,1,0:T(8,128)(2,1)S(1)}, f32[192,128]{1,0:T(8,128)S(1)}, bf16[192,64]{1,0:T(8,128)(2,1)S(1)}) custom-call(bf16[8,256]{1,0:T(8,128)(2,1)S(1)} %copy-done.8, bf16[8,2048]{1,0:T(8,128)(2,1)S(1)} %copy-done.7, bf16[8,32]{1,0:T(8,128)(2,1)S(1)} %copy-done.9, f32[8,9]{1,0:T(8,128)S(1)} %copy.11.mixing), custom_call_target="tpu_custom_call" | custom-call | flops 20000000 | bytes 5000000 | tf_op jit(solution)/shard_map/pallas_call | solution.py:375
  73.8 0.0 collective-permute-done.3.rc
  73.8 0.0 copy-start.1
  73.8 0.0 copy-start.3
  73.8 7.9 %shard_map.100 = s16[8,120,128]{2,1,0:T(8,128)(2,1)} custom-call(bf16[912,128]{1,0:T(8,128)(2,1)S(1)} %get-tuple-element.17.own, bf16[912,128]{1,0:T(8,128)(2,1)S(1)} %collective-permute-done.r3, bf16[912,128]{1,0:T(8,128)(2,1)S(1)} %collective-permute-done.1.r4, bf16[912,128]{1,0:T(8,128)(2,1)S(1)} %collective-permute-done.2.r7, ...), custom_call_target="tpu_custom_call" | custom-call | flops 2000000000 | bytes 10000000 | tf_op jit(solution)/shard_map/pallas_call | solution.py:406
  81.7 5.7 %all-to-all-start.1 = ((s16[8,120,128]{2,1,0:T(8,128)(2,1)}), s16[8,120,128]{2,1,0:T(8,128)(2,1)S(1)}, u32[]{:S(2)}, u32[]{:S(2)}) async-start(s16[8,120,128]{2,1,0:T(8,128)(2,1)} %shard_map.100), calls=%async_computation.1 | async-start | bytes 491520 | tf_op jit(solution)/shard_map/all_to_all | solution.py:414
  87.4 0.0 copy-done.1
  87.4 0.0 copy-done.3
  87.4 0.2 shard_map.97
  87.6 3.4 %collective-permute-start.4 = (bf16[12,40,384]{2,1,0:T(8,128)(2,1)S(1)}, bf16[12,40,384]{2,1,0:T(8,128)(2,1)S(1)}, u32[]{:S(2)}, u32[]{:S(2)}) collective-permute-start(bf16[12,40,384]{2,1,0:T(8,128)(2,1)S(1)} %get-tuple-element.20.own_high), channel_id=1, source_target_pairs={{0,1},{1,2},{2,3},{3,4},{4,5},{5,6},{6,7},{8,9},{9,10},{10,11},{11... | collective-permute-start | bytes 1105928 | tf_op jit(solution)/shard_map/ppermute | solution.py:404
  91.0 2.5 %collective-permute-start.5 = (bf16[12,40,384]{2,1,0:T(8,128)(2,1)S(1)}, bf16[12,40,384]{2,1,0:T(8,128)(2,1)S(1)}, u32[]{:S(2)}, u32[]{:S(2)}) collective-permute-start(bf16[12,40,384]{2,1,0:T(8,128)(2,1)S(1)} %get-tuple-element.19.own_low), channel_id=1, source_target_pairs={{1,0},{2,1},{3,2},{4,3},{5,4},{6,5},{7,6},{9,8},{10,9},{11,10},{12... | collective-permute-start | bytes 1105928 | tf_op jit(solution)/shard_map/ppermute | solution.py:405
  93.5 10.9 %all-to-all-done.1.parts = s16[8,120,128]{2,1,0:T(8,128)(2,1)S(1)} async-done(((s16[8,120,128]{2,1,0:T(8,128)(2,1)}), s16[8,120,128]{2,1,0:T(8,128)(2,1)S(1)}, u32[]{:S(2)}, u32[]{:S(2)}) %all-to-all-start.1) | async-done | bytes 245792 | tf_op jit(solution)/shard_map/all_to_all | solution.py:414
  104.4 0.1 shard_map.101.d_own
  104.5 1.9 %collective-permute-start.6 = (f32[120,128]{1,0:T(8,128)S(1)}, f32[120,128]{1,0:T(8,128)S(1)}, u32[]{:S(2)}, u32[]{:S(2)}) collective-permute-start(f32[120,128]{1,0:T(8,128)S(1)} %shard_map.101.d_own), channel_id=1, source_target_pairs={{0,1},{1,2},{2,3},{3,4},{4,5},{5,6},{6,7},{8,9},{9,10},{10,11},{11... | collective-permute-start | bytes 184328 | tf_op jit(solution)/shard_map/ppermute | solution.py:425
  106.4 3.9 %collective-permute-start.7 = (f32[120,128]{1,0:T(8,128)S(1)}, f32[120,128]{1,0:T(8,128)S(1)}, u32[]{:S(2)}, u32[]{:S(2)}) collective-permute-start(f32[120,128]{1,0:T(8,128)S(1)} %shard_map.101.d_own), channel_id=1, source_target_pairs={{1,0},{2,1},{3,2},{4,3},{5,4},{6,5},{7,6},{9,8},{10,9},{11,10},{12... | collective-permute-start | bytes 184328 | tf_op jit(solution)/shard_map/ppermute | solution.py:426
  110.3 0.0 collective-permute-done.4.z_low
  110.3 0.0 collective-permute-done.5.z_high
  110.4 0.0 copy-done.5
  110.4 0.0 copy-done.6
  110.4 4.0 %shard_map.98 = (f32[3,10,40,384]{3,2,1,0:T(8,128)S(1)}, f32[3,8,40,384]{3,2,1,0:T(8,128)S(1)}, f32[10,40,384]{2,1,0:T(8,128)S(1)}, f32[10,40,384]{2,1,0:T(8,128...) custom-call(f32[3,4,32,256]{3,2,1,0:T(8,128)S(1)} %copy-done.1, s32[4,32,256]{2,1,0:T(8,128)S(1)} %copy-done.3, ...), custom_call_target="tpu_custom_call" | custom-call | flops 20000000 | bytes 5000000 | tf_op jit(solution)/shard_map/pallas_call | solution.py:416
  114.4 0.0 collective-permute-done.6.d_low
  114.4 0.0 collective-permute-done.7.d_high
  114.4 5.5 %shard_map.102 = (f32[3,4,32,256]{3,2,1,0:T(8,128)}, f32[2,3,16,128]{3,2,1,0:T(8,128)}) custom-call(f32[3,10,40,384]{3,2,1,0:T(8,128)S(1)} %get-tuple-element.21.m0, f32[3,8,40,384]{3,2,1,0:T(8,128)S(1)} %get-tuple-element.22.hh, f32[10,40,384]{2,1,0:T(8,128)S(1)} %get-tuple-element.23.wx, f32[10,40,384]{2,1,0:T(8,128)S(1)} %get-tuple-element.24.wy, ...), custom_call_target="tpu_custom_call" | custom-call | flops 50000000 | bytes 5000000 | tf_op jit(solution)/shard_map/pallas_call | solution.py:427
  (8 shorter events, 0.0 us)
Async XLA Ops:
  0.6 1.0 copy-start
  1.6 0.9 copy-start.2
  2.5 0.7 copy-start.4
  3.2 66.9 %copy-start.10 = (f32[8,3,3]{0,2,1:T(4,128)S(1)}, f32[8,3,3]{0,2,1:T(4,128)}, u32[]{:S(2)}) copy-start(f32[8,3,3]{0,2,1:T(4,128)} %param.15) | copy-start | bytes 868
  3.2 67.0 %copy-start.7 = (bf16[8,2048]{1,0:T(8,128)(2,1)S(1)}, bf16[8,2048]{1,0:T(8,128)(2,1)}, u32[]{:S(2)}) copy-start(bf16[8,2048]{1,0:T(8,128)(2,1)} %kernel_y.1) | copy-start | bytes 98308
  3.2 67.0 %copy-start.8 = (bf16[8,256]{1,0:T(8,128)(2,1)S(1)}, bf16[8,256]{1,0:T(8,128)(2,1)}, u32[]{:S(2)}) copy-start(bf16[8,256]{1,0:T(8,128)(2,1)} %kernel_x.1) | copy-start | bytes 12292
  3.2 67.0 %copy-start.9 = (bf16[8,32]{1,0:T(8,128)(2,1)S(1)}, bf16[8,32]{1,0:T(8,128)(2,1)}, u32[]{:S(2)}) copy-start(bf16[8,32]{1,0:T(8,128)(2,1)} %kernel_z.1) | copy-start | bytes 1540
  45.4 10.6 %collective-permute-start = (bf16[912,128]{1,0:T(8,128)(2,1)S(1)}, bf16[912,128]{1,0:T(8,128)(2,1)S(1)}, u32[]{:S(2)}, u32[]{:S(2)}) collective-permute-start(bf16[912,128]{1,0:T(8,128)(2,1)S(1)} %get-tuple-element.17.own), channel_id=1, source_target_pairs={{0,192},{64,128},{128,64},{192,0},{256,448},{320,384},{384,320},{4... | collective-permute-start | bytes 700424 | tf_op jit(solution)/shard_map/ppermute | solution.py:366
  47.3 14.0 %collective-permute-start.1 = (bf16[912,128]{1,0:T(8,128)(2,1)S(1)}, bf16[912,128]{1,0:T(8,128)(2,1)S(1)}, u32[]{:S(2)}, u32[]{:S(2)}) collective-permute-start(bf16[912,128]{1,0:T(8,128)(2,1)S(1)} %get-tuple-element.17.own), channel_id=1, source_target_pairs={{0,256},{64,320},{128,384},{192,448},{256,0},{320,64},{384,128},{4... | collective-permute-start | bytes 700424 | tf_op jit(solution)/shard_map/ppermute | solution.py:366
  52.3 14.5 %collective-permute-start.2 = (bf16[912,128]{1,0:T(8,128)(2,1)S(1)}, bf16[912,128]{1,0:T(8,128)(2,1)S(1)}, u32[]{:S(2)}, u32[]{:S(2)}) collective-permute-start(bf16[912,128]{1,0:T(8,128)(2,1)S(1)} %get-tuple-element.17.own), channel_id=1, source_target_pairs={{0,448},{64,384},{128,320},{192,256},{256,192},{320,128},{384,64},... | collective-permute-start | bytes 700424 | tf_op jit(solution)/shard_map/ppermute | solution.py:366
  68.1 5.7 %collective-permute-start.3 = (bf16[3216,128]{1,0:T(8,128)(2,1)}, bf16[3216,128]{1,0:T(8,128)(2,1)S(1)}, u32[]{:S(2)}, u32[]{:S(2)}) collective-permute-start(bf16[3216,128]{1,0:T(8,128)(2,1)} %constant_dynamic-update-slice_fusion), channel_id=1, source_target_pairs={{0,64},{64,0},{128,192},{192,128},{256,320},{320,256},{384,448},{4... | collective-permute-start | bytes 2469896 | tf_op jit(solution)/shard_map/ppermute | solution.py:366
  73.8 13.6 %copy-start.1 = (f32[3,4,32,256]{3,2,1,0:T(8,128)S(1)}, f32[3,4,32,256]{3,2,1,0:T(8,128)}, u32[]{:S(2)}) copy-start(f32[3,4,32,256]{3,2,1,0:T(8,128)} %mag.7) | copy-start | bytes 1179652
  73.8 13.6 %copy-start.3 = (s32[4,32,256]{2,1,0:T(8,128)S(1)}, s32[4,32,256]{2,1,0:T(8,128)}, u32[]{:S(2)}) copy-start(s32[4,32,256]{2,1,0:T(8,128)} %grains.7) | copy-start | bytes 393220
  81.7 28.6 %copy-start.5 = (f32[16]{0:T(128)S(1)}, f32[16]{0:T(128)}, u32[]{:S(2)}) copy-start(f32[16]{0:T(128)} %sat.3) | copy-start | bytes 196
  81.7 28.6 %copy-start.6 = (f32[16]{0:T(128)S(1)}, f32[16]{0:T(128)}, u32[]{:S(2)}) copy-start(f32[16]{0:T(128)} %stiff.1) | copy-start | bytes 196
  81.7 22.7 %all-to-all-start.1 = ((s16[8,120,128]{2,1,0:T(8,128)(2,1)}), s16[8,120,128]{2,1,0:T(8,128)(2,1)S(1)}, u32[]{:S(2)}, u32[]{:S(2)}) async-start(s16[8,120,128]{2,1,0:T(8,128)(2,1)} %shard_map.100), calls=%async_computation.1 | async-start | bytes 491520 | tf_op jit(solution)/shard_map/all_to_all | solution.py:414
  87.6 22.7 %collective-permute-start.4 = (bf16[12,40,384]{2,1,0:T(8,128)(2,1)S(1)}, bf16[12,40,384]{2,1,0:T(8,128)(2,1)S(1)}, u32[]{:S(2)}, u32[]{:S(2)}) collective-permute-start(bf16[12,40,384]{2,1,0:T(8,128)(2,1)S(1)} %get-tuple-element.20.own_high), channel_id=1, source_target_pairs={{0,1},{1,2},{2,3},{3,4},{4,5},{5,6},{6,7},{8,9},{9,10},{10,11},{11... | collective-permute-start | bytes 1105928 | tf_op jit(solution)/shard_map/ppermute | solution.py:404
  91.0 19.4 %collective-permute-start.5 = (bf16[12,40,384]{2,1,0:T(8,128)(2,1)S(1)}, bf16[12,40,384]{2,1,0:T(8,128)(2,1)S(1)}, u32[]{:S(2)}, u32[]{:S(2)}) collective-permute-start(bf16[12,40,384]{2,1,0:T(8,128)(2,1)S(1)} %get-tuple-element.19.own_low), channel_id=1, source_target_pairs={{1,0},{2,1},{3,2},{4,3},{5,4},{6,5},{7,6},{9,8},{10,9},{11,10},{12... | collective-permute-start | bytes 1105928 | tf_op jit(solution)/shard_map/ppermute | solution.py:405
  104.5 10.0 %collective-permute-start.6 = (f32[120,128]{1,0:T(8,128)S(1)}, f32[120,128]{1,0:T(8,128)S(1)}, u32[]{:S(2)}, u32[]{:S(2)}) collective-permute-start(f32[120,128]{1,0:T(8,128)S(1)} %shard_map.101.d_own), channel_id=1, source_target_pairs={{0,1},{1,2},{2,3},{3,4},{4,5},{5,6},{6,7},{8,9},{9,10},{10,11},{11... | collective-permute-start | bytes 184328 | tf_op jit(solution)/shard_map/ppermute | solution.py:425
  106.4 8.0 %collective-permute-start.7 = (f32[120,128]{1,0:T(8,128)S(1)}, f32[120,128]{1,0:T(8,128)S(1)}, u32[]{:S(2)}, u32[]{:S(2)}) collective-permute-start(f32[120,128]{1,0:T(8,128)S(1)} %shard_map.101.d_own), channel_id=1, source_target_pairs={{1,0},{2,1},{3,2},{4,3},{5,4},{6,5},{7,6},{9,8},{10,9},{11,10},{12... | collective-permute-start | bytes 184328 | tf_op jit(solution)/shard_map/ppermute | solution.py:426

commit v3 on v2

--- a/solution.py
+++ b/solution.py
@@ -9,9 +9,11 @@
 f32, bf16, i32 = jnp.float32, jnp.bfloat16, jnp.int32
 VM = pl.BlockSpec(memory_space=pltpu.VMEM)
 SM = pl.BlockSpec(memory_space=pltpu.SMEM)
+HB = pl.BlockSpec(memory_space=pltpu.MemorySpace.HBM)
 TIME_STEP = 0.02
 DAMPING = 0.3
 SCALE = 32000.0
+FULL = 67_043_328
 
 
 def iota(shape, dim):
@@ -34,7 +36,7 @@
     return level[0]
 
 
-def call(body, out_shape, in_specs, scratch=(), flops=0, nbytes=0, vmem=24):
+def call(body, out_shape, in_specs, scratch=(), flops=0, nbytes=0, vmem=None):
     outs = out_shape if isinstance(out_shape, list) else [out_shape]
     result = pl.pallas_call(
         body,
@@ -42,13 +44,13 @@
         in_specs=in_specs,
         out_specs=[VM] * len(outs),
         scratch_shapes=list(scratch),
-        compiler_params=pltpu.CompilerParams(vmem_limit_bytes=vmem << 20),
+        compiler_params=pltpu.CompilerParams(vmem_limit_bytes=vmem),
         cost_estimate=pl.CostEstimate(flops=flops, bytes_accessed=nbytes, transcendentals=0),
     )
     return result
 
 
-def coarse_kernel(mag, grains, sat, out, scr):
+def coarse_kernel(mag, grains, sat, out, edges, cells_out, scr):
     for a in range(2):
         s0 = lookup(grains[2 * a], sat)
         s1 = lookup(grains[2 * a + 1], sat)
@@ -69,9 +71,22 @@
     edge = one_hot(((k < 3) & (lane == k)) | ((k >= 4) & (k < 7) & (lane == 249 + k)))
     faces = dot(edge, cells, ((1,), (1,)))
     faces = jnp.concatenate([faces[:, 128 * q : 128 * (q + 1)] for q in range(4)], axis=0).astype(bf16)
-    for d in range(8):
-        out[d, 0:96, :] = coarse
-        out[d, 96:128, :] = faces
+    out[0:96, :] = coarse
+    out[96:128, :] = faces
+    cells_out[...] = cells
+    for c in range(4):
+        for z in range(4):
+            at = (c * 4 + z) * 3
+            plane = mag[c, z] if c < 3 else grains[z].astype(f32)
+            edges[0, at : at + 3, :] = plane[0:3]
+            edges[1, at : at + 3, :] = plane[29:32]
+
+
+def pair_kernel(own, other, out):
+    for n in range(4):
+        out[n, 0:96, :] = own[0:96]
+        out[n, 96:192, :] = other[0:96]
+        out[n, 192:224, :] = own[96:128]
 
 
 def toeplitz_kernel(kernel_x, kernel_y, kernel_z, mixing, strip, kx_out, wz_out, kyp):
@@ -117,54 +132,59 @@
         row = pltpu.roll(jnp.broadcast_to(kxr[r : r + 1, :], (24, 256)), 0, 1, stride=1, stride_axis=0)
         total = jnp.zeros((24, 256), f32)
         for l in range(8):
-            shift = (16 * l + 16 * (gx - (gx ^ l)) + 128 + 512) & 255
+            block = 2 * (l % 4) + ((gx & 1) if l < 4 else 1 - (gx & 1))
+            shift = (16 * l + 16 * (gx - block) + 128 + 512) & 255
             total = jnp.where(lane // 16 == l, pltpu.roll(row, shift, 1), total)
         kx_out[r * 24 : (r + 1) * 24, :] = total[:, :128]
 
 
-def faces_kernel(gathered, mag, grains, pay, face_a, rim, scr_a, scr_b):
+def faces_kernel(gathered, other, edges, pay, face_a, rim, low, high):
     gx, gy = lax.axis_index("gx"), lax.axis_index("gy")
-    for k in range(8):
-        pay[k * 96 : (k + 1) * 96, :] = gathered[k, 0:96, :]
-
-    def faces(q):
-        rows = gathered[q, 96:128, :].astype(f32)
+    y = gy & 3
+
+    def faces(rows):
         return jnp.concatenate([rows[8 * n : 8 * (n + 1)] for n in range(4)], axis=1)
 
-    right, left = faces(jnp.minimum(gy + 1, 7)), faces(jnp.maximum(gy - 1, 0))
+    across = faces(other[96:128, :].astype(f32))
+    right = faces(gathered[jnp.minimum(y + 1, 3), 192:224, :].astype(f32))
+    left = faces(gathered[jnp.maximum(y - 1, 0), 192:224, :].astype(f32))
+    right = jnp.where(gy == 3, across, right)
+    left = jnp.where(gy == 4, across, left)
     sel = jnp.where(iota((8, 512), 0) < 4, right, left)
     k, lane = iota((8, 128), 0), iota((8, 128), 1)
     put = one_hot(((k < 3) & (lane == k)) | ((k >= 4) & (k < 7) & (lane == 121 + k)))
     unpacked = dot(sel.astype(bf16), put, ((0,), (0,)))
     rim[...] = unpacked.astype(bf16)
+    for n in range(16):
+        low[3 * n : 3 * n + 3] = unpacked[32 * n : 32 * n + 3]
+        high[3 * n : 3 * n + 3] = unpacked[32 * n + 29 : 32 * n + 32]
     odd = (gx & 1) == 1
-    for c in range(4):
-        for z in range(4):
-            plane = (c * 4 + z) * 32
-            low = mag[c, z, 0:8, :] if c < 3 else grains[z, 0:8, :].astype(f32)
-            high = mag[c, z, 24:32, :] if c < 3 else grains[z, 24:32, :].astype(f32)
-            low = jnp.concatenate([low, unpacked[plane : plane + 8]], axis=1)[0:3]
-            high = jnp.concatenate([high, unpacked[plane + 24 : plane + 32]], axis=1)[5:8]
-            to_b, to_a = jnp.where(odd, high, low), jnp.where(odd, low, high)
-            for q in range(3):
-                at = q * 48 + (c * 4 + z) * 3
-                scr_b[at : at + 3, :] = to_b[:, q * 128 : (q + 1) * 128]
-                scr_a[at : at + 3, :] = to_a[:, q * 128 : (q + 1) * 128]
-    pay[768:912, :] = scr_b[...].astype(bf16)
-    face_a[...] = scr_a[...].astype(bf16)
-
-
-def rims_kernel(mag, grains, rim, rc, r3, r7, low_out, high_out, scr, fa, fb):
+    to_b = [jnp.where(odd, edges[1], edges[0]).astype(bf16), jnp.where(odd, high[...], low[...]).astype(bf16)]
+    to_a = [jnp.where(odd, edges[0], edges[1]).astype(bf16), jnp.where(odd, low[...], high[...]).astype(bf16)]
+    face_a[0:48, :] = to_a[0][:, :128]
+    face_a[48:96, :] = to_a[0][:, 128:]
+    face_a[96:144, :] = to_a[1]
+    for n in range(4):
+        for k in range(4):
+            pay[n, k * 96 : (k + 1) * 96, :] = gathered[k, 0:96, :]
+            pay[n, (k + 4) * 96 : (k + 5) * 96, :] = gathered[k, 96:192, :]
+        pay[n, 768:816, :] = to_b[0][:, :128]
+        pay[n, 816:864, :] = to_b[0][:, 128:]
+        pay[n, 864:912, :] = to_b[1]
+
+
+def rims_kernel(cells, rim, near, rc, low_out, high_out, scr, fa, fb):
     gx = lax.axis_index("gx")
     even = (gx & 1) == 0
-    a = rc[3072:3216, :].astype(f32)
-    b = jnp.where((gx == 3) | (gx == 4), r7[768:912, :].astype(f32), r3[768:912, :].astype(f32))
+    chip = gx // 2
+    a = near[...].astype(f32)
+    b = rc[jnp.where(even, jnp.maximum(chip - 1, 0), jnp.minimum(chip + 1, 3)), 768:912, :].astype(f32)
     fa[...] = jnp.where(even, a, b)
     fb[...] = jnp.where(even, b, a)
     for z in range(4):
         for c in range(4):
             plane = (c * 4 + z) * 32
-            scr[0:32, 0:256] = mag[c, z] if c < 3 else grains[z].astype(f32)
+            scr[0:32, 0:256] = cells[plane : plane + 32, :].astype(f32)
             scr[0:32, 256:384] = rim[plane : plane + 32, :].astype(f32)
             scr[32:40, :] = jnp.zeros((8, 384), f32)
             for q in range(3):
@@ -178,17 +198,18 @@
                 high_out[(z - 1) * 4 + c] = whole
 
 
-def stages_kernel(own, r3, r4, r7, rc, kx, strip, wz, packed, ax, ay, out):
+def stages_kernel(own, rc, kx, strip_hbm, wz, packed, ax, ay, out, strip, sem):
     gy = lax.axis_index("gy")
     kxm = kx[...].astype(bf16)
+    fetch = pltpu.make_async_copy(strip_hbm, strip, sem)
+    fetch.start()
 
     def x_stage(n, carry):
         kp, jz = n // 6, n % 6
         halves = []
         for half in range(2):
             at = pl.multiple_of(((2 * kp + half) * 6 + jz) * 16, 16)
-            base = lambda g: pl.ds(pl.multiple_of(at + 768 * g, 16), 16)
-            parts = [own[base(0)], rc[base(0)], rc[base(1)], r3[base(0)], r4[base(0)], rc[base(2)], rc[base(3)], r7[base(0)]]
+            parts = [ref[n, pl.ds(at, 16), :] for ref in (own, rc) for n in range(4)]
             halves.append(jnp.concatenate(parts, axis=0))
         res = dot(kxm, jnp.concatenate(halves, axis=1))
         for r in range(8):
@@ -197,13 +218,15 @@
 
     lax.fori_loop(0, 24, x_stage, 0)
     ay[...] = jnp.zeros_like(ay)
+    fetch.wait()
 
     def y_stage(r, carry):
         acc = jnp.zeros((144, 256), f32)
         for kp in range(4):
             tiles = []
             for k in (2 * kp, 2 * kp + 1):
-                at = pl.multiple_of(128 * (8 + gy - k), 128)
+                block = (gy & 4) + k if k < 4 else 11 - (gy & 4) - k
+                at = pl.multiple_of(128 * (8 + gy - block), 128)
                 tiles.append(strip[r, :, pl.ds(at, 256)])
             acc = acc + dot(ax[r, :, kp * 256 : (kp + 1) * 256].astype(bf16), jnp.concatenate(tiles, axis=0))
         acc = acc.astype(bf16).astype(f32)
@@ -241,7 +264,7 @@
     out[114:120] = jnp.zeros((6, 128), f32)
 
 
-def weights_kernel(mag, grains, own_low, own_high, z_low, z_high, stiff, sat, m0, hh, wx, wy, wz, ss, aa):
+def weights_kernel(mag, own_low, own_high, z_low, z_high, stiff, sat, m0, hh, wx, wy, wz, ss, aa):
     gx, gy, gz = (lax.axis_index(n) for n in ("gx", "gy", "gz"))
     row, col = iota((40, 384), 0), iota((40, 384), 1)
     inside = ((row < 32) | ((row < 36) & (gx < 7)) | ((row >= 36) & (gx > 0))) & (
@@ -297,8 +320,13 @@
 
 
 def substeps_kernel(
-    m0, hh, wx, wy, wz, ss, d_own, d_low, d_high, state_out, demag_out, m1, m2, fz, field, rows, spread
+    m0_hbm, hh_hbm, wx_hbm, wy_hbm, wz_hbm, ss_hbm, d_own, d_low, d_high, state_out, demag_out,
+    m0, hh, wx, wy, wz, ss, m1, m2, fz, field, rows, spread, sems,
 ):
+    pairs = ((m0_hbm, m0), (hh_hbm, hh), (wx_hbm, wx), (wy_hbm, wy), (wz_hbm, wz), (ss_hbm, ss))
+    fetches = [pltpu.make_async_copy(a, b, sems.at[n]) for n, (a, b) in enumerate(pairs)]
+    for fetch in fetches:
+        fetch.start()
     for q in range(6):
         demag_out[q // 3, q % 3] = d_own[pl.ds(6 + q, 16, stride=6), :]
     lane24 = iota((24, 128), 1)
@@ -331,6 +359,8 @@
         field[g] = dot(tall, hi) + dot(tall, lo)
     for step in range(3):
         src, dst = ((m0, m1), (m1, m2), (m2, None))[step]
+        for fetch in (fetches[:2], fetches[2:], ())[step]:
+            fetch.wait()
         first, last = step + 1, 8 - step
 
         def plane(p, carry):
@@ -366,12 +396,21 @@
     return lax.ppermute(value, axis, [(i, i ^ bit) for i in range(8)])
 
 
-def local(magnet, grains, stiffness_table, saturation_table, kernel_x, kernel_y, kernel_z, mixing):
+def step(magnet, grains, stiffness_table, saturation_table, kernel_x, kernel_y, kernel_z, mixing):
     shape = jax.ShapeDtypeStruct
-    (pay_y,) = call(
-        coarse_kernel, shape((8, 128, 128), bf16), [VM, VM, SM], [pltpu.VMEM((6, 32, 256), f32)], 20_000_000, 600_000
+    up = [(i, i + 1) for i in range(7)]
+    down = [(i + 1, i) for i in range(7)]
+    big = (10, 40, 384)
+    pay, edges, cells = call(
+        coarse_kernel,
+        [shape((128, 128), bf16), shape((2, 48, 256), f32), shape((512, 256), bf16)],
+        [VM, VM, SM],
+        [pltpu.VMEM((6, 32, 256), f32)],
+        20_000_000,
+        600_000,
+        FULL - 520_000,
     )(magnet, grains, saturation_table)
-    gathered = lax.all_to_all(pay_y, "gy", 0, 0, tiled=True)
+    other = swap(pay, "gy", 7)
     strip, kx, wz = call(
         toeplitz_kernel,
         [shape((8, 128, 2176), bf16), shape((192, 128), f32), shape((192, 64), bf16)],
@@ -380,64 +419,72 @@
         20_000_000,
         5_000_000,
     )(kernel_x, kernel_y, kernel_z, mixing.reshape(8, 9))
-    pay_x, face_a, rim = call(
+    (pay,) = call(pair_kernel, shape((4, 224, 128), bf16), [VM] * 2, (), 1000, 400_000, 8 << 20)(pay, other)
+    groups = [[0, 1, 2, 3], [4, 5, 6, 7]]
+    gathered = lax.all_to_all(pay, "gy", 0, 0, tiled=True, axis_index_groups=groups)
+    pay, face_a, rim = call(
         faces_kernel,
-        [shape((912, 128), bf16), shape((144, 128), bf16), shape((512, 128), bf16)],
+        [shape((4, 912, 128), bf16), shape((144, 128), bf16), shape((512, 128), bf16)],
         [VM] * 3,
-        [pltpu.VMEM((144, 128), f32)] * 2,
+        [pltpu.VMEM((48, 128), f32)] * 2,
         1_000_000,
         1_000_000,
-    )(gathered, magnet, grains)
-    x3, x4, x7 = (swap(pay_x, "gx", k) for k in (3, 4, 7))
-    pay_c = jnp.concatenate([pay_x[:768], x3[:768], x4[:768], x7[:768], face_a], axis=0)
-    rc = swap(pay_c, "gx", 1)
+        8 << 20,
+    )(gathered, other, edges)
+    groups = [[0, 2, 4, 6], [1, 3, 5, 7]]
+    gathered = lax.all_to_all(pay, "gx", 0, 0, tiled=True, axis_index_groups=groups)
+    near = swap(face_a, "gx", 1)
+    rc = swap(gathered, "gx", 1)
     own_low, own_high = call(
         rims_kernel,
         [shape((12, 40, 384), bf16)] * 2,
-        [VM] * 6,
+        [VM] * 4,
         [pltpu.VMEM((40, 384), f32), pltpu.VMEM((144, 128), f32), pltpu.VMEM((144, 128), f32)],
         1_000_000,
         2_000_000,
-    )(magnet, grains, rim, rc, x3, x7)
-    up = [(i, i + 1) for i in range(7)]
-    down = [(i + 1, i) for i in range(7)]
+        12 << 20,
+    )(cells, rim, near, rc)
     z_low = lax.ppermute(own_high, "gz", up)
     z_high = lax.ppermute(own_low, "gz", down)
     (parts,) = call(
         stages_kernel,
         shape((8, 120, 128), jnp.int16),
-        [VM] * 8,
-        [pltpu.VMEM((8, 144, 1024), f32), pltpu.VMEM((18, 64, 256), f32), pltpu.VMEM((8, 120, 128), f32)],
+        [VM, VM, VM, HB, VM],
+        [pltpu.VMEM((8, 144, 1024), f32), pltpu.VMEM((18, 64, 256), f32), pltpu.VMEM((8, 120, 128), f32)]
+        + [pltpu.VMEM((8, 128, 2176), bf16), pltpu.SemaphoreType.DMA],
         2_000_000_000,
         10_000_000,
-    )(pay_x, x3, x4, x7, rc, kx, strip, wz)
+        FULL - (4 << 20),
+    )(gathered, rc, kx, strip, wz)
     parts = lax.all_to_all(parts, "gz", 0, 0, tiled=True)
-    big = (10, 40, 384)
-    m0, hh, wx, wy, wz, ss = call(
+    fields = call(
         weights_kernel,
         [shape((3,) + big, f32), shape((3, 8, 40, 384), f32)] + [shape(big, f32)] * 4,
-        [VM] * 6 + [SM] * 2,
+        [VM] * 5 + [SM] * 2,
         [pltpu.VMEM(big, f32)],
         20_000_000,
         5_000_000,
-    )(magnet, grains, own_low, own_high, z_low, z_high, stiffness_table, saturation_table)
-    (d_own,) = call(sum_kernel, shape((120, 128), f32), [VM], (), 100_000, 300_000)(parts)
+    )(magnet, own_low, own_high, z_low, z_high, stiffness_table, saturation_table)
+    (d_own,) = call(sum_kernel, shape((120, 128), f32), [VM], (), 100_000, 300_000, 8 << 20)(parts)
     d_low = lax.ppermute(d_own, "gz", up)
     d_high = lax.ppermute(d_own, "gz", down)
     state, demag = call(
         substeps_kernel,
         [shape((3, 4, 32, 256), f32), shape((2, 3, 16, 128), f32)],
-        [VM] * 9,
-        [pltpu.VMEM((3,) + big, f32)] * 2
+        [HB] * 6 + [VM] * 3,
+        [pltpu.VMEM((3,) + big, f32), pltpu.VMEM((3, 8, 40, 384), f32)]
+        + [pltpu.VMEM(big, f32)] * 4
+        + [pltpu.VMEM((3,) + big, f32)] * 2
         + [pltpu.VMEM((3, 40, 384), f32), pltpu.VMEM((12, 40, 384), f32)]
-        + [pltpu.VMEM((288, 256), f32), pltpu.VMEM((288, 384), f32)],
+        + [pltpu.VMEM((288, 256), f32), pltpu.VMEM((288, 384), f32), pltpu.SemaphoreType.DMA((6,))],
         50_000_000,
         5_000_000,
-    )(m0, hh, wx, wy, wz, ss, d_own, d_low, d_high)
+        FULL - 300_000,
+    )(*fields, d_own, d_low, d_high)
     return (state, demag)
 
 
 def solution(mesh):
     in_specs = (P(None, "gz", "gx", "gy"), P("gz", "gx", "gy"), P(), P(), P(), P(), P(), P())
     out_specs = (P(None, "gz", "gx", "gy"), P("gz", None, "gx", "gy"))
-    return jax.shard_map(local, mesh=mesh, in_specs=in_specs, out_specs=out_specs, check_vma=False)
+    return jax.shard_map(step, mesh=mesh, in_specs=in_specs, out_specs=out_specs, check_vma=False)

time: 120 us -> 119 us (level)
  blocking collectives: 41 us -> 24.5 us
  starting transfers between devices: 29.3 us -> 44 us
  waiting for transfers between devices: 20.4 us -> 10.3 us
  Pallas kernels: 22.5 us -> 32.5 us
    all_to_all x1 -> x2, blocking collectives: 41 us -> 24.5 us  [the longest x1 15.6 us: step(): lax.all_to_all(pay, 'gx', 0, 0, tiled=True, axis_index_groups=groups)]
    pallas_call x8 -> x9, Pallas kernels: 22.5 us -> 32.5 us  [the longest x1 9.4 us: step(): call(stages_kernel, shape((8, 120, 128), jnp.int16), [VM, VM, VM, HB, VM]...]
    ppermute x4 -> x3, starting transfers between devices: 11.9 us -> 21.1 us  [swap(): return lax.ppermute(value, axis, [(i, i ^ bit) for i in range(8)])]
    ppermute x4 -> x3, waiting for transfers between devices: 9.43 us -> 3.62 us  [swap(): return lax.ppermute(value, axis, [(i, i ^ bit) for i in range(8)])]
    all_to_all x1, starting transfers between devices: 5.69 us -> 11.3 us  [step(): parts = lax.all_to_all(parts, 'gz', 0, 0, tiled=True)]
    all_to_all x1, waiting for transfers between devices: 10.9 us -> 6.65 us  [step(): parts = lax.all_to_all(parts, 'gz', 0, 0, tiled=True)]
    unnamed x26 -> x28, local copies, waits for them, and re-layouts: 5.34 us -> 5.86 us
  transfers between devices with their start and end apart: 9 -> 8, of which waited for: 3 -> 3; matrix products, arithmetic and copies ran while one was open for 2% -> 1% of each run, Pallas kernels for 7% -> 11%
where the time goes in v3:
time: 119 us
  starting transfers between devices  44 us (37%)
  Pallas kernels  32.5 us (27%)
  blocking collectives  24.5 us (21%)
  waiting for transfers between devices  10.3 us (9%)
  local copies, waits for them, and re-layouts  6.54 us (5%)
    ppermute x3, starting transfers between devices, swap(): return lax.ppermute(value, axis, [(i, i ^ bit) for i in range(8)])  21.1 us
    all_to_all x1, blocking collectives, step(): lax.all_to_all(pay, 'gx', 0, 0, tiled=True, axis_index_groups=groups)  15.6 us
    all_to_all x1, starting transfers between devices, step(): parts = lax.all_to_all(parts, 'gz', 0, 0, tiled=True)  11.3 us
    pallas_call x1, Pallas kernels, step(): call(stages_kernel, shape((8, 120, 128), jnp.int16), [VM, VM, VM, HB, VM]...  9.4 us
    all_to_all x1, blocking collectives, step(): lax.all_to_all(pay, 'gy', 0, 0, tiled=True, axis_index_groups=groups)  8.88 us
    pallas_call x1, Pallas kernels, step(): call(substeps_kernel, [shape((3, 4, 32, 256), f32), shape((2, 3, 16, 128)...  7.53 us
    pallas_call x1, Pallas kernels, step(): call(weights_kernel, [shape((3,) + big, f32), shape((3, 8, 40, 384), f32)...  6.94 us
    all_to_all x1, waiting for transfers between devices, step(): parts = lax.all_to_all(parts, 'gz', 0, 0, tiled=True)  6.65 us
  transfers between devices with their start and end apart: 8, of which 3 were waited for; matrix products, arithmetic and copies ran while one was open for 1% of the time, Pallas kernels for 11%

profile of v3, /device:TPU:32, one launch (start us, length us, event | category | flops | bytes accessed | tf_op | source)
XLA Modules:
  0.0 118.6 jit_solution(14749097007458487499)
XLA Ops:
  0.6 0.0 copy-start.13
  0.6 2.1 %shard_map.95 = (bf16[128,128]{1,0:T(8,128)(2,1)}, f32[2,48,256]{2,1,0:T(8,128)}, bf16[512,256]{1,0:T(8,128)(2,1)}) custom-call(f32[3,4,32,256]{3,2,1,0:T(8,128)} %mag.3, s32[4,32,256]{2,1,0:T(8,128)} %grains.1, f32[16]{0:T(128)} %sat.3), custom_call_target="tpu_custom_call" | custom-call | flops 20000000 | bytes 600000 | tf_op jit(solution)/shard_map/pallas_call | solution.py:404
  2.8 17.3 %collective-permute-start = (bf16[128,128]{1,0:T(8,128)(2,1)}, bf16[128,128]{1,0:T(8,128)(2,1)S(1)}, u32[]{:S(2)}, u32[]{:S(2)}) collective-permute-start(bf16[128,128]{1,0:T(8,128)(2,1)} %get-tuple-element.20.own), channel_id=1, source_target_pairs={{0,56},{8,48},{16,40},{24,32},{32,24},{40,16},{48,8},{56,0},{1,57}... | collective-permute-start | bytes 98312 | tf_op jit(solution)/shard_map/ppermute | solution.py:396
  20.0 2.4 %collective-permute-done.other = bf16[128,128]{1,0:T(8,128)(2,1)S(1)} collective-permute-done((bf16[128,128]{1,0:T(8,128)(2,1)}, bf16[128,128]{1,0:T(8,128)(2,1)S(1)}, u32[]{:S(2)}, u32[]{:S(2)}) %collective-permute-start) | collective-permute-done | bytes 32800 | tf_op jit(solution)/shard_map/ppermute | solution.py:396
  22.5 0.8 copy-done.7
  23.3 8.9 %all_to_all.15.gathered = bf16[4,224,128]{2,1,0:T(8,128)(2,1)S(1)} all-to-all(bf16[4,224,128]{2,1,0:T(8,128)(2,1)S(1)} %shard_map.96), channel_id=1, replica_groups={{0,8,16,24},{32,40,48,56},{1,9,17,25},{33,41,49,57},{2,10,18,26},{34,42..., dimensions={0} | all-to-all | bytes 458752 | tf_op jit(solution)/shard_map/all_to_all | solution.py:424
  32.1 0.9 copy-done.6
  33.0 0.3 shard_map.97
  33.3 15.6 %all_to_all.16.own = bf16[4,912,128]{2,1,0:T(8,128)(2,1)S(1)} all-to-all(bf16[4,912,128]{2,1,0:T(8,128)(2,1)S(1)} %get-tuple-element.24), channel_id=1, replica_groups={{0,128,256,384},{64,192,320,448},{1,129,257,385},{65,193,321,449},{2,13..., dimensions={0} | all-to-all | bytes 1867776 | tf_op jit(solution)/shard_map/all_to_all | solution.py:435
  48.9 1.9 %collective-permute-start.2 = (bf16[4,912,128]{2,1,0:T(8,128)(2,1)S(1)}, bf16[4,912,128]{2,1,0:T(8,128)(2,1)S(1)}, u32[]{:S(2)}, u32[]{:S(2)}) collective-permute-start(bf16[4,912,128]{2,1,0:T(8,128)(2,1)S(1)} %all_to_all.16.own), channel_id=1, source_target_pairs={{0,64},{64,0},{128,192},{192,128},{256,320},{320,256},{384,448},{4... | collective-permute-start | bytes 2801672 | tf_op jit(solution)/shard_map/ppermute | solution.py:396
  50.8 0.0 copy-done.13
  50.9 0.7 copy.11.mixing
  51.5 5.9 %shard_map.100 = (bf16[8,128,2176]{2,1,0:T(8,128)(2,1)}, f32[192,128]{1,0:T(8,128)}, bf16[192,64]{1,0:T(8,128)(2,1)}) custom-call(bf16[8,256]{1,0:T(8,128)(2,1)} %kernel_x.1, bf16[8,2048]{1,0:T(8,128)(2,1)} %kernel_y.1, bf16[8,32]{1,0:T(8,128)(2,1)} %kernel_z.1, f32[8,9]{1,0:T(8,128)} %copy.11.mixing), custom_call_target="tpu_custom_call" | custom-call | flops 20000000 | bytes 5000000 | tf_op jit(solution)/shard_map/pallas_call | solution.py:414
  57.4 0.0 collective-permute-done.2.rc
  57.4 0.0 copy-done.8
  57.5 0.9 copy-done
  58.4 9.4 %shard_map.101 = s16[8,120,128]{2,1,0:T(8,128)(2,1)} custom-call(bf16[4,912,128]{2,1,0:T(8,128)(2,1)} %copy-done.8, bf16[4,912,128]{2,1,0:T(8,128)(2,1)} %copy-done, f32[192,128]{1,0:T(8,128)} %get-tuple-element.33.kx, bf16[8,128,2176]{2,1,0:T(8,128)(2,1)} %get-tuple-element.34.strip_hbm, bf16[192,64]{1,0:T(8,128)(2,1)} %get-tuple-element.35.wz), custom_call_target="tpu_custom_call" | custom-call | flops 2000000000 | bytes 10000000 | tf_op jit(solution)/shard_map/pallas_call | solution.py:449
  67.8 11.3 %all-to-all-start.2 = ((s16[8,120,128]{2,1,0:T(8,128)(2,1)}), s16[8,120,128]{2,1,0:T(8,128)(2,1)S(1)}, u32[]{:S(2)}, u32[]{:S(2)}) async-start(s16[8,120,128]{2,1,0:T(8,128)(2,1)} %shard_map.101), calls=%async_computation.2 | async-start | bytes 491520 | tf_op jit(solution)/shard_map/all_to_all | solution.py:459
  79.1 1.9 %collective-permute-start.1 = (bf16[144,128]{1,0:T(8,128)(2,1)S(1)}, bf16[144,128]{1,0:T(8,128)(2,1)S(1)}, u32[]{:S(2)}, u32[]{:S(2)}) collective-permute-start(bf16[144,128]{1,0:T(8,128)(2,1)S(1)} %get-tuple-element.23), channel_id=1, source_target_pairs={{0,64},{64,0},{128,192},{192,128},{256,320},{320,256},{384,448},{4... | collective-permute-start | bytes 110600 | tf_op jit(solution)/shard_map/ppermute | solution.py:396
  81.0 1.2 collective-permute-done.1.near
  82.2 0.0 copy-done.4
  82.2 1.2 copy-done.1
  83.3 0.2 shard_map.98
  83.5 0.0 copy-start.2
  83.5 0.0 copy-start.3
  83.5 1.9 %collective-permute-start.4 = (bf16[12,40,384]{2,1,0:T(8,128)(2,1)S(1)}, bf16[12,40,384]{2,1,0:T(8,128)(2,1)S(1)}, u32[]{:S(2)}, u32[]{:S(2)}) collective-permute-start(bf16[12,40,384]{2,1,0:T(8,128)(2,1)S(1)} %get-tuple-element.25.own_low), channel_id=1, source_target_pairs={{1,0},{2,1},{3,2},{4,3},{5,4},{6,5},{7,6},{9,8},{10,9},{11,10},{12... | collective-permute-start | bytes 1105928 | tf_op jit(solution)/shard_map/ppermute | solution.py:448
  85.5 3.9 %collective-permute-start.3 = (bf16[12,40,384]{2,1,0:T(8,128)(2,1)S(1)}, bf16[12,40,384]{2,1,0:T(8,128)(2,1)S(1)}, u32[]{:S(2)}, u32[]{:S(2)}) collective-permute-start(bf16[12,40,384]{2,1,0:T(8,128)(2,1)S(1)} %get-tuple-element.26.own_high), channel_id=1, source_target_pairs={{0,1},{1,2},{2,3},{3,4},{4,5},{5,6},{6,7},{8,9},{9,10},{10,11},{11... | collective-permute-start | bytes 1105928 | tf_op jit(solution)/shard_map/ppermute | solution.py:447
  89.4 6.6 %all-to-all-done.2.parts = s16[8,120,128]{2,1,0:T(8,128)(2,1)S(1)} async-done(((s16[8,120,128]{2,1,0:T(8,128)(2,1)}), s16[8,120,128]{2,1,0:T(8,128)(2,1)S(1)}, u32[]{:S(2)}, u32[]{:S(2)}) %all-to-all-start.2) | async-done | bytes 245792 | tf_op jit(solution)/shard_map/all_to_all | solution.py:459
  96.0 0.1 shard_map.102.d_own
  96.1 0.0 copy-start.5
  96.1 1.9 %collective-permute-start.6 = (f32[120,128]{1,0:T(8,128)S(1)}, f32[120,128]{1,0:T(8,128)S(1)}, u32[]{:S(2)}, u32[]{:S(2)}) collective-permute-start(f32[120,128]{1,0:T(8,128)S(1)} %shard_map.102.d_own), channel_id=1, source_target_pairs={{1,0},{2,1},{3,2},{4,3},{5,4},{6,5},{7,6},{9,8},{10,9},{11,10},{12... | collective-permute-start | bytes 184328 | tf_op jit(solution)/shard_map/ppermute | solution.py:470
  98.1 3.9 %collective-permute-start.5 = (f32[120,128]{1,0:T(8,128)S(1)}, f32[120,128]{1,0:T(8,128)S(1)}, u32[]{:S(2)}, u32[]{:S(2)}) collective-permute-start(f32[120,128]{1,0:T(8,128)S(1)} %shard_map.102.d_own), channel_id=1, source_target_pairs={{0,1},{1,2},{2,3},{3,4},{4,5},{5,6},{6,7},{8,9},{9,10},{10,11},{11... | collective-permute-start | bytes 184328 | tf_op jit(solution)/shard_map/ppermute | solution.py:469
  102.0 0.0 collective-permute-done.4.z_high
  102.0 0.0 copy-start.9
  102.0 0.0 collective-permute-done.3.z_low
  102.0 0.0 copy-done.2
  102.0 0.0 copy-done.3
  102.0 0.7 copy-done.9
  102.8 0.7 copy-done.10
  103.5 6.9 %shard_map.99 = (f32[3,10,40,384]{3,2,1,0:T(8,128)}, f32[3,8,40,384]{3,2,1,0:T(8,128)}, f32[10,40,384]{2,1,0:T(8,128)}, f32[10,40,384]{2,1,0:T(8,128)}, f32[10,40,384]{2,1,0:T(8,128)}, /*index=5*/f32[10,40,384]{2,1,0:T(8,128)}) custom-call(f32[3,4,32,256]{3,2,1,0:T(8,128)} %mag.3, bf16[12,40,384]{2,1,0:T(8,128)(2,1)} %copy-done.2, ...), custom_call_target="tpu_custom_call" | custom-call | flops 20000000 | bytes 5000000 | tf_op jit(solution)/shard_map/pallas_call | solution.py:460
  110.4 0.0 collective-permute-done.6.d_high
  110.4 0.0 copy-start.11
  110.5 0.0 collective-permute-done.5.d_low
  110.5 0.0 copy-start.12
  110.5 0.0 copy-done.5
  110.5 0.6 copy-done.11
  111.1 0.0 copy-done.12
  111.1 7.5 %shard_map.103 = (f32[3,4,32,256]{3,2,1,0:T(8,128)}, f32[2,3,16,128]{3,2,1,0:T(8,128)}) custom-call(f32[3,10,40,384]{3,2,1,0:T(8,128)} %get-tuple-element.27.m0_hbm, f32[3,8,40,384]{3,2,1,0:T(8,128)} %get-tuple-element.28.hh_hbm, f32[10,40,384]{2,1,0:T(8,128)} %get-tuple-element.29.wx_hbm, f32[10,40,384]{2,1,0:T(8,128)} %get-tuple-element.30.wy_hbm, ...), custom_call_target="tpu_custom_call" | custom-call | flops 50000000 | bytes 5000000 | tf_op jit(solution)/shard_map/pallas_call | solution.py:471
  (9 shorter events, 0.1 us)
Async XLA Ops:
  0.6 50.2 %copy-start.13 = (f32[8,3,3]{0,2,1:T(4,128)S(1)}, f32[8,3,3]{0,2,1:T(4,128)}, u32[]{:S(2)}) copy-start(f32[8,3,3]{0,2,1:T(4,128)} %param.15) | copy-start | bytes 868
  2.8 19.7 %collective-permute-start = (bf16[128,128]{1,0:T(8,128)(2,1)}, bf16[128,128]{1,0:T(8,128)(2,1)S(1)}, u32[]{:S(2)}, u32[]{:S(2)}) collective-permute-start(bf16[128,128]{1,0:T(8,128)(2,1)} %get-tuple-element.20.own), channel_id=1, source_target_pairs={{0,56},{8,48},{16,40},{24,32},{32,24},{40,16},{48,8},{56,0},{1,57}... | collective-permute-start | bytes 98312 | tf_op jit(solution)/shard_map/ppermute | solution.py:396
  22.5 0.8 copy-start.7
  32.1 0.9 copy-start.6
  48.9 8.5 %copy-start.8 = (bf16[4,912,128]{2,1,0:T(8,128)(2,1)}, bf16[4,912,128]{2,1,0:T(8,128)(2,1)S(1)}, u32[]{:S(2)}) copy-start(bf16[4,912,128]{2,1,0:T(8,128)(2,1)S(1)} %all_to_all.16.own) | copy-start | bytes 2801668
  48.9 8.5 %collective-permute-start.2 = (bf16[4,912,128]{2,1,0:T(8,128)(2,1)S(1)}, bf16[4,912,128]{2,1,0:T(8,128)(2,1)S(1)}, u32[]{:S(2)}, u32[]{:S(2)}) collective-permute-start(bf16[4,912,128]{2,1,0:T(8,128)(2,1)S(1)} %all_to_all.16.own), channel_id=1, source_target_pairs={{0,64},{64,0},{128,192},{192,128},{256,320},{320,256},{384,448},{4... | collective-permute-start | bytes 2801672 | tf_op jit(solution)/shard_map/ppermute | solution.py:396
  57.4 0.9 copy-start
  58.4 23.8 %copy-start.4 = (bf16[512,256]{1,0:T(8,128)(2,1)S(1)}, bf16[512,256]{1,0:T(8,128)(2,1)}, u32[]{:S(2)}) copy-start(bf16[512,256]{1,0:T(8,128)(2,1)} %get-tuple-element.19.cells) | copy-start | bytes 786436
  67.8 28.2 %all-to-all-start.2 = ((s16[8,120,128]{2,1,0:T(8,128)(2,1)}), s16[8,120,128]{2,1,0:T(8,128)(2,1)S(1)}, u32[]{:S(2)}, u32[]{:S(2)}) async-start(s16[8,120,128]{2,1,0:T(8,128)(2,1)} %shard_map.101), calls=%async_computation.2 | async-start | bytes 491520 | tf_op jit(solution)/shard_map/all_to_all | solution.py:459
  79.1 3.1 %collective-permute-start.1 = (bf16[144,128]{1,0:T(8,128)(2,1)S(1)}, bf16[144,128]{1,0:T(8,128)(2,1)S(1)}, u32[]{:S(2)}, u32[]{:S(2)}) collective-permute-start(bf16[144,128]{1,0:T(8,128)(2,1)S(1)} %get-tuple-element.23), channel_id=1, source_target_pairs={{0,64},{64,0},{128,192},{192,128},{256,320},{320,256},{384,448},{4... | collective-permute-start | bytes 110600 | tf_op jit(solution)/shard_map/ppermute | solution.py:396
  82.2 1.2 copy-start.1
  83.5 18.5 %copy-start.2 = (bf16[12,40,384]{2,1,0:T(8,128)(2,1)}, bf16[12,40,384]{2,1,0:T(8,128)(2,1)S(1)}, u32[]{:S(2)}) copy-start(bf16[12,40,384]{2,1,0:T(8,128)(2,1)S(1)} %get-tuple-element.25.own_low) | copy-start | bytes 1105924
  83.5 18.5 %copy-start.3 = (bf16[12,40,384]{2,1,0:T(8,128)(2,1)}, bf16[12,40,384]{2,1,0:T(8,128)(2,1)S(1)}, u32[]{:S(2)}) copy-start(bf16[12,40,384]{2,1,0:T(8,128)(2,1)S(1)} %get-tuple-element.26.own_high) | copy-start | bytes 1105924
  83.5 18.5 %collective-permute-start.4 = (bf16[12,40,384]{2,1,0:T(8,128)(2,1)S(1)}, bf16[12,40,384]{2,1,0:T(8,128)(2,1)S(1)}, u32[]{:S(2)}, u32[]{:S(2)}) collective-permute-start(bf16[12,40,384]{2,1,0:T(8,128)(2,1)S(1)} %get-tuple-element.25.own_low), channel_id=1, source_target_pairs={{1,0},{2,1},{3,2},{4,3},{5,4},{6,5},{7,6},{9,8},{10,9},{11,10},{12... | collective-permute-start | bytes 1105928 | tf_op jit(solution)/shard_map/ppermute | solution.py:448
  85.5 16.5 %collective-permute-start.3 = (bf16[12,40,384]{2,1,0:T(8,128)(2,1)S(1)}, bf16[12,40,384]{2,1,0:T(8,128)(2,1)S(1)}, u32[]{:S(2)}, u32[]{:S(2)}) collective-permute-start(bf16[12,40,384]{2,1,0:T(8,128)(2,1)S(1)} %get-tuple-element.26.own_high), channel_id=1, source_target_pairs={{0,1},{1,2},{2,3},{3,4},{4,5},{5,6},{6,7},{8,9},{9,10},{10,11},{11... | collective-permute-start | bytes 1105928 | tf_op jit(solution)/shard_map/ppermute | solution.py:447
  96.1 14.4 %copy-start.5 = (f32[120,128]{1,0:T(8,128)}, f32[120,128]{1,0:T(8,128)S(1)}, u32[]{:S(2)}) copy-start(f32[120,128]{1,0:T(8,128)S(1)} %shard_map.102.d_own) | copy-start | bytes 184324
  96.1 14.3 %collective-permute-start.6 = (f32[120,128]{1,0:T(8,128)S(1)}, f32[120,128]{1,0:T(8,128)S(1)}, u32[]{:S(2)}, u32[]{:S(2)}) collective-permute-start(f32[120,128]{1,0:T(8,128)S(1)} %shard_map.102.d_own), channel_id=1, source_target_pairs={{1,0},{2,1},{3,2},{4,3},{5,4},{6,5},{7,6},{9,8},{10,9},{11,10},{12... | collective-permute-start | bytes 184328 | tf_op jit(solution)/shard_map/ppermute | solution.py:470
  98.1 12.4 %collective-permute-start.5 = (f32[120,128]{1,0:T(8,128)S(1)}, f32[120,128]{1,0:T(8,128)S(1)}, u32[]{:S(2)}, u32[]{:S(2)}) collective-permute-start(f32[120,128]{1,0:T(8,128)S(1)} %shard_map.102.d_own), channel_id=1, source_target_pairs={{0,1},{1,2},{2,3},{3,4},{4,5},{5,6},{6,7},{8,9},{9,10},{10,11},{11... | collective-permute-start | bytes 184328 | tf_op jit(solution)/shard_map/ppermute | solution.py:469
  102.0 0.8 copy-start.9
  102.8 0.7 copy-start.10
  110.4 0.6 copy-start.11
  110.5 0.6 copy-start.12

commit v4 on v3

--- a/solution.py
+++ b/solution.py
@@ -93,7 +93,6 @@
     gx, gz = lax.axis_index("gx"), lax.axis_index("gz")
     kyp[...] = jnp.zeros_like(kyp)
     kyp[:, 0:2048] = kernel_y[...].astype(f32)
-    kyp[...] = pltpu.roll(kyp[...], 64, 1)
     mirror = one_hot(iota((256, 256), 0) + iota((256, 256), 1) == 255)
     kxr = dot(kernel_x[...], mirror)
     row, col = iota((64, 32), 0), iota((64, 32), 1)
@@ -111,15 +110,15 @@
         line = jnp.zeros((1, 64), f32)
         for r in range(8):
             for j in range(3):
-                line = jnp.where(rj_of[0:1] == r * 4 + j, mixing[r, i * 3 + j], line)
+                line = jnp.where(rj_of[0:1] == r * 4 + j, mixing[i, j, r], line)
         mix = jnp.where(i_of == i, line, mix)
     w = mix * total
     hi = w.astype(bf16)
     rest = w - hi.astype(f32)
     mid = rest.astype(bf16)
-    wz_out[0:64] = hi
-    wz_out[64:128] = mid
-    wz_out[128:192] = (rest - mid.astype(f32)).astype(bf16)
+    wz_out[:, 0:64] = hi
+    wz_out[:, 64:128] = mid
+    wz_out[:, 128:192] = (rest - mid.astype(f32)).astype(bf16)
 
     def one(r, carry):
         row = jnp.broadcast_to(kyp[pl.ds(r, 1), :], (128, 2176))
@@ -204,21 +203,28 @@
     fetch = pltpu.make_async_copy(strip_hbm, strip, sem)
     fetch.start()
 
-    def x_stage(n, carry):
-        kp, jz = n // 6, n % 6
-        halves = []
+    def x_stage(kp, carry):
+        for pair in range(3):
+            res = []
+            for jz in range(2):
+                halves = []
+                for half in range(2):
+                    at = pl.multiple_of(((2 * kp + half) * 6 + 2 * pair + jz) * 16, 16)
+                    parts = [ref[n, pl.ds(at, 16), :] for ref in (own, rc) for n in range(4)]
+                    halves.append(jnp.concatenate(parts, axis=0))
+                res.append(dot(kxm, jnp.concatenate(halves, axis=1)))
+            for r in range(8):
+                both = jnp.concatenate([res[0][r * 24 : (r + 1) * 24], res[1][r * 24 : (r + 1) * 24]], axis=0)
+                ax[r, pair * 48 : pair * 48 + 48, pl.ds(pl.multiple_of(kp * 256, 256), 256)] = both.astype(bf16)
+        return carry
+
+    lax.fori_loop(0, 4, x_stage, 0)
+    for r in range(8):
         for half in range(2):
-            at = pl.multiple_of(((2 * kp + half) * 6 + jz) * 16, 16)
-            parts = [ref[n, pl.ds(at, 16), :] for ref in (own, rc) for n in range(4)]
-            halves.append(jnp.concatenate(parts, axis=0))
-        res = dot(kxm, jnp.concatenate(halves, axis=1))
-        for r in range(8):
-            ax[r, pl.ds(pl.multiple_of(jz * 24, 8), 24), pl.ds(pl.multiple_of(kp * 256, 256), 256)] = res[r * 24 : (r + 1) * 24]
-        return carry
-
-    lax.fori_loop(0, 24, x_stage, 0)
-    ay[...] = jnp.zeros_like(ay)
+            ay[r, half, 144:192, :] = jnp.zeros((48, 128), f32)
     fetch.wait()
+
+    first_half = iota((128, 128), 1) < 64
 
     def y_stage(r, carry):
         acc = jnp.zeros((144, 256), f32)
@@ -227,21 +233,25 @@
             for k in (2 * kp, 2 * kp + 1):
                 block = (gy & 4) + k if k < 4 else 11 - (gy & 4) - k
                 at = pl.multiple_of(128 * (8 + gy - block), 128)
-                tiles.append(strip[r, :, pl.ds(at, 256)])
-            acc = acc + dot(ax[r, :, kp * 256 : (kp + 1) * 256].astype(bf16), jnp.concatenate(tiles, axis=0))
-        acc = acc.astype(bf16).astype(f32)
-        for jz in range(6):
-            for a in range(18):
-                ay[a, pl.ds(r * 8 + jz, 1), :] = acc[jz * 24 + a : jz * 24 + a + 1, :]
+                after, before = strip[r, :, pl.ds(at + 128, 128)], strip[r, :, pl.ds(at - 128, 128)]
+                ends = jnp.where(first_half, after, before)
+                tiles.append(jnp.concatenate([strip[r, :, pl.ds(at, 128)], ends], axis=1))
+            acc = acc + dot(ax[r, :, kp * 256 : (kp + 1) * 256], jnp.concatenate(tiles, axis=0))
+        for half in range(2):
+            ay[r, half, 0:144, :] = acc[:, 128 * half : 128 * half + 128]
         return carry
 
-    lax.fori_loop(0, 8, y_stage, 0)
+    lax.fori_loop(0, 8, y_stage, 0, unroll=2)
     w = wz[...]
     lane = iota((64, 128), 1)
     rims = jnp.zeros((64, 128), f32)
     for a in range(18):
-        o3 = dot(w, ay[a].astype(bf16))
-        o = pltpu.roll(o3[0:64] + o3[64:128] + o3[128:192], 192, 1)
+        halves = [
+            jnp.concatenate([ay[r, half, pl.ds(a, 8, stride=24), :] for r in range(8)], axis=0).astype(bf16)
+            for half in range(2)
+        ]
+        col = jnp.concatenate(halves, axis=1)
+        o = dot(w, jnp.concatenate([col, col, col], axis=0))
         rims = jnp.where(lane // 2 == a, pltpu.roll(o[:, 128:], 2 * a + 1, 1), rims)
         for d in range(8):
             out[d, a * 6 : a * 6 + 6, :] = o[d * 8 : d * 8 + 6, :128]
@@ -325,7 +335,7 @@
 ):
     pairs = ((m0_hbm, m0), (hh_hbm, hh), (wx_hbm, wx), (wy_hbm, wy), (wz_hbm, wz), (ss_hbm, ss))
     fetches = [pltpu.make_async_copy(a, b, sems.at[n]) for n, (a, b) in enumerate(pairs)]
-    for fetch in fetches:
+    for fetch in fetches[:2]:
         fetch.start()
     for q in range(6):
         demag_out[q // 3, q % 3] = d_own[pl.ds(6 + q, 16, stride=6), :]
@@ -361,6 +371,9 @@
         src, dst = ((m0, m1), (m1, m2), (m2, None))[step]
         for fetch in (fetches[:2], fetches[2:], ())[step]:
             fetch.wait()
+        if step == 0:
+            for fetch in fetches[2:]:
+                fetch.start()
         first, last = step + 1, 8 - step
 
         def plane(p, carry):
@@ -413,12 +426,12 @@
     other = swap(pay, "gy", 7)
     strip, kx, wz = call(
         toeplitz_kernel,
-        [shape((8, 128, 2176), bf16), shape((192, 128), f32), shape((192, 64), bf16)],
+        [shape((8, 128, 2176), bf16), shape((192, 128), f32), shape((64, 192), bf16)],
         [VM, VM, VM, SM],
         [pltpu.VMEM((8, 2176), f32)],
         20_000_000,
         5_000_000,
-    )(kernel_x, kernel_y, kernel_z, mixing.reshape(8, 9))
+    )(kernel_x, kernel_y, kernel_z, mixing.transpose(1, 2, 0))
     (pay,) = call(pair_kernel, shape((4, 224, 128), bf16), [VM] * 2, (), 1000, 400_000, 8 << 20)(pay, other)
     groups = [[0, 1, 2, 3], [4, 5, 6, 7]]
     gathered = lax.all_to_all(pay, "gy", 0, 0, tiled=True, axis_index_groups=groups)
@@ -450,7 +463,7 @@
         stages_kernel,
         shape((8, 120, 128), jnp.int16),
         [VM, VM, VM, HB, VM],
-        [pltpu.VMEM((8, 144, 1024), f32), pltpu.VMEM((18, 64, 256), f32), pltpu.VMEM((8, 120, 128), f32)]
+        [pltpu.VMEM((8, 144, 1024), bf16), pltpu.VMEM((8, 2, 192, 128), f32), pltpu.VMEM((8, 120, 128), f32)]
         + [pltpu.VMEM((8, 128, 2176), bf16), pltpu.SemaphoreType.DMA],
         2_000_000_000,
         10_000_000,

time: 119 us -> 117 us (0.983)
  Pallas kernels: 32.5 us -> 30.6 us
    pallas_call x1, Pallas kernels: 9.4 us -> 6.6 us  [step(): call(stages_kernel, shape((8, 120, 128), jnp.int16), [VM, VM, VM, HB, VM]...]
    unnamed x28 -> x26, local copies, waits for them, and re-layouts: 5.86 us -> 5.89 us
  transfers between devices with their start and end apart: 8 -> 8, of which waited for: 3 -> 3; matrix products, arithmetic and copies ran while one was open for 1% -> 0% of each run, Pallas kernels for 11% -> 11%
where the time goes in v4:
time: 117 us; the launch traced here: 116 us
  starting transfers between devices  44 us (38%)
  Pallas kernels  30.6 us (26%)
  blocking collectives  24.5 us (21%)
  waiting for transfers between devices  10.3 us (9%)
  local copies, waits for them, and re-layouts  5.89 us (5%)
    ppermute x3, starting transfers between devices, swap(): return lax.ppermute(value, axis, [(i, i ^ bit) for i in range(8)])  21.1 us
    all_to_all x1, blocking collectives, step(): lax.all_to_all(pay, 'gx', 0, 0, tiled=True, axis_index_groups=groups)  15.6 us
    all_to_all x1, starting transfers between devices, step(): parts = lax.all_to_all(parts, 'gz', 0, 0, tiled=True)  11.3 us
    all_to_all x1, blocking collectives, step(): lax.all_to_all(pay, 'gy', 0, 0, tiled=True, axis_index_groups=groups)  8.88 us
    pallas_call x1, Pallas kernels, step(): call(substeps_kernel, [shape((3, 4, 32, 256), f32), shape((2, 3, 16, 128)...  8.32 us
    pallas_call x1, Pallas kernels, step(): call(weights_kernel, [shape((3,) + big, f32), shape((3, 8, 40, 384), f32)...  6.94 us
    all_to_all x1, waiting for transfers between devices, step(): parts = lax.all_to_all(parts, 'gz', 0, 0, tiled=True)  6.65 us
    pallas_call x1, Pallas kernels, step(): call(stages_kernel, shape((8, 120, 128), jnp.int16), [VM, VM, VM, HB, VM]...  6.6 us
  transfers between devices with their start and end apart: 8, of which 3 were waited for; matrix products, arithmetic and copies ran while one was open for 0% of the time, Pallas kernels for 11%

profile of v4, /device:TPU:32, one launch (start us, length us, event | category | flops | bytes accessed | tf_op | source)
XLA Modules:
  0.0 116.1 jit_solution(8956182804516564351)
XLA Ops:
  0.6 2.1 %shard_map.95 = (bf16[128,128]{1,0:T(8,128)(2,1)}, f32[2,48,256]{2,1,0:T(8,128)}, bf16[512,256]{1,0:T(8,128)(2,1)}) custom-call(f32[3,4,32,256]{3,2,1,0:T(8,128)} %mag.3, s32[4,32,256]{2,1,0:T(8,128)} %grains.1, f32[16]{0:T(128)} %sat.3), custom_call_target="tpu_custom_call" | custom-call | flops 20000000 | bytes 600000 | tf_op jit(solution)/shard_map/pallas_call | solution.py:417
  2.8 17.3 %collective-permute-start = (bf16[128,128]{1,0:T(8,128)(2,1)}, bf16[128,128]{1,0:T(8,128)(2,1)S(1)}, u32[]{:S(2)}, u32[]{:S(2)}) collective-permute-start(bf16[128,128]{1,0:T(8,128)(2,1)} %get-tuple-element.20.own), channel_id=1, source_target_pairs={{0,56},{8,48},{16,40},{24,32},{32,24},{40,16},{48,8},{56,0},{1,57}... | collective-permute-start | bytes 98312 | tf_op jit(solution)/shard_map/ppermute | solution.py:409
  20.0 2.4 %collective-permute-done.other = bf16[128,128]{1,0:T(8,128)(2,1)S(1)} collective-permute-done((bf16[128,128]{1,0:T(8,128)(2,1)}, bf16[128,128]{1,0:T(8,128)(2,1)S(1)}, u32[]{:S(2)}, u32[]{:S(2)}) %collective-permute-start) | collective-permute-done | bytes 32800 | tf_op jit(solution)/shard_map/ppermute | solution.py:409
  22.5 0.0 copy-start.7
  22.5 0.8 copy-done.7
  23.3 8.9 %all_to_all.15.gathered = bf16[4,224,128]{2,1,0:T(8,128)(2,1)S(1)} all-to-all(bf16[4,224,128]{2,1,0:T(8,128)(2,1)S(1)} %shard_map.96), channel_id=1, replica_groups={{0,8,16,24},{32,40,48,56},{1,9,17,25},{33,41,49,57},{2,10,18,26},{34,42..., dimensions={0} | all-to-all | bytes 458752 | tf_op jit(solution)/shard_map/all_to_all | solution.py:437
  32.1 0.9 copy-done.6
  33.0 0.3 shard_map.97
  33.3 15.6 %all_to_all.16.own = bf16[4,912,128]{2,1,0:T(8,128)(2,1)S(1)} all-to-all(bf16[4,912,128]{2,1,0:T(8,128)(2,1)S(1)} %get-tuple-element.24), channel_id=1, replica_groups={{0,128,256,384},{64,192,320,448},{1,129,257,385},{65,193,321,449},{2,13..., dimensions={0} | all-to-all | bytes 1867776 | tf_op jit(solution)/shard_map/all_to_all | solution.py:448
  48.9 0.0 copy-start.8
  48.9 1.9 %collective-permute-start.2 = (bf16[4,912,128]{2,1,0:T(8,128)(2,1)S(1)}, bf16[4,912,128]{2,1,0:T(8,128)(2,1)S(1)}, u32[]{:S(2)}, u32[]{:S(2)}) collective-permute-start(bf16[4,912,128]{2,1,0:T(8,128)(2,1)S(1)} %all_to_all.16.own), channel_id=1, source_target_pairs={{0,64},{64,0},{128,192},{192,128},{256,320},{320,256},{384,448},{4... | collective-permute-start | bytes 2801672 | tf_op jit(solution)/shard_map/ppermute | solution.py:409
  50.8 6.0 %shard_map.100 = (bf16[8,128,2176]{2,1,0:T(8,128)(2,1)}, f32[192,128]{1,0:T(8,128)}, bf16[64,192]{1,0:T(8,128)(2,1)}) custom-call(bf16[8,256]{1,0:T(8,128)(2,1)} %kernel_x.1, bf16[8,2048]{1,0:T(8,128)(2,1)} %kernel_y.1, bf16[8,32]{1,0:T(8,128)(2,1)} %kernel_z.1, f32[3,3,8]{2,1,0:T(4,128)} %bitcast.1), custom_call_target="tpu_custom_call" | custom-call | flops 20000000 | bytes 5000000 | tf_op jit(solution)/shard_map/pallas_call | solution.py:427
  56.8 0.0 collective-permute-done.2.rc
  56.8 0.0 copy-start
  56.8 0.0 copy-done.8
  56.9 1.0 copy-done
  57.8 6.6 %shard_map.101 = s16[8,120,128]{2,1,0:T(8,128)(2,1)} custom-call(bf16[4,912,128]{2,1,0:T(8,128)(2,1)} %copy-done.8, bf16[4,912,128]{2,1,0:T(8,128)(2,1)} %copy-done, f32[192,128]{1,0:T(8,128)} %get-tuple-element.33.kx, bf16[8,128,2176]{2,1,0:T(8,128)(2,1)} %get-tuple-element.34.strip_hbm, bf16[64,192]{1,0:T(8,128)(2,1)} %get-tuple-element.35.wz), custom_call_target="tpu_custom_call" | custom-call | flops 2000000000 | bytes 10000000 | tf_op jit(solution)/shard_map/pallas_call | solution.py:462
  64.4 11.3 %all-to-all-start.2 = ((s16[8,120,128]{2,1,0:T(8,128)(2,1)}), s16[8,120,128]{2,1,0:T(8,128)(2,1)S(1)}, u32[]{:S(2)}, u32[]{:S(2)}) async-start(s16[8,120,128]{2,1,0:T(8,128)(2,1)} %shard_map.101), calls=%async_computation.2 | async-start | bytes 491520 | tf_op jit(solution)/shard_map/all_to_all | solution.py:472
  75.7 1.9 %collective-permute-start.1 = (bf16[144,128]{1,0:T(8,128)(2,1)S(1)}, bf16[144,128]{1,0:T(8,128)(2,1)S(1)}, u32[]{:S(2)}, u32[]{:S(2)}) collective-permute-start(bf16[144,128]{1,0:T(8,128)(2,1)S(1)} %get-tuple-element.23), channel_id=1, source_target_pairs={{0,64},{64,0},{128,192},{192,128},{256,320},{320,256},{384,448},{4... | collective-permute-start | bytes 110600 | tf_op jit(solution)/shard_map/ppermute | solution.py:409
  77.6 1.2 %collective-permute-done.1.near = bf16[144,128]{1,0:T(8,128)(2,1)S(1)} collective-permute-done((bf16[144,128]{1,0:T(8,128)(2,1)S(1)}, bf16[144,128]{1,0:T(8,128)(2,1)S(1)}, u32[]{:S(2)}, u32[]{:S(2)}) %collective-permute-start.1) | collective-permute-done | bytes 36896 | tf_op jit(solution)/shard_map/ppermute | solution.py:409
  78.8 0.0 copy-done.4
  78.8 1.2 %copy-done.1 = bf16[4,912,128]{2,1,0:T(8,128)(2,1)S(1)} copy-done((bf16[4,912,128]{2,1,0:T(8,128)(2,1)S(1)}, bf16[4,912,128]{2,1,0:T(8,128)(2,1)}, u32[]{:S(2)}) %copy-start.1) | copy-done | bytes 933912
  80.0 0.2 shard_map.98
  80.1 0.0 copy-start.2
  80.2 0.0 copy-start.3
  80.2 1.9 %collective-permute-start.4 = (bf16[12,40,384]{2,1,0:T(8,128)(2,1)S(1)}, bf16[12,40,384]{2,1,0:T(8,128)(2,1)S(1)}, u32[]{:S(2)}, u32[]{:S(2)}) collective-permute-start(bf16[12,40,384]{2,1,0:T(8,128)(2,1)S(1)} %get-tuple-element.25.own_low), channel_id=1, source_target_pairs={{1,0},{2,1},{3,2},{4,3},{5,4},{6,5},{7,6},{9,8},{10,9},{11,10},{12... | collective-permute-start | bytes 1105928 | tf_op jit(solution)/shard_map/ppermute | solution.py:461
  82.1 3.9 %collective-permute-start.3 = (bf16[12,40,384]{2,1,0:T(8,128)(2,1)S(1)}, bf16[12,40,384]{2,1,0:T(8,128)(2,1)S(1)}, u32[]{:S(2)}, u32[]{:S(2)}) collective-permute-start(bf16[12,40,384]{2,1,0:T(8,128)(2,1)S(1)} %get-tuple-element.26.own_high), channel_id=1, source_target_pairs={{0,1},{1,2},{2,3},{3,4},{4,5},{5,6},{6,7},{8,9},{9,10},{10,11},{11... | collective-permute-start | bytes 1105928 | tf_op jit(solution)/shard_map/ppermute | solution.py:460
  86.0 6.6 %all-to-all-done.2.parts = s16[8,120,128]{2,1,0:T(8,128)(2,1)S(1)} async-done(((s16[8,120,128]{2,1,0:T(8,128)(2,1)}), s16[8,120,128]{2,1,0:T(8,128)(2,1)S(1)}, u32[]{:S(2)}, u32[]{:S(2)}) %all-to-all-start.2) | async-done | bytes 245792 | tf_op jit(solution)/shard_map/all_to_all | solution.py:472
  92.7 0.1 shard_map.102.d_own
  92.7 0.0 copy-start.5
  92.8 1.9 %collective-permute-start.6 = (f32[120,128]{1,0:T(8,128)S(1)}, f32[120,128]{1,0:T(8,128)S(1)}, u32[]{:S(2)}, u32[]{:S(2)}) collective-permute-start(f32[120,128]{1,0:T(8,128)S(1)} %shard_map.102.d_own), channel_id=1, source_target_pairs={{1,0},{2,1},{3,2},{4,3},{5,4},{6,5},{7,6},{9,8},{10,9},{11,10},{12... | collective-permute-start | bytes 184328 | tf_op jit(solution)/shard_map/ppermute | solution.py:483
  94.7 3.9 %collective-permute-start.5 = (f32[120,128]{1,0:T(8,128)S(1)}, f32[120,128]{1,0:T(8,128)S(1)}, u32[]{:S(2)}, u32[]{:S(2)}) collective-permute-start(f32[120,128]{1,0:T(8,128)S(1)} %shard_map.102.d_own), channel_id=1, source_target_pairs={{0,1},{1,2},{2,3},{3,4},{4,5},{5,6},{6,7},{8,9},{9,10},{10,11},{11... | collective-permute-start | bytes 184328 | tf_op jit(solution)/shard_map/ppermute | solution.py:482
  98.6 0.0 collective-permute-done.4.z_high
  98.6 0.0 copy-start.9
  98.6 0.0 collective-permute-done.3.z_low
  98.6 0.0 copy-done.2
  98.7 0.0 copy-done.3
  98.7 0.7 copy-done.9
  99.4 0.7 copy-done.10
  100.1 6.9 %shard_map.99 = (f32[3,10,40,384]{3,2,1,0:T(8,128)}, f32[3,8,40,384]{3,2,1,0:T(8,128)}, f32[10,40,384]{2,1,0:T(8,128)}, f32[10,40,384]{2,1,0:T(8,128)}, f32[10,40,384]{2,1,0:T(8,128)}, /*index=5*/f32[10,40,384]{2,1,0:T(8,128)}) custom-call(f32[3,4,32,256]{3,2,1,0:T(8,128)} %mag.3, bf16[12,40,384]{2,1,0:T(8,128)(2,1)} %copy-done.2, ...), custom_call_target="tpu_custom_call" | custom-call | flops 20000000 | bytes 5000000 | tf_op jit(solution)/shard_map/pallas_call | solution.py:473
  107.1 0.0 collective-permute-done.6.d_high
  107.1 0.0 copy-start.11
  107.1 0.0 collective-permute-done.5.d_low
  107.1 0.0 copy-start.12
  107.1 0.0 copy-done.5
  107.1 0.6 copy-done.11
  107.7 0.0 copy-done.12
  107.7 8.3 %shard_map.103 = (f32[3,4,32,256]{3,2,1,0:T(8,128)}, f32[2,3,16,128]{3,2,1,0:T(8,128)}) custom-call(f32[3,10,40,384]{3,2,1,0:T(8,128)} %get-tuple-element.27.m0_hbm, f32[3,8,40,384]{3,2,1,0:T(8,128)} %get-tuple-element.28.hh_hbm, f32[10,40,384]{2,1,0:T(8,128)} %get-tuple-element.29.wx_hbm, f32[10,40,384]{2,1,0:T(8,128)} %get-tuple-element.30.wy_hbm, ...), custom_call_target="tpu_custom_call" | custom-call | flops 50000000 | bytes 5000000 | tf_op jit(solution)/shard_map/pallas_call | solution.py:484
  (5 shorter events, 0.0 us)
Async XLA Ops:
  2.8 19.7 %collective-permute-start = (bf16[128,128]{1,0:T(8,128)(2,1)}, bf16[128,128]{1,0:T(8,128)(2,1)S(1)}, u32[]{:S(2)}, u32[]{:S(2)}) collective-permute-start(bf16[128,128]{1,0:T(8,128)(2,1)} %get-tuple-element.20.own), channel_id=1, source_target_pairs={{0,56},{8,48},{16,40},{24,32},{32,24},{40,16},{48,8},{56,0},{1,57}... | collective-permute-start | bytes 98312 | tf_op jit(solution)/shard_map/ppermute | solution.py:409
  22.5 0.8 copy-start.7
  32.1 0.9 copy-start.6
  48.9 7.9 %copy-start.8 = (bf16[4,912,128]{2,1,0:T(8,128)(2,1)}, bf16[4,912,128]{2,1,0:T(8,128)(2,1)S(1)}, u32[]{:S(2)}) copy-start(bf16[4,912,128]{2,1,0:T(8,128)(2,1)S(1)} %all_to_all.16.own) | copy-start | bytes 2801668
  48.9 7.9 %collective-permute-start.2 = (bf16[4,912,128]{2,1,0:T(8,128)(2,1)S(1)}, bf16[4,912,128]{2,1,0:T(8,128)(2,1)S(1)}, u32[]{:S(2)}, u32[]{:S(2)}) collective-permute-start(bf16[4,912,128]{2,1,0:T(8,128)(2,1)S(1)} %all_to_all.16.own), channel_id=1, source_target_pairs={{0,64},{64,0},{128,192},{192,128},{256,320},{320,256},{384,448},{4... | collective-permute-start | bytes 2801672 | tf_op jit(solution)/shard_map/ppermute | solution.py:409
  56.8 1.0 copy-start
  57.8 21.0 %copy-start.4 = (bf16[512,256]{1,0:T(8,128)(2,1)S(1)}, bf16[512,256]{1,0:T(8,128)(2,1)}, u32[]{:S(2)}) copy-start(bf16[512,256]{1,0:T(8,128)(2,1)} %get-tuple-element.19.cells) | copy-start | bytes 786436
  64.4 28.2 %all-to-all-start.2 = ((s16[8,120,128]{2,1,0:T(8,128)(2,1)}), s16[8,120,128]{2,1,0:T(8,128)(2,1)S(1)}, u32[]{:S(2)}, u32[]{:S(2)}) async-start(s16[8,120,128]{2,1,0:T(8,128)(2,1)} %shard_map.101), calls=%async_computation.2 | async-start | bytes 491520 | tf_op jit(solution)/shard_map/all_to_all | solution.py:472
  75.7 3.1 %collective-permute-start.1 = (bf16[144,128]{1,0:T(8,128)(2,1)S(1)}, bf16[144,128]{1,0:T(8,128)(2,1)S(1)}, u32[]{:S(2)}, u32[]{:S(2)}) collective-permute-start(bf16[144,128]{1,0:T(8,128)(2,1)S(1)} %get-tuple-element.23), channel_id=1, source_target_pairs={{0,64},{64,0},{128,192},{192,128},{256,320},{320,256},{384,448},{4... | collective-permute-start | bytes 110600 | tf_op jit(solution)/shard_map/ppermute | solution.py:409
  78.8 1.2 %copy-start.1 = (bf16[4,912,128]{2,1,0:T(8,128)(2,1)S(1)}, bf16[4,912,128]{2,1,0:T(8,128)(2,1)}, u32[]{:S(2)}) copy-start(bf16[4,912,128]{2,1,0:T(8,128)(2,1)} %copy-done) | copy-start | bytes 2801668
  80.1 18.5 %copy-start.2 = (bf16[12,40,384]{2,1,0:T(8,128)(2,1)}, bf16[12,40,384]{2,1,0:T(8,128)(2,1)S(1)}, u32[]{:S(2)}) copy-start(bf16[12,40,384]{2,1,0:T(8,128)(2,1)S(1)} %get-tuple-element.25.own_low) | copy-start | bytes 1105924
  80.2 18.5 %copy-start.3 = (bf16[12,40,384]{2,1,0:T(8,128)(2,1)}, bf16[12,40,384]{2,1,0:T(8,128)(2,1)S(1)}, u32[]{:S(2)}) copy-start(bf16[12,40,384]{2,1,0:T(8,128)(2,1)S(1)} %get-tuple-element.26.own_high) | copy-start | bytes 1105924
  80.2 18.5 %collective-permute-start.4 = (bf16[12,40,384]{2,1,0:T(8,128)(2,1)S(1)}, bf16[12,40,384]{2,1,0:T(8,128)(2,1)S(1)}, u32[]{:S(2)}, u32[]{:S(2)}) collective-permute-start(bf16[12,40,384]{2,1,0:T(8,128)(2,1)S(1)} %get-tuple-element.25.own_low), channel_id=1, source_target_pairs={{1,0},{2,1},{3,2},{4,3},{5,4},{6,5},{7,6},{9,8},{10,9},{11,10},{12... | collective-permute-start | bytes 1105928 | tf_op jit(solution)/shard_map/ppermute | solution.py:461
  82.1 16.5 %collective-permute-start.3 = (bf16[12,40,384]{2,1,0:T(8,128)(2,1)S(1)}, bf16[12,40,384]{2,1,0:T(8,128)(2,1)S(1)}, u32[]{:S(2)}, u32[]{:S(2)}) collective-permute-start(bf16[12,40,384]{2,1,0:T(8,128)(2,1)S(1)} %get-tuple-element.26.own_high), channel_id=1, source_target_pairs={{0,1},{1,2},{2,3},{3,4},{4,5},{5,6},{6,7},{8,9},{9,10},{10,11},{11... | collective-permute-start | bytes 1105928 | tf_op jit(solution)/shard_map/ppermute | solution.py:460
  92.7 14.4 %copy-start.5 = (f32[120,128]{1,0:T(8,128)}, f32[120,128]{1,0:T(8,128)S(1)}, u32[]{:S(2)}) copy-start(f32[120,128]{1,0:T(8,128)S(1)} %shard_map.102.d_own) | copy-start | bytes 184324
  92.8 14.3 %collective-permute-start.6 = (f32[120,128]{1,0:T(8,128)S(1)}, f32[120,128]{1,0:T(8,128)S(1)}, u32[]{:S(2)}, u32[]{:S(2)}) collective-permute-start(f32[120,128]{1,0:T(8,128)S(1)} %shard_map.102.d_own), channel_id=1, source_target_pairs={{1,0},{2,1},{3,2},{4,3},{5,4},{6,5},{7,6},{9,8},{10,9},{11,10},{12... | collective-permute-start | bytes 184328 | tf_op jit(solution)/shard_map/ppermute | solution.py:483
  94.7 12.4 %collective-permute-start.5 = (f32[120,128]{1,0:T(8,128)S(1)}, f32[120,128]{1,0:T(8,128)S(1)}, u32[]{:S(2)}, u32[]{:S(2)}) collective-permute-start(f32[120,128]{1,0:T(8,128)S(1)} %shard_map.102.d_own), channel_id=1, source_target_pairs={{0,1},{1,2},{2,3},{3,4},{4,5},{5,6},{6,7},{8,9},{9,10},{10,11},{11... | collective-permute-start | bytes 184328 | tf_op jit(solution)/shard_map/ppermute | solution.py:482
  98.6 0.8 copy-start.9
  99.4 0.8 copy-start.10
  107.1 0.6 copy-start.11
  107.1 0.6 copy-start.12

commit v5 on v4

--- a/solution.py
+++ b/solution.py
@@ -28,6 +28,28 @@
     return lax.dot_general(a, b, (dims, ((), ())), preferred_element_type=f32)
 
 
+class Planes:
+    def __init__(self, ref, base, inner=0):
+        self.ref, self.base, self.inner = ref, base, inner
+
+    def key(self, k):
+        k = k if isinstance(k, tuple) else (k,)
+        if self.inner:
+            return (self.base + k[0] * self.inner + k[1],) + k[2:]
+        return (self.base + k[0],) + k[1:]
+
+    def __getitem__(self, k):
+        return self.ref[self.key(k)]
+
+    def __setitem__(self, k, value):
+        self.ref[self.key(k)] = value
+
+
+def parts_of(ref):
+    layout = ((0, 10), (30, 8), (54, 0), (64, 0), (74, 0), (84, 0))
+    return [Planes(ref, base, inner) for base, inner in layout]
+
+
 def lookup(ids, table):
     bits = [(ids & (1 << k)) != 0 for k in range(4)]
     level = [table[k] for k in range(16)]
@@ -36,7 +58,7 @@
     return level[0]
 
 
-def call(body, out_shape, in_specs, scratch=(), flops=0, nbytes=0, vmem=None):
+def call(body, out_shape, in_specs, scratch=(), flops=0, nbytes=0, vmem=None, alias={}):
     outs = out_shape if isinstance(out_shape, list) else [out_shape]
     result = pl.pallas_call(
         body,
@@ -44,13 +66,14 @@
         in_specs=in_specs,
         out_specs=[VM] * len(outs),
         scratch_shapes=list(scratch),
+        input_output_aliases=alias,
         compiler_params=pltpu.CompilerParams(vmem_limit_bytes=vmem),
         cost_estimate=pl.CostEstimate(flops=flops, bytes_accessed=nbytes, transcendentals=0),
     )
     return result
 
 
-def coarse_kernel(mag, grains, sat, out, edges, cells_out, scr):
+def coarse_kernel(mag, grains, sat, out, scr):
     for a in range(2):
         s0 = lookup(grains[2 * a], sat)
         s1 = lookup(grains[2 * a + 1], sat)
@@ -73,20 +96,24 @@
     faces = jnp.concatenate([faces[:, 128 * q : 128 * (q + 1)] for q in range(4)], axis=0).astype(bf16)
     out[0:96, :] = coarse
     out[96:128, :] = faces
-    cells_out[...] = cells
+
+
+def block_kernel(mag, grains, own, edges, cells, out):
+    for n in range(4):
+        out[n, 0:128, :] = own[...]
+        out[n, 128:256, :] = own[...]
     for c in range(4):
         for z in range(4):
-            at = (c * 4 + z) * 3
+            at = c * 4 + z
             plane = mag[c, z] if c < 3 else grains[z].astype(f32)
-            edges[0, at : at + 3, :] = plane[0:3]
-            edges[1, at : at + 3, :] = plane[29:32]
-
-
-def pair_kernel(own, other, out):
+            edges[0, 3 * at : 3 * at + 3, :] = plane[0:3]
+            edges[1, 3 * at : 3 * at + 3, :] = plane[29:32]
+            cells[32 * at : 32 * at + 32, :] = plane.astype(bf16)
+
+
+def pair_kernel(block, other, out):
     for n in range(4):
-        out[n, 0:96, :] = own[0:96]
-        out[n, 96:192, :] = other[0:96]
-        out[n, 192:224, :] = own[96:128]
+        out[n, 128:256, :] = other[...]
 
 
 def toeplitz_kernel(kernel_x, kernel_y, kernel_z, mixing, strip, kx_out, wz_out, kyp):
@@ -137,18 +164,16 @@
         kx_out[r * 24 : (r + 1) * 24, :] = total[:, :128]
 
 
-def faces_kernel(gathered, other, edges, pay, face_a, rim, low, high):
+def faces_kernel(gathered, edges, pay, face_a, rim, low, high):
     gx, gy = lax.axis_index("gx"), lax.axis_index("gy")
     y = gy & 3
 
-    def faces(rows):
-        return jnp.concatenate([rows[8 * n : 8 * (n + 1)] for n in range(4)], axis=1)
-
-    across = faces(other[96:128, :].astype(f32))
-    right = faces(gathered[jnp.minimum(y + 1, 3), 192:224, :].astype(f32))
-    left = faces(gathered[jnp.maximum(y - 1, 0), 192:224, :].astype(f32))
-    right = jnp.where(gy == 3, across, right)
-    left = jnp.where(gy == 4, across, left)
+    def faces(n, row):
+        rows = gathered[n, row : row + 32, :].astype(f32)
+        return jnp.concatenate([rows[8 * q : 8 * (q + 1)] for q in range(4)], axis=1)
+
+    right = jnp.where(gy == 3, faces(0, 224), faces(jnp.minimum(y + 1, 3), 96))
+    left = jnp.where(gy == 4, faces(3, 224), faces(jnp.maximum(y - 1, 0), 96))
     sel = jnp.where(iota((8, 512), 0) < 4, right, left)
     k, lane = iota((8, 128), 0), iota((8, 128), 1)
     put = one_hot(((k < 3) & (lane == k)) | ((k >= 4) & (k < 7) & (lane == 121 + k)))
@@ -166,7 +191,7 @@
     for n in range(4):
         for k in range(4):
             pay[n, k * 96 : (k + 1) * 96, :] = gathered[k, 0:96, :]
-            pay[n, (k + 4) * 96 : (k + 5) * 96, :] = gathered[k, 96:192, :]
+            pay[n, (k + 4) * 96 : (k + 5) * 96, :] = gathered[k, 128:224, :]
         pay[n, 768:816, :] = to_b[0][:, :128]
         pay[n, 816:864, :] = to_b[0][:, 128:]
         pay[n, 864:912, :] = to_b[1]
@@ -231,7 +256,7 @@
         for kp in range(4):
             tiles = []
             for k in (2 * kp, 2 * kp + 1):
-                block = (gy & 4) + k if k < 4 else 11 - (gy & 4) - k
+                block = (gy & 4) + k if k < 4 else k - (gy & 4)
                 at = pl.multiple_of(128 * (8 + gy - block), 128)
                 after, before = strip[r, :, pl.ds(at + 128, 128)], strip[r, :, pl.ds(at - 128, 128)]
                 ends = jnp.where(first_half, after, before)
@@ -274,7 +299,8 @@
     out[114:120] = jnp.zeros((6, 128), f32)
 
 
-def weights_kernel(mag, own_low, own_high, z_low, z_high, stiff, sat, m0, hh, wx, wy, wz, ss, aa):
+def weights_kernel(mag, own_low, own_high, z_low, z_high, stiff, sat, fields, aa):
+    m0, hh, wx, wy, wz, ss = parts_of(fields)
     gx, gy, gz = (lax.axis_index(n) for n in ("gx", "gy", "gz"))
     row, col = iota((40, 384), 0), iota((40, 384), 1)
     inside = ((row < 32) | ((row < 36) & (gx < 7)) | ((row >= 36) & (gx > 0))) & (
@@ -330,12 +356,12 @@
 
 
 def substeps_kernel(
-    m0_hbm, hh_hbm, wx_hbm, wy_hbm, wz_hbm, ss_hbm, d_own, d_low, d_high, state_out, demag_out,
-    m0, hh, wx, wy, wz, ss, m1, m2, fz, field, rows, spread, sems,
+    fields_hbm, d_own, d_low, d_high, state_out, demag_out, fields, m1, m2, fz, field, rows, spread, sems
 ):
-    pairs = ((m0_hbm, m0), (hh_hbm, hh), (wx_hbm, wx), (wy_hbm, wy), (wz_hbm, wz), (ss_hbm, ss))
-    fetches = [pltpu.make_async_copy(a, b, sems.at[n]) for n, (a, b) in enumerate(pairs)]
-    for fetch in fetches[:2]:
+    m0, hh, wx, wy, wz, ss = parts_of(fields)
+    cuts = (pl.ds(0, 54), pl.ds(54, 40))
+    fetches = [pltpu.make_async_copy(fields_hbm.at[c], fields.at[c], sems.at[n]) for n, c in enumerate(cuts)]
+    for fetch in fetches:
         fetch.start()
     for q in range(6):
         demag_out[q // 3, q % 3] = d_own[pl.ds(6 + q, 16, stride=6), :]
@@ -369,11 +395,8 @@
         field[g] = dot(tall, hi) + dot(tall, lo)
     for step in range(3):
         src, dst = ((m0, m1), (m1, m2), (m2, None))[step]
-        for fetch in (fetches[:2], fetches[2:], ())[step]:
-            fetch.wait()
-        if step == 0:
-            for fetch in fetches[2:]:
-                fetch.start()
+        if step < 2:
+            fetches[step].wait()
         first, last = step + 1, 8 - step
 
         def plane(p, carry):
@@ -414,16 +437,24 @@
     up = [(i, i + 1) for i in range(7)]
     down = [(i + 1, i) for i in range(7)]
     big = (10, 40, 384)
-    pay, edges, cells = call(
+    (pay,) = call(
         coarse_kernel,
-        [shape((128, 128), bf16), shape((2, 48, 256), f32), shape((512, 256), bf16)],
+        shape((128, 128), bf16),
         [VM, VM, SM],
         [pltpu.VMEM((6, 32, 256), f32)],
         20_000_000,
         600_000,
-        FULL - 520_000,
     )(magnet, grains, saturation_table)
-    other = swap(pay, "gy", 7)
+    other = swap(pay, "gy", 4)
+    edges, cells, block = call(
+        block_kernel,
+        [shape((2, 48, 256), f32), shape((512, 256), bf16), shape((4, 256, 128), bf16)],
+        [VM] * 3,
+        (),
+        1_000_000,
+        1_500_000,
+        16 << 20,
+    )(magnet, grains, pay)
     strip, kx, wz = call(
         toeplitz_kernel,
         [shape((8, 128, 2176), bf16), shape((192, 128), f32), shape((64, 192), bf16)],
@@ -431,19 +462,20 @@
         [pltpu.VMEM((8, 2176), f32)],
         20_000_000,
         5_000_000,
+        FULL - 14_000_000,
     )(kernel_x, kernel_y, kernel_z, mixing.transpose(1, 2, 0))
-    (pay,) = call(pair_kernel, shape((4, 224, 128), bf16), [VM] * 2, (), 1000, 400_000, 8 << 20)(pay, other)
+    (pay,) = call(pair_kernel, shape((4, 256, 128), bf16), [VM] * 2, (), 1000, 400_000, 8 << 20, {0: 0})(block, other)
     groups = [[0, 1, 2, 3], [4, 5, 6, 7]]
     gathered = lax.all_to_all(pay, "gy", 0, 0, tiled=True, axis_index_groups=groups)
     pay, face_a, rim = call(
         faces_kernel,
         [shape((4, 912, 128), bf16), shape((144, 128), bf16), shape((512, 128), bf16)],
-        [VM] * 3,
+        [VM] * 2,
         [pltpu.VMEM((48, 128), f32)] * 2,
         1_000_000,
         1_000_000,
         8 << 20,
-    )(gathered, other, edges)
+    )(gathered, edges)
     groups = [[0, 2, 4, 6], [1, 3, 5, 7]]
     gathered = lax.all_to_all(pay, "gx", 0, 0, tiled=True, axis_index_groups=groups)
     near = swap(face_a, "gx", 1)
@@ -467,12 +499,12 @@
         + [pltpu.VMEM((8, 128, 2176), bf16), pltpu.SemaphoreType.DMA],
         2_000_000_000,
         10_000_000,
-        FULL - (4 << 20),
+        FULL - (16 << 20),
     )(gathered, rc, kx, strip, wz)
     parts = lax.all_to_all(parts, "gz", 0, 0, tiled=True)
-    fields = call(
+    (fields,) = call(
         weights_kernel,
-        [shape((3,) + big, f32), shape((3, 8, 40, 384), f32)] + [shape(big, f32)] * 4,
+        shape((94, 40, 384), f32),
         [VM] * 5 + [SM] * 2,
         [pltpu.VMEM(big, f32)],
         20_000_000,
@@ -484,16 +516,15 @@
     state, demag = call(
         substeps_kernel,
         [shape((3, 4, 32, 256), f32), shape((2, 3, 16, 128), f32)],
-        [HB] * 6 + [VM] * 3,
-        [pltpu.VMEM((3,) + big, f32), pltpu.VMEM((3, 8, 40, 384), f32)]
-        + [pltpu.VMEM(big, f32)] * 4
+        [HB] + [VM] * 3,
+        [pltpu.VMEM((94, 40, 384), f32)]
         + [pltpu.VMEM((3,) + big, f32)] * 2
         + [pltpu.VMEM((3, 40, 384), f32), pltpu.VMEM((12, 40, 384), f32)]
-        + [pltpu.VMEM((288, 256), f32), pltpu.VMEM((288, 384), f32), pltpu.SemaphoreType.DMA((6,))],
+        + [pltpu.VMEM((288, 256), f32), pltpu.VMEM((288, 384), f32), pltpu.SemaphoreType.DMA((2,))],
         50_000_000,
         5_000_000,
-        FULL - 300_000,
-    )(*fields, d_own, d_low, d_high)
+        FULL - 14_000_000,
+    )(fields, d_own, d_low, d_high)
     return (state, demag)
 
 

time: 117 us -> 112 us (0.957)
  starting transfers between devices: 44 us -> 40 us
  Pallas kernels: 30.6 us -> 27.5 us
  blocking collectives: 24.5 us -> 27.2 us
  waiting for transfers between devices: 10.3 us -> 9.04 us
    ppermute x3, starting transfers between devices: 21.1 us -> 18.6 us  [swap(): return lax.ppermute(value, axis, [(i, i ^ bit) for i in range(8)])]
    ppermute x3, waiting for transfers between devices: 3.62 us -> 1.18 us  [swap(): return lax.ppermute(value, axis, [(i, i ^ bit) for i in range(8)])]
    all_to_all x1, blocking collectives: 8.88 us -> 10.9 us  [step(): lax.all_to_all(pay, 'gy', 0, 0, tiled=True, axis_index_groups=groups)]
    pallas_call x1, Pallas kernels: 8.32 us -> 6.69 us  [step(): call(substeps_kernel, [shape((3, 4, 32, 256), f32), shape((2, 3, 16, 128)...]
    all_to_all x1, starting transfers between devices: 11.3 us -> 9.69 us  [step(): parts = lax.all_to_all(parts, 'gz', 0, 0, tiled=True)]
    pallas_call x1, Pallas kernels: 6.6 us -> 5.1 us  [step(): call(stages_kernel, shape((8, 120, 128), jnp.int16), [VM, VM, VM, HB, VM]...]
    all_to_all x1, waiting for transfers between devices: 6.65 us -> 7.84 us  [step(): parts = lax.all_to_all(parts, 'gz', 0, 0, tiled=True)]
    unnamed x26 -> x22, local copies, waits for them, and re-layouts: 5.89 us -> 6.95 us
  transfers between devices with their start and end apart: 8 -> 8, of which waited for: 3 -> 2; matrix products, arithmetic and copies ran while one was open for 0% -> 0% of each run, Pallas kernels for 11% -> 12%
where the time goes in v5:
time: 112 us
  starting transfers between devices  40 us (36%)
  Pallas kernels  27.5 us (25%)
  blocking collectives  27.2 us (24%)
  waiting for transfers between devices  9.04 us (8%)
  local copies, waits for them, and re-layouts  6.95 us (6%)
    ppermute x3, starting transfers between devices, swap(): return lax.ppermute(value, axis, [(i, i ^ bit) for i in range(8)])  18.6 us
    all_to_all x1, blocking collectives, step(): lax.all_to_all(pay, 'gx', 0, 0, tiled=True, axis_index_groups=groups)  16.3 us
    all_to_all x1, blocking collectives, step(): lax.all_to_all(pay, 'gy', 0, 0, tiled=True, axis_index_groups=groups)  10.9 us
    all_to_all x1, starting transfers between devices, step(): parts = lax.all_to_all(parts, 'gz', 0, 0, tiled=True)  9.69 us
    all_to_all x1, waiting for transfers between devices, step(): parts = lax.all_to_all(parts, 'gz', 0, 0, tiled=True)  7.84 us
    pallas_call x1, Pallas kernels, step(): call(weights_kernel, shape((94, 40, 384), f32), [VM] * 5 + [SM] * 2, [plt...  7.35 us
    unnamed x22, local copies, waits for them, and re-layouts  6.95 us
    pallas_call x1, Pallas kernels, step(): call(substeps_kernel, [shape((3, 4, 32, 256), f32), shape((2, 3, 16, 128)...  6.69 us
  transfers between devices with their start and end apart: 8, of which 2 were waited for; matrix products, arithmetic and copies ran while one was open for 0% of the time, Pallas kernels for 12%

profile of v5, /device:TPU:32, one launch (start us, length us, event | category | flops | bytes accessed | tf_op | source)
XLA Modules:
  0.0 111.5 jit_solution(8254502872107869618)
XLA Ops:
  0.6 2.1 %shard_map.95.own = bf16[128,128]{1,0:T(8,128)(2,1)} custom-call(f32[3,4,32,256]{3,2,1,0:T(8,128)} %mag.5, s32[4,32,256]{2,1,0:T(8,128)} %grains.3, f32[16]{0:T(128)} %sat.3), custom_call_target="tpu_custom_call" | custom-call | flops 20000000 | bytes 600000 | tf_op jit(solution)/shard_map/pallas_call | solution.py:440
  2.7 14.8 %collective-permute-start = (bf16[128,128]{1,0:T(8,128)(2,1)}, bf16[128,128]{1,0:T(8,128)(2,1)S(1)}, u32[]{:S(2)}, u32[]{:S(2)}) collective-permute-start(bf16[128,128]{1,0:T(8,128)(2,1)} %shard_map.95.own), channel_id=1, source_target_pairs={{0,32},{8,40},{16,48},{24,56},{32,0},{40,8},{48,16},{56,24},{1,33}... | collective-permute-start | bytes 98312 | tf_op jit(solution)/shard_map/ppermute | solution.py:432
  17.5 0.0 copy-start
  17.5 1.0 copy-done
  18.5 0.0 copy-start.1
  18.5 0.9 copy-done.1
  19.4 0.0 copy-start.4
  19.4 0.8 copy-done.4
  20.2 0.1 shard_map.96
  20.2 0.0 collective-permute-done.other
  20.3 10.9 %all_to_all.15.gathered = bf16[4,256,128]{2,1,0:T(8,128)(2,1)S(1)} all-to-all(bf16[4,256,128]{2,1,0:T(8,128)(2,1)S(1)} %shard_map.97), channel_id=1, replica_groups={{0,8,16,24},{32,40,48,56},{1,9,17,25},{33,41,49,57},{2,10,18,26},{34,42..., dimensions={0} | all-to-all | bytes 524288 | tf_op jit(solution)/shard_map/all_to_all | solution.py:469
  31.2 0.3 shard_map.98
  31.5 16.3 %all_to_all.16.own = bf16[4,912,128]{2,1,0:T(8,128)(2,1)S(1)} all-to-all(bf16[4,912,128]{2,1,0:T(8,128)(2,1)S(1)} %get-tuple-element.18), channel_id=1, replica_groups={{0,128,256,384},{64,192,320,448},{1,129,257,385},{65,193,321,449},{2,13..., dimensions={0} | all-to-all | bytes 1867776 | tf_op jit(solution)/shard_map/all_to_all | solution.py:480
  47.8 1.9 %collective-permute-start.2 = (bf16[4,912,128]{2,1,0:T(8,128)(2,1)S(1)}, bf16[4,912,128]{2,1,0:T(8,128)(2,1)S(1)}, u32[]{:S(2)}, u32[]{:S(2)}) collective-permute-start(bf16[4,912,128]{2,1,0:T(8,128)(2,1)S(1)} %all_to_all.16.own), channel_id=1, source_target_pairs={{0,64},{64,0},{128,192},{192,128},{256,320},{320,256},{384,448},{4... | collective-permute-start | bytes 2801672 | tf_op jit(solution)/shard_map/ppermute | solution.py:432
  49.7 0.0 copy-start.5
  49.7 0.7 copy-done.5
  50.5 0.0 copy-start.6
  50.5 0.7 copy-done.6
  51.1 0.0 copy-start.7
  51.2 0.7 copy-done.7
  51.8 0.0 copy-start.8
  51.8 0.7 copy-done.8
  52.5 5.7 %shard_map.101 = (bf16[8,128,2176]{2,1,0:T(8,128)(2,1)}, f32[192,128]{1,0:T(8,128)S(1)}, bf16[64,192]{1,0:T(8,128)(2,1)S(1)}) custom-call(bf16[8,256]{1,0:T(8,128)(2,1)S(1)} %copy-done.7, bf16[8,2048]{1,0:T(8,128)(2,1)S(1)} %copy-done.5, bf16[8,32]{1,0:T(8,128)(2,1)S(1)} %copy-done.8, f32[3,3,8]{2,1,0:T(4,128)S(1)} %bitcast.1), custom_call_target="tpu_custom_call" | custom-call | flops 20000000 | bytes 5000000 | tf_op jit(solution)/shard_map/pallas_call | solution.py:458
  58.2 0.0 collective-permute-done.2.rc
  58.2 5.1 %shard_map.102 = s16[8,120,128]{2,1,0:T(8,128)(2,1)} custom-call(bf16[4,912,128]{2,1,0:T(8,128)(2,1)S(1)} %all_to_all.16.own, bf16[4,912,128]{2,1,0:T(8,128)(2,1)S(1)} %collective-permute-done.2.rc, f32[192,128]{1,0:T(8,128)S(1)} %get-tuple-element.21.kx, bf16[8,128,2176]{2,1,0:T(8,128)(2,1)} %get-tuple-element.22.strip_hbm, ...), custom_call_target="tpu_custom_call" | custom-call | flops 2000000000 | bytes 10000000 | tf_op jit(solution)/shard_map/pallas_call | solution.py:494
  63.4 9.7 %all-to-all-start.2 = ((s16[8,120,128]{2,1,0:T(8,128)(2,1)}), s16[8,120,128]{2,1,0:T(8,128)(2,1)S(1)}, u32[]{:S(2)}, u32[]{:S(2)}) async-start(s16[8,120,128]{2,1,0:T(8,128)(2,1)} %shard_map.102), calls=%async_computation.2 | async-start | bytes 491520 | tf_op jit(solution)/shard_map/all_to_all | solution.py:504
  73.0 1.9 %collective-permute-start.1 = (bf16[144,128]{1,0:T(8,128)(2,1)S(1)}, bf16[144,128]{1,0:T(8,128)(2,1)S(1)}, u32[]{:S(2)}, u32[]{:S(2)}) collective-permute-start(bf16[144,128]{1,0:T(8,128)(2,1)S(1)} %get-tuple-element.17), channel_id=1, source_target_pairs={{0,64},{64,0},{128,192},{192,128},{256,320},{320,256},{384,448},{4... | collective-permute-start | bytes 110600 | tf_op jit(solution)/shard_map/ppermute | solution.py:432
  75.0 1.2 %collective-permute-done.1.near = bf16[144,128]{1,0:T(8,128)(2,1)S(1)} collective-permute-done((bf16[144,128]{1,0:T(8,128)(2,1)S(1)}, bf16[144,128]{1,0:T(8,128)(2,1)S(1)}, u32[]{:S(2)}, u32[]{:S(2)}) %collective-permute-start.1) | collective-permute-done | bytes 36896 | tf_op jit(solution)/shard_map/ppermute | solution.py:432
  76.1 0.2 shard_map.99
  76.3 0.0 copy-start.2
  76.3 0.0 copy-start.3
  76.3 1.9 %collective-permute-start.4 = (bf16[12,40,384]{2,1,0:T(8,128)(2,1)S(1)}, bf16[12,40,384]{2,1,0:T(8,128)(2,1)S(1)}, u32[]{:S(2)}, u32[]{:S(2)}) collective-permute-start(bf16[12,40,384]{2,1,0:T(8,128)(2,1)S(1)} %get-tuple-element.19.own_low), channel_id=1, source_target_pairs={{1,0},{2,1},{3,2},{4,3},{5,4},{6,5},{7,6},{9,8},{10,9},{11,10},{12... | collective-permute-start | bytes 1105928 | tf_op jit(solution)/shard_map/ppermute | solution.py:493
  78.3 3.9 %collective-permute-start.3 = (bf16[12,40,384]{2,1,0:T(8,128)(2,1)S(1)}, bf16[12,40,384]{2,1,0:T(8,128)(2,1)S(1)}, u32[]{:S(2)}, u32[]{:S(2)}) collective-permute-start(bf16[12,40,384]{2,1,0:T(8,128)(2,1)S(1)} %get-tuple-element.20.own_high), channel_id=1, source_target_pairs={{0,1},{1,2},{2,3},{3,4},{4,5},{5,6},{6,7},{8,9},{9,10},{10,11},{11... | collective-permute-start | bytes 1105928 | tf_op jit(solution)/shard_map/ppermute | solution.py:492
  82.2 7.8 %all-to-all-done.2.parts = s16[8,120,128]{2,1,0:T(8,128)(2,1)S(1)} async-done(((s16[8,120,128]{2,1,0:T(8,128)(2,1)}), s16[8,120,128]{2,1,0:T(8,128)(2,1)S(1)}, u32[]{:S(2)}, u32[]{:S(2)}) %all-to-all-start.2) | async-done | bytes 245792 | tf_op jit(solution)/shard_map/all_to_all | solution.py:504
  90.0 0.1 shard_map.103.d_own
  90.1 2.1 %collective-permute-start.6 = (f32[120,128]{1,0:T(8,128)S(1)}, f32[120,128]{1,0:T(8,128)S(1)}, u32[]{:S(2)}, u32[]{:S(2)}) collective-permute-start(f32[120,128]{1,0:T(8,128)S(1)} %shard_map.103.d_own), channel_id=1, source_target_pairs={{1,0},{2,1},{3,2},{4,3},{5,4},{6,5},{7,6},{9,8},{10,9},{11,10},{12... | collective-permute-start | bytes 184328 | tf_op jit(solution)/shard_map/ppermute | solution.py:515
  92.2 3.7 %collective-permute-start.5 = (f32[120,128]{1,0:T(8,128)S(1)}, f32[120,128]{1,0:T(8,128)S(1)}, u32[]{:S(2)}, u32[]{:S(2)}) collective-permute-start(f32[120,128]{1,0:T(8,128)S(1)} %shard_map.103.d_own), channel_id=1, source_target_pairs={{0,1},{1,2},{2,3},{3,4},{4,5},{5,6},{6,7},{8,9},{9,10},{10,11},{11... | collective-permute-start | bytes 184328 | tf_op jit(solution)/shard_map/ppermute | solution.py:514
  96.0 0.0 collective-permute-done.4.z_high
  96.0 0.0 copy-start.9
  96.0 0.0 collective-permute-done.3.z_low
  96.0 0.0 copy-done.2
  96.0 0.0 copy-done.3
  96.0 0.7 copy-done.9
  96.7 0.8 copy-done.10
  97.5 7.4 %shard_map.100.fields_hbm = f32[94,40,384]{2,1,0:T(8,128)} custom-call(f32[3,4,32,256]{3,2,1,0:T(8,128)} %mag.5, bf16[12,40,384]{2,1,0:T(8,128)(2,1)} %copy-done.2, bf16[12,40,384]{2,1,0:T(8,128)(2,1)} %copy-done.3, bf16[12,40,384]{2,1,0:T(8,128)(2,1)} %copy-done.10, bf16[12,40,384]{2,1,0:T(8,128)(2,1)} %copy-done.9, f32[16]{0:T(128)} %stiff.1, f32[16]{0:T(128)} %sat.3), custom_call_target="tpu_custom_call" | custom-call | flops 20000000 | bytes 5000000 | tf_op jit(solution)/shard_map/pallas_call | solution.py:505
  104.8 0.0 collective-permute-done.6.d_high
  104.8 0.0 collective-permute-done.5.d_low
  104.9 6.7 %shard_map.104 = (f32[3,4,32,256]{3,2,1,0:T(8,128)}, f32[2,3,16,128]{3,2,1,0:T(8,128)}) custom-call(f32[94,40,384]{2,1,0:T(8,128)} %shard_map.100.fields_hbm, f32[120,128]{1,0:T(8,128)S(1)} %shard_map.103.d_own, f32[120,128]{1,0:T(8,128)S(1)} %collective-permute-done.5.d_low, f32[120,128]{1,0:T(8,128)S(1)} %collective-permute-done.6.d_high), custom_call_target="tpu_custom_call" | custom-call | flops 50000000 | bytes 5000000 | tf_op jit(solution)/shard_map/pallas_call | solution.py:516
  (2 shorter events, 0.0 us)
Async XLA Ops:
  2.7 17.6 %collective-permute-start = (bf16[128,128]{1,0:T(8,128)(2,1)}, bf16[128,128]{1,0:T(8,128)(2,1)S(1)}, u32[]{:S(2)}, u32[]{:S(2)}) collective-permute-start(bf16[128,128]{1,0:T(8,128)(2,1)} %shard_map.95.own), channel_id=1, source_target_pairs={{0,32},{8,40},{16,48},{24,56},{32,0},{40,8},{48,16},{56,24},{1,33}... | collective-permute-start | bytes 98312 | tf_op jit(solution)/shard_map/ppermute | solution.py:432
  17.5 1.0 copy-start
  18.5 0.9 copy-start.1
  19.4 0.8 copy-start.4
  47.8 10.5 %collective-permute-start.2 = (bf16[4,912,128]{2,1,0:T(8,128)(2,1)S(1)}, bf16[4,912,128]{2,1,0:T(8,128)(2,1)S(1)}, u32[]{:S(2)}, u32[]{:S(2)}) collective-permute-start(bf16[4,912,128]{2,1,0:T(8,128)(2,1)S(1)} %all_to_all.16.own), channel_id=1, source_target_pairs={{0,64},{64,0},{128,192},{192,128},{256,320},{320,256},{384,448},{4... | collective-permute-start | bytes 2801672 | tf_op jit(solution)/shard_map/ppermute | solution.py:432
  49.7 0.8 copy-start.5
  50.5 0.7 copy-start.6
  51.1 0.7 copy-start.7
  51.8 0.7 copy-start.8
  63.4 26.7 %all-to-all-start.2 = ((s16[8,120,128]{2,1,0:T(8,128)(2,1)}), s16[8,120,128]{2,1,0:T(8,128)(2,1)S(1)}, u32[]{:S(2)}, u32[]{:S(2)}) async-start(s16[8,120,128]{2,1,0:T(8,128)(2,1)} %shard_map.102), calls=%async_computation.2 | async-start | bytes 491520 | tf_op jit(solution)/shard_map/all_to_all | solution.py:504
  73.0 3.1 %collective-permute-start.1 = (bf16[144,128]{1,0:T(8,128)(2,1)S(1)}, bf16[144,128]{1,0:T(8,128)(2,1)S(1)}, u32[]{:S(2)}, u32[]{:S(2)}) collective-permute-start(bf16[144,128]{1,0:T(8,128)(2,1)S(1)} %get-tuple-element.17), channel_id=1, source_target_pairs={{0,64},{64,0},{128,192},{192,128},{256,320},{320,256},{384,448},{4... | collective-permute-start | bytes 110600 | tf_op jit(solution)/shard_map/ppermute | solution.py:432
  76.3 19.7 %copy-start.2 = (bf16[12,40,384]{2,1,0:T(8,128)(2,1)}, bf16[12,40,384]{2,1,0:T(8,128)(2,1)S(1)}, u32[]{:S(2)}) copy-start(bf16[12,40,384]{2,1,0:T(8,128)(2,1)S(1)} %get-tuple-element.19.own_low) | copy-start | bytes 1105924
  76.3 19.7 %copy-start.3 = (bf16[12,40,384]{2,1,0:T(8,128)(2,1)}, bf16[12,40,384]{2,1,0:T(8,128)(2,1)S(1)}, u32[]{:S(2)}) copy-start(bf16[12,40,384]{2,1,0:T(8,128)(2,1)S(1)} %get-tuple-element.20.own_high) | copy-start | bytes 1105924
  76.3 19.6 %collective-permute-start.4 = (bf16[12,40,384]{2,1,0:T(8,128)(2,1)S(1)}, bf16[12,40,384]{2,1,0:T(8,128)(2,1)S(1)}, u32[]{:S(2)}, u32[]{:S(2)}) collective-permute-start(bf16[12,40,384]{2,1,0:T(8,128)(2,1)S(1)} %get-tuple-element.19.own_low), channel_id=1, source_target_pairs={{1,0},{2,1},{3,2},{4,3},{5,4},{6,5},{7,6},{9,8},{10,9},{11,10},{12... | collective-permute-start | bytes 1105928 | tf_op jit(solution)/shard_map/ppermute | solution.py:493
  78.3 17.7 %collective-permute-start.3 = (bf16[12,40,384]{2,1,0:T(8,128)(2,1)S(1)}, bf16[12,40,384]{2,1,0:T(8,128)(2,1)S(1)}, u32[]{:S(2)}, u32[]{:S(2)}) collective-permute-start(bf16[12,40,384]{2,1,0:T(8,128)(2,1)S(1)} %get-tuple-element.20.own_high), channel_id=1, source_target_pairs={{0,1},{1,2},{2,3},{3,4},{4,5},{5,6},{6,7},{8,9},{9,10},{10,11},{11... | collective-permute-start | bytes 1105928 | tf_op jit(solution)/shard_map/ppermute | solution.py:492
  90.1 14.7 %collective-permute-start.6 = (f32[120,128]{1,0:T(8,128)S(1)}, f32[120,128]{1,0:T(8,128)S(1)}, u32[]{:S(2)}, u32[]{:S(2)}) collective-permute-start(f32[120,128]{1,0:T(8,128)S(1)} %shard_map.103.d_own), channel_id=1, source_target_pairs={{1,0},{2,1},{3,2},{4,3},{5,4},{6,5},{7,6},{9,8},{10,9},{11,10},{12... | collective-permute-start | bytes 184328 | tf_op jit(solution)/shard_map/ppermute | solution.py:515
  92.2 12.6 %collective-permute-start.5 = (f32[120,128]{1,0:T(8,128)S(1)}, f32[120,128]{1,0:T(8,128)S(1)}, u32[]{:S(2)}, u32[]{:S(2)}) collective-permute-start(f32[120,128]{1,0:T(8,128)S(1)} %shard_map.103.d_own), channel_id=1, source_target_pairs={{0,1},{1,2},{2,3},{3,4},{4,5},{5,6},{6,7},{8,9},{9,10},{10,11},{11... | collective-permute-start | bytes 184328 | tf_op jit(solution)/shard_map/ppermute | solution.py:514
  96.0 0.7 copy-start.9
  96.7 0.8 copy-start.10

commit v6 on v5

--- a/solution.py
+++ b/solution.py
@@ -58,13 +58,13 @@
     return level[0]
 
 
-def call(body, out_shape, in_specs, scratch=(), flops=0, nbytes=0, vmem=None, alias={}):
+def call(body, out_shape, in_specs, scratch=(), flops=0, nbytes=0, vmem=None, out_specs=None, alias={}):
     outs = out_shape if isinstance(out_shape, list) else [out_shape]
     result = pl.pallas_call(
         body,
         out_shape=outs,
         in_specs=in_specs,
-        out_specs=[VM] * len(outs),
+        out_specs=out_specs or [VM] * len(outs),
         scratch_shapes=list(scratch),
         input_output_aliases=alias,
         compiler_params=pltpu.CompilerParams(vmem_limit_bytes=vmem),
@@ -116,10 +116,21 @@
         out[n, 128:256, :] = other[...]
 
 
-def toeplitz_kernel(kernel_x, kernel_y, kernel_z, mixing, strip, kx_out, wz_out, kyp):
+def toeplitz_kernel(kernel_x, kernel_y, kernel_z, mixing, strip_hbm, kx_out, wz_out, kyp, strip, sems):
     gx, gz = lax.axis_index("gx"), lax.axis_index("gz")
     kyp[...] = jnp.zeros_like(kyp)
     kyp[:, 0:2048] = kernel_y[...].astype(f32)
+
+    def send(r):
+        return pltpu.make_async_copy(strip.at[r], strip_hbm.at[r], sems.at[r])
+
+    def one(r, carry):
+        row = jnp.broadcast_to(kyp[pl.ds(r, 1), :], (128, 2176))
+        strip[pl.ds(r, 1)] = pltpu.roll(row, 0, 1, stride=1, stride_axis=0).astype(bf16)[None]
+        send(r).start()
+        return carry
+
+    lax.fori_loop(0, 8, one, 0)
     mirror = one_hot(iota((256, 256), 0) + iota((256, 256), 1) == 255)
     kxr = dot(kernel_x[...], mirror)
     row, col = iota((64, 32), 0), iota((64, 32), 1)
@@ -147,12 +158,6 @@
     wz_out[:, 64:128] = mid
     wz_out[:, 128:192] = (rest - mid.astype(f32)).astype(bf16)
 
-    def one(r, carry):
-        row = jnp.broadcast_to(kyp[pl.ds(r, 1), :], (128, 2176))
-        strip[pl.ds(r, 1)] = pltpu.roll(row, 0, 1, stride=1, stride_axis=0).astype(bf16)[None]
-        return carry
-
-    lax.fori_loop(0, 8, one, 0)
     lane = iota((24, 256), 1)
     for r in range(8):
         row = pltpu.roll(jnp.broadcast_to(kxr[r : r + 1, :], (24, 256)), 0, 1, stride=1, stride_axis=0)
@@ -162,6 +167,8 @@
             shift = (16 * l + 16 * (gx - block) + 128 + 512) & 255
             total = jnp.where(lane // 16 == l, pltpu.roll(row, shift, 1), total)
         kx_out[r * 24 : (r + 1) * 24, :] = total[:, :128]
+    for r in range(8):
+        send(r).wait()
 
 
 def faces_kernel(gathered, edges, pay, face_a, rim, low, high):
@@ -205,21 +212,36 @@
     b = rc[jnp.where(even, jnp.maximum(chip - 1, 0), jnp.minimum(chip + 1, 3)), 768:912, :].astype(f32)
     fa[...] = jnp.where(even, a, b)
     fb[...] = jnp.where(even, b, a)
+    scr[2, 640:672, :] = jnp.zeros((32, 128), f32)
     for z in range(4):
         for c in range(4):
-            plane = (c * 4 + z) * 32
-            scr[0:32, 0:256] = cells[plane : plane + 32, :].astype(f32)
-            scr[0:32, 256:384] = rim[plane : plane + 32, :].astype(f32)
-            scr[32:40, :] = jnp.zeros((8, 384), f32)
+            plane, top, at = (c * 4 + z) * 32, (z * 4 + c) * 40, (c * 4 + z) * 3
             for q in range(3):
-                at = q * 48 + (c * 4 + z) * 3
-                scr[32:35, q * 128 : (q + 1) * 128] = fa[at : at + 3, :]
-                scr[37:40, q * 128 : (q + 1) * 128] = fb[at : at + 3, :]
-            whole = scr[...].astype(bf16)
-            if z < 3:
-                low_out[z * 4 + c] = whole
-            if z > 0:
-                high_out[(z - 1) * 4 + c] = whole
+                if q < 2:
+                    scr[q, top : top + 32] = cells[plane : plane + 32, q * 128 : (q + 1) * 128].astype(f32)
+                else:
+                    scr[q, top : top + 32] = rim[plane : plane + 32, :].astype(f32)
+                scr[q, top + 32 : top + 40] = jnp.zeros((8, 128), f32)
+                scr[q, top + 32 : top + 35] = fa[q * 48 + at : q * 48 + at + 3, :]
+                scr[q, top + 37 : top + 40] = fb[q * 48 + at : q * 48 + at + 3, :]
+    for out, first in ((low_out, 0), (high_out, 160)):
+        for q in range(2):
+            out[q * 480 : (q + 1) * 480, :] = scr[q, first : first + 480].astype(bf16)
+        ends = dot(rim_lanes(), scr[2, first : first + 512].astype(bf16), ((1,), (1,)))
+        ends = jnp.concatenate([ends[:, 128 * n : 128 * (n + 1)] for n in range(4)], axis=0)
+        out[960:992, :] = ends.astype(bf16)
+
+
+def rim_lanes():
+    k, lane = iota((8, 128), 0), iota((8, 128), 1)
+    return one_hot(((k < 3) & (lane == k)) | ((k >= 4) & (k < 7) & (lane == 121 + k)))
+
+
+def unpack_rims(ref):
+    ends = ref[960:992, :].astype(f32)
+    ends = jnp.concatenate([ends[8 * n : 8 * (n + 1)] for n in range(4)], axis=1)
+    ends = dot(ends.astype(bf16), rim_lanes(), ((0,), (0,)))
+    return [ref[0:480, :].astype(f32), ref[480:960, :].astype(f32), ends]
 
 
 def stages_kernel(own, rc, kx, strip_hbm, wz, packed, ax, ay, out, strip, sem):
@@ -306,18 +328,18 @@
     inside = ((row < 32) | ((row < 36) & (gx < 7)) | ((row >= 36) & (gx > 0))) & (
         (col < 256) | ((col < 320) & (gy < 7)) | ((col >= 320) & (gy > 0))
     )
+    unpacked = [unpack_rims(ref) for ref in (z_low, own_low, own_high, z_high)]
     for p in range(10):
         z = p - 3
         if z < 0:
-            whole = [z_low[p * 4 + c].astype(f32) for c in range(4)]
-            ok = gz > 0
+            chunks, at, ok = unpacked[0], p * 4, gz > 0
         elif z > 3:
-            whole = [z_high[(z - 4) * 4 + c].astype(f32) for c in range(4)]
-            ok = gz < 7
+            chunks, at, ok = unpacked[3], (z - 4) * 4, gz < 7
+        elif z < 3:
+            chunks, at, ok = unpacked[1], z * 4, gz >= 0
         else:
-            ref, at = (own_low, z * 4) if z < 3 else (own_high, 8)
-            whole = [ref[at + c].astype(f32) for c in range(4)]
-            ok = gz >= 0
+            chunks, at, ok = unpacked[2], 8, gz >= 0
+        whole = [jnp.concatenate([v[40 * (at + c) : 40 * (at + c) + 40] for v in chunks], axis=1) for c in range(4)]
         for c in range(3):
             m0[c, p] = whole[c]
             if 0 <= z < 4:
@@ -459,12 +481,13 @@
         toeplitz_kernel,
         [shape((8, 128, 2176), bf16), shape((192, 128), f32), shape((64, 192), bf16)],
         [VM, VM, VM, SM],
-        [pltpu.VMEM((8, 2176), f32)],
+        [pltpu.VMEM((8, 2176), f32), pltpu.VMEM((8, 128, 2176), bf16), pltpu.SemaphoreType.DMA((8,))],
         20_000_000,
         5_000_000,
         FULL - 14_000_000,
+        [HB, VM, VM],
     )(kernel_x, kernel_y, kernel_z, mixing.transpose(1, 2, 0))
-    (pay,) = call(pair_kernel, shape((4, 256, 128), bf16), [VM] * 2, (), 1000, 400_000, 8 << 20, {0: 0})(block, other)
+    (pay,) = call(pair_kernel, shape((4, 256, 128), bf16), [VM] * 2, (), 1000, 400_000, 8 << 20, None, {0: 0})(block, other)
     groups = [[0, 1, 2, 3], [4, 5, 6, 7]]
     gathered = lax.all_to_all(pay, "gy", 0, 0, tiled=True, axis_index_groups=groups)
     pay, face_a, rim = call(
@@ -482,9 +505,9 @@
     rc = swap(gathered, "gx", 1)
     own_low, own_high = call(
         rims_kernel,
-        [shape((12, 40, 384), bf16)] * 2,
+        [shape((992, 128), bf16)] * 2,
         [VM] * 4,
-        [pltpu.VMEM((40, 384), f32), pltpu.VMEM((144, 128), f32), pltpu.VMEM((144, 128), f32)],
+        [pltpu.VMEM((3, 672, 128), f32), pltpu.VMEM((144, 128), f32), pltpu.VMEM((144, 128), f32)],
         1_000_000,
         2_000_000,
         12 << 20,

time: 112 us -> 110 us (0.982)
  Pallas kernels: 27.5 us -> 25.4 us
    pallas_call x1, Pallas kernels: 5.72 us -> 3.51 us  [step(): call(toeplitz_kernel, [shape((8, 128, 2176), bf16), shape((192, 128), f32...]
  transfers between devices with their start and end apart: 8 -> 8, of which waited for: 2 -> 2; matrix products, arithmetic and copies ran while one was open for 0% -> 0% of each run, Pallas kernels for 12% -> 10%
where the time goes in v6:
time: 110 us; the launch traced here: 109 us
  starting transfers between devices  40 us (36%)
  blocking collectives  27.2 us (25%)
  Pallas kernels  25.4 us (23%)
  waiting for transfers between devices  8.93 us (8%)
  local copies, waits for them, and re-layouts  6.83 us (6%)
    ppermute x3, starting transfers between devices, swap(): return lax.ppermute(value, axis, [(i, i ^ bit) for i in range(8)])  18.6 us
    all_to_all x1, blocking collectives, step(): lax.all_to_all(pay, 'gx', 0, 0, tiled=True, axis_index_groups=groups)  16.3 us
    all_to_all x1, blocking collectives, step(): lax.all_to_all(pay, 'gy', 0, 0, tiled=True, axis_index_groups=groups)  10.9 us
    all_to_all x1, starting transfers between devices, step(): parts = lax.all_to_all(parts, 'gz', 0, 0, tiled=True)  9.68 us
    all_to_all x1, waiting for transfers between devices, step(): parts = lax.all_to_all(parts, 'gz', 0, 0, tiled=True)  7.74 us
    pallas_call x1, Pallas kernels, step(): call(weights_kernel, shape((94, 40, 384), f32), [VM] * 5 + [SM] * 2, [plt...  7.34 us
    unnamed x22, local copies, waits for them, and re-layouts  6.83 us
    pallas_call x1, Pallas kernels, step(): call(substeps_kernel, [shape((3, 4, 32, 256), f32), shape((2, 3, 16, 128)...  6.69 us
  transfers between devices with their start and end apart: 8, of which 2 were waited for; matrix products, arithmetic and copies ran while one was open for 0% of the time, Pallas kernels for 10%

profile of v6, /device:TPU:32, one launch (start us, length us, event | category | flops | bytes accessed | tf_op | source)
XLA Modules:
  0.0 109.2 jit_solution(3921223110104339309)
XLA Ops:
  0.6 2.1 %shard_map.95.own = bf16[128,128]{1,0:T(8,128)(2,1)} custom-call(f32[3,4,32,256]{3,2,1,0:T(8,128)} %mag.5, s32[4,32,256]{2,1,0:T(8,128)} %grains.3, f32[16]{0:T(128)} %sat.3), custom_call_target="tpu_custom_call" | custom-call | flops 20000000 | bytes 600000 | tf_op jit(solution)/shard_map/pallas_call | solution.py:462
  2.7 14.8 %collective-permute-start = (bf16[128,128]{1,0:T(8,128)(2,1)}, bf16[128,128]{1,0:T(8,128)(2,1)S(1)}, u32[]{:S(2)}, u32[]{:S(2)}) collective-permute-start(bf16[128,128]{1,0:T(8,128)(2,1)} %shard_map.95.own), channel_id=1, source_target_pairs={{0,32},{8,40},{16,48},{24,56},{32,0},{40,8},{48,16},{56,24},{1,33}... | collective-permute-start | bytes 98312 | tf_op jit(solution)/shard_map/ppermute | solution.py:454
  17.5 0.0 copy-start
  17.5 1.0 copy-done
  18.5 0.0 copy-start.1
  18.5 0.9 copy-done.1
  19.4 0.0 copy-start.4
  19.4 0.8 copy-done.4
  20.2 0.1 shard_map.96
  20.2 0.0 collective-permute-done.other
  20.3 10.9 %all_to_all.15.gathered = bf16[4,256,128]{2,1,0:T(8,128)(2,1)S(1)} all-to-all(bf16[4,256,128]{2,1,0:T(8,128)(2,1)S(1)} %shard_map.97), channel_id=1, replica_groups={{0,8,16,24},{32,40,48,56},{1,9,17,25},{33,41,49,57},{2,10,18,26},{34,42..., dimensions={0} | all-to-all | bytes 524288 | tf_op jit(solution)/shard_map/all_to_all | solution.py:492
  31.2 0.3 shard_map.98
  31.5 16.3 %all_to_all.16.own = bf16[4,912,128]{2,1,0:T(8,128)(2,1)S(1)} all-to-all(bf16[4,912,128]{2,1,0:T(8,128)(2,1)S(1)} %get-tuple-element.18), channel_id=1, replica_groups={{0,128,256,384},{64,192,320,448},{1,129,257,385},{65,193,321,449},{2,13..., dimensions={0} | all-to-all | bytes 1867776 | tf_op jit(solution)/shard_map/all_to_all | solution.py:503
  47.8 1.9 %collective-permute-start.2 = (bf16[4,912,128]{2,1,0:T(8,128)(2,1)S(1)}, bf16[4,912,128]{2,1,0:T(8,128)(2,1)S(1)}, u32[]{:S(2)}, u32[]{:S(2)}) collective-permute-start(bf16[4,912,128]{2,1,0:T(8,128)(2,1)S(1)} %all_to_all.16.own), channel_id=1, source_target_pairs={{0,64},{64,0},{128,192},{192,128},{256,320},{320,256},{384,448},{4... | collective-permute-start | bytes 2801672 | tf_op jit(solution)/shard_map/ppermute | solution.py:454
  49.7 0.0 copy-start.5
  49.7 0.7 copy-done.5
  50.5 0.0 copy-start.6
  50.5 0.7 copy-done.6
  51.1 0.0 copy-start.7
  51.2 0.7 copy-done.7
  51.8 0.0 copy-start.8
  51.8 0.7 copy-done.8
  52.5 3.5 %shard_map.101 = (bf16[8,128,2176]{2,1,0:T(8,128)(2,1)}, f32[192,128]{1,0:T(8,128)S(1)}, bf16[64,192]{1,0:T(8,128)(2,1)S(1)}) custom-call(bf16[8,256]{1,0:T(8,128)(2,1)S(1)} %copy-done.7, bf16[8,2048]{1,0:T(8,128)(2,1)S(1)} %copy-done.5, bf16[8,32]{1,0:T(8,128)(2,1)S(1)} %copy-done.8, f32[3,3,8]{2,1,0:T(4,128)S(1)} %bitcast.1), custom_call_target="tpu_custom_call" | custom-call | flops 20000000 | bytes 5000000 | tf_op jit(solution)/shard_map/pallas_call | solution.py:480
  56.0 0.0 collective-permute-done.2.rc
  56.1 5.1 %shard_map.102 = s16[8,120,128]{2,1,0:T(8,128)(2,1)} custom-call(bf16[4,912,128]{2,1,0:T(8,128)(2,1)S(1)} %all_to_all.16.own, bf16[4,912,128]{2,1,0:T(8,128)(2,1)S(1)} %collective-permute-done.2.rc, f32[192,128]{1,0:T(8,128)S(1)} %get-tuple-element.21.kx, bf16[8,128,2176]{2,1,0:T(8,128)(2,1)} %get-tuple-element.22.strip_hbm, ...), custom_call_target="tpu_custom_call" | custom-call | flops 2000000000 | bytes 10000000 | tf_op jit(solution)/shard_map/pallas_call | solution.py:517
  61.2 9.7 %all-to-all-start.2 = ((s16[8,120,128]{2,1,0:T(8,128)(2,1)}), s16[8,120,128]{2,1,0:T(8,128)(2,1)S(1)}, u32[]{:S(2)}, u32[]{:S(2)}) async-start(s16[8,120,128]{2,1,0:T(8,128)(2,1)} %shard_map.102), calls=%async_computation.2 | async-start | bytes 491520 | tf_op jit(solution)/shard_map/all_to_all | solution.py:527
  70.9 1.9 %collective-permute-start.1 = (bf16[144,128]{1,0:T(8,128)(2,1)S(1)}, bf16[144,128]{1,0:T(8,128)(2,1)S(1)}, u32[]{:S(2)}, u32[]{:S(2)}) collective-permute-start(bf16[144,128]{1,0:T(8,128)(2,1)S(1)} %get-tuple-element.17), channel_id=1, source_target_pairs={{0,64},{64,0},{128,192},{192,128},{256,320},{320,256},{384,448},{4... | collective-permute-start | bytes 110600 | tf_op jit(solution)/shard_map/ppermute | solution.py:454
  72.8 1.2 %collective-permute-done.1.near = bf16[144,128]{1,0:T(8,128)(2,1)S(1)} collective-permute-done((bf16[144,128]{1,0:T(8,128)(2,1)S(1)}, bf16[144,128]{1,0:T(8,128)(2,1)S(1)}, u32[]{:S(2)}, u32[]{:S(2)}) %collective-permute-start.1) | collective-permute-done | bytes 36896 | tf_op jit(solution)/shard_map/ppermute | solution.py:454
  73.9 0.3 shard_map.99
  74.2 0.0 copy-start.2
  74.2 0.0 copy-start.3
  74.2 1.9 %collective-permute-start.4 = (bf16[992,128]{1,0:T(8,128)(2,1)S(1)}, bf16[992,128]{1,0:T(8,128)(2,1)S(1)}, u32[]{:S(2)}, u32[]{:S(2)}) collective-permute-start(bf16[992,128]{1,0:T(8,128)(2,1)S(1)} %get-tuple-element.19.own_low), channel_id=1, source_target_pairs={{1,0},{2,1},{3,2},{4,3},{5,4},{6,5},{7,6},{9,8},{10,9},{11,10},{12... | collective-permute-start | bytes 761864 | tf_op jit(solution)/shard_map/ppermute | solution.py:516
  76.2 3.9 %collective-permute-start.3 = (bf16[992,128]{1,0:T(8,128)(2,1)S(1)}, bf16[992,128]{1,0:T(8,128)(2,1)S(1)}, u32[]{:S(2)}, u32[]{:S(2)}) collective-permute-start(bf16[992,128]{1,0:T(8,128)(2,1)S(1)} %get-tuple-element.20.own_high), channel_id=1, source_target_pairs={{0,1},{1,2},{2,3},{3,4},{4,5},{5,6},{6,7},{8,9},{9,10},{10,11},{11... | collective-permute-start | bytes 761864 | tf_op jit(solution)/shard_map/ppermute | solution.py:515
  80.1 7.7 %all-to-all-done.2.parts = s16[8,120,128]{2,1,0:T(8,128)(2,1)S(1)} async-done(((s16[8,120,128]{2,1,0:T(8,128)(2,1)}), s16[8,120,128]{2,1,0:T(8,128)(2,1)S(1)}, u32[]{:S(2)}, u32[]{:S(2)}) %all-to-all-start.2) | async-done | bytes 245792 | tf_op jit(solution)/shard_map/all_to_all | solution.py:527
  87.8 0.1 shard_map.103.d_own
  87.9 2.1 %collective-permute-start.6 = (f32[120,128]{1,0:T(8,128)S(1)}, f32[120,128]{1,0:T(8,128)S(1)}, u32[]{:S(2)}, u32[]{:S(2)}) collective-permute-start(f32[120,128]{1,0:T(8,128)S(1)} %shard_map.103.d_own), channel_id=1, source_target_pairs={{1,0},{2,1},{3,2},{4,3},{5,4},{6,5},{7,6},{9,8},{10,9},{11,10},{12... | collective-permute-start | bytes 184328 | tf_op jit(solution)/shard_map/ppermute | solution.py:538
  90.0 3.7 %collective-permute-start.5 = (f32[120,128]{1,0:T(8,128)S(1)}, f32[120,128]{1,0:T(8,128)S(1)}, u32[]{:S(2)}, u32[]{:S(2)}) collective-permute-start(f32[120,128]{1,0:T(8,128)S(1)} %shard_map.103.d_own), channel_id=1, source_target_pairs={{0,1},{1,2},{2,3},{3,4},{4,5},{5,6},{6,7},{8,9},{9,10},{10,11},{11... | collective-permute-start | bytes 184328 | tf_op jit(solution)/shard_map/ppermute | solution.py:537
  93.8 0.0 collective-permute-done.4.z_high
  93.8 0.0 copy-start.9
  93.8 0.0 collective-permute-done.3.z_low
  93.8 0.0 copy-done.2
  93.8 0.0 copy-done.3
  93.8 0.7 copy-done.9
  94.5 0.7 copy-done.10
  95.2 7.3 %shard_map.100.fields_hbm = f32[94,40,384]{2,1,0:T(8,128)} custom-call(f32[3,4,32,256]{3,2,1,0:T(8,128)} %mag.5, bf16[992,128]{1,0:T(8,128)(2,1)} %copy-done.2, bf16[992,128]{1,0:T(8,128)(2,1)} %copy-done.3, bf16[992,128]{1,0:T(8,128)(2,1)} %copy-done.10, bf16[992,128]{1,0:T(8,128)(2,1)} %copy-done.9, f32[16]{0:T(128)} %stiff.1, f32[16]{0:T(128)} %sat.3), custom_call_target="tpu_custom_call" | custom-call | flops 20000000 | bytes 5000000 | tf_op jit(solution)/shard_map/pallas_call | solution.py:528
  102.5 0.0 collective-permute-done.6.d_high
  102.5 0.0 collective-permute-done.5.d_low
  102.5 6.7 %shard_map.104 = (f32[3,4,32,256]{3,2,1,0:T(8,128)}, f32[2,3,16,128]{3,2,1,0:T(8,128)}) custom-call(f32[94,40,384]{2,1,0:T(8,128)} %shard_map.100.fields_hbm, f32[120,128]{1,0:T(8,128)S(1)} %shard_map.103.d_own, f32[120,128]{1,0:T(8,128)S(1)} %collective-permute-done.5.d_low, f32[120,128]{1,0:T(8,128)S(1)} %collective-permute-done.6.d_high), custom_call_target="tpu_custom_call" | custom-call | flops 50000000 | bytes 5000000 | tf_op jit(solution)/shard_map/pallas_call | solution.py:539
  (2 shorter events, 0.0 us)
Async XLA Ops:
  2.7 17.6 %collective-permute-start = (bf16[128,128]{1,0:T(8,128)(2,1)}, bf16[128,128]{1,0:T(8,128)(2,1)S(1)}, u32[]{:S(2)}, u32[]{:S(2)}) collective-permute-start(bf16[128,128]{1,0:T(8,128)(2,1)} %shard_map.95.own), channel_id=1, source_target_pairs={{0,32},{8,40},{16,48},{24,56},{32,0},{40,8},{48,16},{56,24},{1,33}... | collective-permute-start | bytes 98312 | tf_op jit(solution)/shard_map/ppermute | solution.py:454
  17.5 1.0 copy-start
  18.5 0.9 copy-start.1
  19.4 0.8 copy-start.4
  47.8 8.3 %collective-permute-start.2 = (bf16[4,912,128]{2,1,0:T(8,128)(2,1)S(1)}, bf16[4,912,128]{2,1,0:T(8,128)(2,1)S(1)}, u32[]{:S(2)}, u32[]{:S(2)}) collective-permute-start(bf16[4,912,128]{2,1,0:T(8,128)(2,1)S(1)} %all_to_all.16.own), channel_id=1, source_target_pairs={{0,64},{64,0},{128,192},{192,128},{256,320},{320,256},{384,448},{4... | collective-permute-start | bytes 2801672 | tf_op jit(solution)/shard_map/ppermute | solution.py:454
  49.7 0.8 copy-start.5
  50.5 0.7 copy-start.6
  51.1 0.7 copy-start.7
  51.8 0.7 copy-start.8
  61.2 26.7 %all-to-all-start.2 = ((s16[8,120,128]{2,1,0:T(8,128)(2,1)}), s16[8,120,128]{2,1,0:T(8,128)(2,1)S(1)}, u32[]{:S(2)}, u32[]{:S(2)}) async-start(s16[8,120,128]{2,1,0:T(8,128)(2,1)} %shard_map.102), calls=%async_computation.2 | async-start | bytes 491520 | tf_op jit(solution)/shard_map/all_to_all | solution.py:527
  70.9 3.1 %collective-permute-start.1 = (bf16[144,128]{1,0:T(8,128)(2,1)S(1)}, bf16[144,128]{1,0:T(8,128)(2,1)S(1)}, u32[]{:S(2)}, u32[]{:S(2)}) collective-permute-start(bf16[144,128]{1,0:T(8,128)(2,1)S(1)} %get-tuple-element.17), channel_id=1, source_target_pairs={{0,64},{64,0},{128,192},{192,128},{256,320},{320,256},{384,448},{4... | collective-permute-start | bytes 110600 | tf_op jit(solution)/shard_map/ppermute | solution.py:454
  74.2 19.6 %copy-start.2 = (bf16[992,128]{1,0:T(8,128)(2,1)}, bf16[992,128]{1,0:T(8,128)(2,1)S(1)}, u32[]{:S(2)}) copy-start(bf16[992,128]{1,0:T(8,128)(2,1)S(1)} %get-tuple-element.19.own_low) | copy-start | bytes 761860
  74.2 19.6 %copy-start.3 = (bf16[992,128]{1,0:T(8,128)(2,1)}, bf16[992,128]{1,0:T(8,128)(2,1)S(1)}, u32[]{:S(2)}) copy-start(bf16[992,128]{1,0:T(8,128)(2,1)S(1)} %get-tuple-element.20.own_high) | copy-start | bytes 761860
  74.2 19.5 %collective-permute-start.4 = (bf16[992,128]{1,0:T(8,128)(2,1)S(1)}, bf16[992,128]{1,0:T(8,128)(2,1)S(1)}, u32[]{:S(2)}, u32[]{:S(2)}) collective-permute-start(bf16[992,128]{1,0:T(8,128)(2,1)S(1)} %get-tuple-element.19.own_low), channel_id=1, source_target_pairs={{1,0},{2,1},{3,2},{4,3},{5,4},{6,5},{7,6},{9,8},{10,9},{11,10},{12... | collective-permute-start | bytes 761864 | tf_op jit(solution)/shard_map/ppermute | solution.py:516
  76.2 17.6 %collective-permute-start.3 = (bf16[992,128]{1,0:T(8,128)(2,1)S(1)}, bf16[992,128]{1,0:T(8,128)(2,1)S(1)}, u32[]{:S(2)}, u32[]{:S(2)}) collective-permute-start(bf16[992,128]{1,0:T(8,128)(2,1)S(1)} %get-tuple-element.20.own_high), channel_id=1, source_target_pairs={{0,1},{1,2},{2,3},{3,4},{4,5},{5,6},{6,7},{8,9},{9,10},{10,11},{11... | collective-permute-start | bytes 761864 | tf_op jit(solution)/shard_map/ppermute | solution.py:515
  87.9 14.6 %collective-permute-start.6 = (f32[120,128]{1,0:T(8,128)S(1)}, f32[120,128]{1,0:T(8,128)S(1)}, u32[]{:S(2)}, u32[]{:S(2)}) collective-permute-start(f32[120,128]{1,0:T(8,128)S(1)} %shard_map.103.d_own), channel_id=1, source_target_pairs={{1,0},{2,1},{3,2},{4,3},{5,4},{6,5},{7,6},{9,8},{10,9},{11,10},{12... | collective-permute-start | bytes 184328 | tf_op jit(solution)/shard_map/ppermute | solution.py:538
  90.0 12.5 %collective-permute-start.5 = (f32[120,128]{1,0:T(8,128)S(1)}, f32[120,128]{1,0:T(8,128)S(1)}, u32[]{:S(2)}, u32[]{:S(2)}) collective-permute-start(f32[120,128]{1,0:T(8,128)S(1)} %shard_map.103.d_own), channel_id=1, source_target_pairs={{0,1},{1,2},{2,3},{3,4},{4,5},{5,6},{6,7},{8,9},{9,10},{10,11},{11... | collective-permute-start | bytes 184328 | tf_op jit(solution)/shard_map/ppermute | solution.py:537
  93.8 0.7 copy-start.9
  94.5 0.7 copy-start.10

commit v7 on v6

--- a/solution.py
+++ b/solution.py
@@ -346,7 +346,7 @@
                 m0[c, p, 0:32, 0:256] = mag[c, z]
         ids = whole[3].astype(i32)
         aa[p] = jnp.where(inside & ok, lookup(ids, stiff), 0.0)
-        ss[p] = 2.0 / lookup(ids, sat)
+        ss[p] = (2.0 * TIME_STEP) / lookup(ids, sat)
 
     def weight(u, v):
         den = u + v
@@ -378,47 +378,49 @@
 
 
 def substeps_kernel(
-    fields_hbm, d_own, d_low, d_high, state_out, demag_out, fields, m1, m2, fz, field, rows, spread, sems
+    fields_hbm, d_own, d_low, d_high, state_out, demag_out, fields, m1, m2, fz, field, rows, sems
 ):
     m0, hh, wx, wy, wz, ss = parts_of(fields)
-    cuts = (pl.ds(0, 54), pl.ds(54, 40))
+    spans = ((1, 8), (11, 8), (21, 8), (30, 24), (56, 6), (66, 6), (75, 7), (86, 6))
+    cuts = [pl.ds(first, count) for first, count in spans]
     fetches = [pltpu.make_async_copy(fields_hbm.at[c], fields.at[c], sems.at[n]) for n, c in enumerate(cuts)]
     for fetch in fetches:
         fetch.start()
     for q in range(6):
         demag_out[q // 3, q % 3] = d_own[pl.ds(6 + q, 16, stride=6), :]
-    lane24 = iota((24, 128), 1)
-    row24 = iota((24, 128), 0)
+    lane24, row24 = iota((24, 128), 1), iota((24, 128), 0)
+    coarse_x = jnp.where(row24 == 17, 0, row24 + 1)
     sources = [(d_low, 3), (d_own, 0), (d_own, 3), (d_high, 0)]
-    rows[...] = jnp.zeros_like(rows)
     for level in range(4):
         ref, first = sources[level]
         for i in range(3):
-            g = level * 3 + i
-            q = first + i
-            rows[g * 24 : g * 24 + 18, 0:128] = ref[pl.ds(q, 18, stride=6), :]
+            top, q = (level * 3 + i) * 24, first + i
+            rows[top : top + 16, 0:128] = ref[pl.ds(6 + q, 16, stride=6), :]
+            ends = jnp.where(row24[0:8] == 0, ref[102 + q : 103 + q, :], ref[q : q + 1, :])
+            rows[top + 16 : top + 24, 0:128] = ends
             rim = jnp.broadcast_to(ref[108 + q : 109 + q, :], (24, 128))
-            rows[g * 24 : g * 24 + 24, 128:256] = jnp.where(lane24 // 2 == row24, rim, 0.0)
+            rows[top : top + 24, 128:256] = jnp.where(lane24 // 2 == coarse_x, rim, 0.0)
     x = rows[...]
     hi = x.astype(bf16)
     lo = (x - hi.astype(f32)).astype(bf16)
-    a, b = iota((128, 256), 0), iota((128, 256), 1)
+    a, b = iota((256, 256), 0) % 128, iota((256, 256), 1)
     wide = one_hot(b // 2 == a)
-    a, b = iota((128, 128), 0), iota((128, 128), 1)
+    a, b = iota((256, 128), 0) % 128, iota((256, 128), 1)
     ends = one_hot(((a % 2 == 1) & (b < 2)) | ((a % 2 == 0) & (b >= 126)))
-    spread[:, 0:256] = dot(hi[:, :128], wide) + dot(lo[:, :128], wide)
-    spread[:, 256:384] = dot(hi[:, 128:], ends) + dot(lo[:, 128:], ends)
-    r40, c24 = iota((40, 24), 0), iota((40, 24), 1)
-    tall = one_hot(((r40 < 32) & (c24 == 1 + r40 // 2)) | ((r40 >= 32) & (r40 < 34) & (c24 == 17)) | ((r40 >= 38) & (c24 == 0)))
+    block = dot(jnp.concatenate([hi[:, :128], lo[:, :128]], axis=1), wide) * TIME_STEP
+    sides = dot(jnp.concatenate([hi[:, 128:], lo[:, 128:]], axis=1), ends) * TIME_STEP
+    row8 = iota((8, 128), 0)
     for g in range(12):
-        v = spread[g * 24 : (g + 1) * 24, :]
-        hi = v.astype(bf16)
-        lo = (v - hi.astype(f32)).astype(bf16)
-        field[g] = dot(tall, hi) + dot(tall, lo)
+        for q in range(3):
+            v = block[g * 24 : (g + 1) * 24, q * 128 : (q + 1) * 128] if q < 2 else sides[g * 24 : (g + 1) * 24]
+            field[g, q, pl.ds(0, 16, stride=2), :] = v[0:16]
+            field[g, q, pl.ds(1, 16, stride=2), :] = v[0:16]
+            field[g, q, 32:40, :] = jnp.where(row8 < 2, v[16:17], jnp.where(row8 >= 6, v[17:18], 0.0))
     for step in range(3):
         src, dst = ((m0, m1), (m1, m2), (m2, None))[step]
         if step < 2:
-            fetches[step].wait()
+            for fetch in (fetches[:4], fetches[4:])[step]:
+                fetch.wait()
         first, last = step + 1, 8 - step
 
         def plane(p, carry):
@@ -432,10 +434,10 @@
                     total, up = exchange(src, wx, wy, wz, c, p, fz[c])
                     fz[c] = up
                     total = total * ss[p]
-                h.append(total + field[level * 3 + c])
+                h.append(total + jnp.concatenate([field[level * 3 + c, q] for q in range(3)], axis=1))
             t = [m[1] * h[2] - m[2] * h[1], m[2] * h[0] - m[0] * h[2], m[0] * h[1] - m[1] * h[0]]
             u = [m[1] * t[2] - m[2] * t[1], m[2] * t[0] - m[0] * t[2], m[0] * t[1] - m[1] * t[0]]
-            raw = [m[c] - TIME_STEP * (t[c] + DAMPING * u[c]) for c in range(3)]
+            raw = [m[c] - (t[c] + DAMPING * u[c]) for c in range(3)]
             scale = lax.rsqrt(jnp.maximum(raw[0] * raw[0] + raw[1] * raw[1] + raw[2] * raw[2], 1e-30))
             for c in range(3):
                 if step < 2:
@@ -542,8 +544,8 @@
         [HB] + [VM] * 3,
         [pltpu.VMEM((94, 40, 384), f32)]
         + [pltpu.VMEM((3,) + big, f32)] * 2
-        + [pltpu.VMEM((3, 40, 384), f32), pltpu.VMEM((12, 40, 384), f32)]
-        + [pltpu.VMEM((288, 256), f32), pltpu.VMEM((288, 384), f32), pltpu.SemaphoreType.DMA((2,))],
+        + [pltpu.VMEM((3, 40, 384), f32), pltpu.VMEM((12, 3, 40, 128), f32)]
+        + [pltpu.VMEM((288, 256), f32), pltpu.SemaphoreType.DMA((8,))],
         50_000_000,
         5_000_000,
         FULL - 14_000_000,

time: 110 us -> 110 us (level)
  no operation moved by 1% of the time
where the time goes in v7:
time: 110 us; the launch traced here: 109 us
  starting transfers between devices  40 us (36%)
  blocking collectives  27.2 us (25%)
  Pallas kernels  25.4 us (23%)
  waiting for transfers between devices  8.93 us (8%)
  local copies, waits for them, and re-layouts  6.83 us (6%)
    ppermute x3, starting transfers between devices, swap(): return lax.ppermute(value, axis, [(i, i ^ bit) for i in range(8)])  18.6 us
    all_to_all x1, blocking collectives, step(): lax.all_to_all(pay, 'gx', 0, 0, tiled=True, axis_index_groups=groups)  16.3 us
    all_to_all x1, blocking collectives, step(): lax.all_to_all(pay, 'gy', 0, 0, tiled=True, axis_index_groups=groups)  10.9 us
    all_to_all x1, starting transfers between devices, step(): parts = lax.all_to_all(parts, 'gz', 0, 0, tiled=True)  9.68 us
    all_to_all x1, waiting for transfers between devices, step(): parts = lax.all_to_all(parts, 'gz', 0, 0, tiled=True)  7.74 us
    pallas_call x1, Pallas kernels, step(): call(weights_kernel, shape((94, 40, 384), f32), [VM] * 5 + [SM] * 2, [plt...  7.34 us
    unnamed x22, local copies, waits for them, and re-layouts  6.83 us
    pallas_call x1, Pallas kernels, step(): call(substeps_kernel, [shape((3, 4, 32, 256), f32), shape((2, 3, 16, 128)...  6.65 us
  transfers between devices with their start and end apart: 8, of which 2 were waited for; matrix products, arithmetic and copies ran while one was open for 0% of the time, Pallas kernels for 10%

profile of v7, /device:TPU:32, one launch (start us, length us, event | category | flops | bytes accessed | tf_op | source)
XLA Modules:
  0.0 109.2 jit_solution(3454746462820074846)
XLA Ops:
  0.6 2.1 %shard_map.95.own = bf16[128,128]{1,0:T(8,128)(2,1)} custom-call(f32[3,4,32,256]{3,2,1,0:T(8,128)} %mag.5, s32[4,32,256]{2,1,0:T(8,128)} %grains.3, f32[16]{0:T(128)} %sat.3), custom_call_target="tpu_custom_call" | custom-call | flops 20000000 | bytes 600000 | tf_op jit(solution)/shard_map/pallas_call | solution.py:464
  2.7 14.8 %collective-permute-start = (bf16[128,128]{1,0:T(8,128)(2,1)}, bf16[128,128]{1,0:T(8,128)(2,1)S(1)}, u32[]{:S(2)}, u32[]{:S(2)}) collective-permute-start(bf16[128,128]{1,0:T(8,128)(2,1)} %shard_map.95.own), channel_id=1, source_target_pairs={{0,32},{8,40},{16,48},{24,56},{32,0},{40,8},{48,16},{56,24},{1,33}... | collective-permute-start | bytes 98312 | tf_op jit(solution)/shard_map/ppermute | solution.py:456
  17.5 0.0 copy-start
  17.5 1.0 copy-done
  18.5 0.0 copy-start.1
  18.5 0.9 copy-done.1
  19.4 0.0 copy-start.4
  19.4 0.8 copy-done.4
  20.2 0.1 shard_map.96
  20.2 0.0 collective-permute-done.other
  20.3 10.9 %all_to_all.15.gathered = bf16[4,256,128]{2,1,0:T(8,128)(2,1)S(1)} all-to-all(bf16[4,256,128]{2,1,0:T(8,128)(2,1)S(1)} %shard_map.97), channel_id=1, replica_groups={{0,8,16,24},{32,40,48,56},{1,9,17,25},{33,41,49,57},{2,10,18,26},{34,42..., dimensions={0} | all-to-all | bytes 524288 | tf_op jit(solution)/shard_map/all_to_all | solution.py:494
  31.2 0.3 shard_map.98
  31.5 16.3 %all_to_all.16.own = bf16[4,912,128]{2,1,0:T(8,128)(2,1)S(1)} all-to-all(bf16[4,912,128]{2,1,0:T(8,128)(2,1)S(1)} %get-tuple-element.18), channel_id=1, replica_groups={{0,128,256,384},{64,192,320,448},{1,129,257,385},{65,193,321,449},{2,13..., dimensions={0} | all-to-all | bytes 1867776 | tf_op jit(solution)/shard_map/all_to_all | solution.py:505
  47.8 1.9 %collective-permute-start.2 = (bf16[4,912,128]{2,1,0:T(8,128)(2,1)S(1)}, bf16[4,912,128]{2,1,0:T(8,128)(2,1)S(1)}, u32[]{:S(2)}, u32[]{:S(2)}) collective-permute-start(bf16[4,912,128]{2,1,0:T(8,128)(2,1)S(1)} %all_to_all.16.own), channel_id=1, source_target_pairs={{0,64},{64,0},{128,192},{192,128},{256,320},{320,256},{384,448},{4... | collective-permute-start | bytes 2801672 | tf_op jit(solution)/shard_map/ppermute | solution.py:456
  49.7 0.0 copy-start.5
  49.7 0.7 copy-done.5
  50.5 0.0 copy-start.6
  50.5 0.7 copy-done.6
  51.1 0.0 copy-start.7
  51.2 0.7 copy-done.7
  51.8 0.0 copy-start.8
  51.8 0.7 copy-done.8
  52.5 3.5 %shard_map.101 = (bf16[8,128,2176]{2,1,0:T(8,128)(2,1)}, f32[192,128]{1,0:T(8,128)S(1)}, bf16[64,192]{1,0:T(8,128)(2,1)S(1)}) custom-call(bf16[8,256]{1,0:T(8,128)(2,1)S(1)} %copy-done.7, bf16[8,2048]{1,0:T(8,128)(2,1)S(1)} %copy-done.5, bf16[8,32]{1,0:T(8,128)(2,1)S(1)} %copy-done.8, f32[3,3,8]{2,1,0:T(4,128)S(1)} %bitcast.1), custom_call_target="tpu_custom_call" | custom-call | flops 20000000 | bytes 5000000 | tf_op jit(solution)/shard_map/pallas_call | solution.py:482
  56.0 0.0 collective-permute-done.2.rc
  56.1 5.1 %shard_map.102 = s16[8,120,128]{2,1,0:T(8,128)(2,1)} custom-call(bf16[4,912,128]{2,1,0:T(8,128)(2,1)S(1)} %all_to_all.16.own, bf16[4,912,128]{2,1,0:T(8,128)(2,1)S(1)} %collective-permute-done.2.rc, f32[192,128]{1,0:T(8,128)S(1)} %get-tuple-element.21.kx, bf16[8,128,2176]{2,1,0:T(8,128)(2,1)} %get-tuple-element.22.strip_hbm, ...), custom_call_target="tpu_custom_call" | custom-call | flops 2000000000 | bytes 10000000 | tf_op jit(solution)/shard_map/pallas_call | solution.py:519
  61.2 9.7 %all-to-all-start.2 = ((s16[8,120,128]{2,1,0:T(8,128)(2,1)}), s16[8,120,128]{2,1,0:T(8,128)(2,1)S(1)}, u32[]{:S(2)}, u32[]{:S(2)}) async-start(s16[8,120,128]{2,1,0:T(8,128)(2,1)} %shard_map.102), calls=%async_computation.2 | async-start | bytes 491520 | tf_op jit(solution)/shard_map/all_to_all | solution.py:529
  70.9 1.9 %collective-permute-start.1 = (bf16[144,128]{1,0:T(8,128)(2,1)S(1)}, bf16[144,128]{1,0:T(8,128)(2,1)S(1)}, u32[]{:S(2)}, u32[]{:S(2)}) collective-permute-start(bf16[144,128]{1,0:T(8,128)(2,1)S(1)} %get-tuple-element.17), channel_id=1, source_target_pairs={{0,64},{64,0},{128,192},{192,128},{256,320},{320,256},{384,448},{4... | collective-permute-start | bytes 110600 | tf_op jit(solution)/shard_map/ppermute | solution.py:456
  72.8 1.2 %collective-permute-done.1.near = bf16[144,128]{1,0:T(8,128)(2,1)S(1)} collective-permute-done((bf16[144,128]{1,0:T(8,128)(2,1)S(1)}, bf16[144,128]{1,0:T(8,128)(2,1)S(1)}, u32[]{:S(2)}, u32[]{:S(2)}) %collective-permute-start.1) | collective-permute-done | bytes 36896 | tf_op jit(solution)/shard_map/ppermute | solution.py:456
  73.9 0.3 shard_map.99
  74.2 0.0 copy-start.2
  74.2 0.0 copy-start.3
  74.2 1.9 %collective-permute-start.4 = (bf16[992,128]{1,0:T(8,128)(2,1)S(1)}, bf16[992,128]{1,0:T(8,128)(2,1)S(1)}, u32[]{:S(2)}, u32[]{:S(2)}) collective-permute-start(bf16[992,128]{1,0:T(8,128)(2,1)S(1)} %get-tuple-element.19.own_low), channel_id=1, source_target_pairs={{1,0},{2,1},{3,2},{4,3},{5,4},{6,5},{7,6},{9,8},{10,9},{11,10},{12... | collective-permute-start | bytes 761864 | tf_op jit(solution)/shard_map/ppermute | solution.py:518
  76.2 3.9 %collective-permute-start.3 = (bf16[992,128]{1,0:T(8,128)(2,1)S(1)}, bf16[992,128]{1,0:T(8,128)(2,1)S(1)}, u32[]{:S(2)}, u32[]{:S(2)}) collective-permute-start(bf16[992,128]{1,0:T(8,128)(2,1)S(1)} %get-tuple-element.20.own_high), channel_id=1, source_target_pairs={{0,1},{1,2},{2,3},{3,4},{4,5},{5,6},{6,7},{8,9},{9,10},{10,11},{11... | collective-permute-start | bytes 761864 | tf_op jit(solution)/shard_map/ppermute | solution.py:517
  80.1 7.7 %all-to-all-done.2.parts = s16[8,120,128]{2,1,0:T(8,128)(2,1)S(1)} async-done(((s16[8,120,128]{2,1,0:T(8,128)(2,1)}), s16[8,120,128]{2,1,0:T(8,128)(2,1)S(1)}, u32[]{:S(2)}, u32[]{:S(2)}) %all-to-all-start.2) | async-done | bytes 245792 | tf_op jit(solution)/shard_map/all_to_all | solution.py:529
  87.8 0.1 shard_map.103.d_own
  87.9 2.1 %collective-permute-start.6 = (f32[120,128]{1,0:T(8,128)S(1)}, f32[120,128]{1,0:T(8,128)S(1)}, u32[]{:S(2)}, u32[]{:S(2)}) collective-permute-start(f32[120,128]{1,0:T(8,128)S(1)} %shard_map.103.d_own), channel_id=1, source_target_pairs={{1,0},{2,1},{3,2},{4,3},{5,4},{6,5},{7,6},{9,8},{10,9},{11,10},{12... | collective-permute-start | bytes 184328 | tf_op jit(solution)/shard_map/ppermute | solution.py:540
  90.0 3.7 %collective-permute-start.5 = (f32[120,128]{1,0:T(8,128)S(1)}, f32[120,128]{1,0:T(8,128)S(1)}, u32[]{:S(2)}, u32[]{:S(2)}) collective-permute-start(f32[120,128]{1,0:T(8,128)S(1)} %shard_map.103.d_own), channel_id=1, source_target_pairs={{0,1},{1,2},{2,3},{3,4},{4,5},{5,6},{6,7},{8,9},{9,10},{10,11},{11... | collective-permute-start | bytes 184328 | tf_op jit(solution)/shard_map/ppermute | solution.py:539
  93.8 0.0 collective-permute-done.4.z_high
  93.8 0.0 copy-start.9
  93.8 0.0 collective-permute-done.3.z_low
  93.8 0.0 copy-done.2
  93.8 0.0 copy-done.3
  93.8 0.7 copy-done.9
  94.5 0.7 copy-done.10
  95.2 7.3 %shard_map.100.fields_hbm = f32[94,40,384]{2,1,0:T(8,128)} custom-call(f32[3,4,32,256]{3,2,1,0:T(8,128)} %mag.5, bf16[992,128]{1,0:T(8,128)(2,1)} %copy-done.2, bf16[992,128]{1,0:T(8,128)(2,1)} %copy-done.3, bf16[992,128]{1,0:T(8,128)(2,1)} %copy-done.10, bf16[992,128]{1,0:T(8,128)(2,1)} %copy-done.9, f32[16]{0:T(128)} %stiff.1, f32[16]{0:T(128)} %sat.3), custom_call_target="tpu_custom_call" | custom-call | flops 20000000 | bytes 5000000 | tf_op jit(solution)/shard_map/pallas_call | solution.py:530
  102.5 0.0 collective-permute-done.6.d_high
  102.5 0.0 collective-permute-done.5.d_low
  102.5 6.6 %shard_map.104 = (f32[3,4,32,256]{3,2,1,0:T(8,128)}, f32[2,3,16,128]{3,2,1,0:T(8,128)}) custom-call(f32[94,40,384]{2,1,0:T(8,128)} %shard_map.100.fields_hbm, f32[120,128]{1,0:T(8,128)S(1)} %shard_map.103.d_own, f32[120,128]{1,0:T(8,128)S(1)} %collective-permute-done.5.d_low, f32[120,128]{1,0:T(8,128)S(1)} %collective-permute-done.6.d_high), custom_call_target="tpu_custom_call" | custom-call | flops 50000000 | bytes 5000000 | tf_op jit(solution)/shard_map/pallas_call | solution.py:541
  (2 shorter events, 0.0 us)
Async XLA Ops:
  2.7 17.6 %collective-permute-start = (bf16[128,128]{1,0:T(8,128)(2,1)}, bf16[128,128]{1,0:T(8,128)(2,1)S(1)}, u32[]{:S(2)}, u32[]{:S(2)}) collective-permute-start(bf16[128,128]{1,0:T(8,128)(2,1)} %shard_map.95.own), channel_id=1, source_target_pairs={{0,32},{8,40},{16,48},{24,56},{32,0},{40,8},{48,16},{56,24},{1,33}... | collective-permute-start | bytes 98312 | tf_op jit(solution)/shard_map/ppermute | solution.py:456
  17.5 1.0 copy-start
  18.5 0.9 copy-start.1
  19.4 0.8 copy-start.4
  47.8 8.3 %collective-permute-start.2 = (bf16[4,912,128]{2,1,0:T(8,128)(2,1)S(1)}, bf16[4,912,128]{2,1,0:T(8,128)(2,1)S(1)}, u32[]{:S(2)}, u32[]{:S(2)}) collective-permute-start(bf16[4,912,128]{2,1,0:T(8,128)(2,1)S(1)} %all_to_all.16.own), channel_id=1, source_target_pairs={{0,64},{64,0},{128,192},{192,128},{256,320},{320,256},{384,448},{4... | collective-permute-start | bytes 2801672 | tf_op jit(solution)/shard_map/ppermute | solution.py:456
  49.7 0.8 copy-start.5
  50.5 0.7 copy-start.6
  51.1 0.7 copy-start.7
  51.8 0.7 copy-start.8
  61.2 26.7 %all-to-all-start.2 = ((s16[8,120,128]{2,1,0:T(8,128)(2,1)}), s16[8,120,128]{2,1,0:T(8,128)(2,1)S(1)}, u32[]{:S(2)}, u32[]{:S(2)}) async-start(s16[8,120,128]{2,1,0:T(8,128)(2,1)} %shard_map.102), calls=%async_computation.2 | async-start | bytes 491520 | tf_op jit(solution)/shard_map/all_to_all | solution.py:529
  70.9 3.1 %collective-permute-start.1 = (bf16[144,128]{1,0:T(8,128)(2,1)S(1)}, bf16[144,128]{1,0:T(8,128)(2,1)S(1)}, u32[]{:S(2)}, u32[]{:S(2)}) collective-permute-start(bf16[144,128]{1,0:T(8,128)(2,1)S(1)} %get-tuple-element.17), channel_id=1, source_target_pairs={{0,64},{64,0},{128,192},{192,128},{256,320},{320,256},{384,448},{4... | collective-permute-start | bytes 110600 | tf_op jit(solution)/shard_map/ppermute | solution.py:456
  74.2 19.6 %copy-start.2 = (bf16[992,128]{1,0:T(8,128)(2,1)}, bf16[992,128]{1,0:T(8,128)(2,1)S(1)}, u32[]{:S(2)}) copy-start(bf16[992,128]{1,0:T(8,128)(2,1)S(1)} %get-tuple-element.19.own_low) | copy-start | bytes 761860
  74.2 19.6 %copy-start.3 = (bf16[992,128]{1,0:T(8,128)(2,1)}, bf16[992,128]{1,0:T(8,128)(2,1)S(1)}, u32[]{:S(2)}) copy-start(bf16[992,128]{1,0:T(8,128)(2,1)S(1)} %get-tuple-element.20.own_high) | copy-start | bytes 761860
  74.2 19.5 %collective-permute-start.4 = (bf16[992,128]{1,0:T(8,128)(2,1)S(1)}, bf16[992,128]{1,0:T(8,128)(2,1)S(1)}, u32[]{:S(2)}, u32[]{:S(2)}) collective-permute-start(bf16[992,128]{1,0:T(8,128)(2,1)S(1)} %get-tuple-element.19.own_low), channel_id=1, source_target_pairs={{1,0},{2,1},{3,2},{4,3},{5,4},{6,5},{7,6},{9,8},{10,9},{11,10},{12... | collective-permute-start | bytes 761864 | tf_op jit(solution)/shard_map/ppermute | solution.py:518
  76.2 17.6 %collective-permute-start.3 = (bf16[992,128]{1,0:T(8,128)(2,1)S(1)}, bf16[992,128]{1,0:T(8,128)(2,1)S(1)}, u32[]{:S(2)}, u32[]{:S(2)}) collective-permute-start(bf16[992,128]{1,0:T(8,128)(2,1)S(1)} %get-tuple-element.20.own_high), channel_id=1, source_target_pairs={{0,1},{1,2},{2,3},{3,4},{4,5},{5,6},{6,7},{8,9},{9,10},{10,11},{11... | collective-permute-start | bytes 761864 | tf_op jit(solution)/shard_map/ppermute | solution.py:517
  87.9 14.6 %collective-permute-start.6 = (f32[120,128]{1,0:T(8,128)S(1)}, f32[120,128]{1,0:T(8,128)S(1)}, u32[]{:S(2)}, u32[]{:S(2)}) collective-permute-start(f32[120,128]{1,0:T(8,128)S(1)} %shard_map.103.d_own), channel_id=1, source_target_pairs={{1,0},{2,1},{3,2},{4,3},{5,4},{6,5},{7,6},{9,8},{10,9},{11,10},{12... | collective-permute-start | bytes 184328 | tf_op jit(solution)/shard_map/ppermute | solution.py:540
  90.0 12.5 %collective-permute-start.5 = (f32[120,128]{1,0:T(8,128)S(1)}, f32[120,128]{1,0:T(8,128)S(1)}, u32[]{:S(2)}, u32[]{:S(2)}) collective-permute-start(f32[120,128]{1,0:T(8,128)S(1)} %shard_map.103.d_own), channel_id=1, source_target_pairs={{0,1},{1,2},{2,3},{3,4},{4,5},{5,6},{6,7},{8,9},{9,10},{10,11},{11... | collective-permute-start | bytes 184328 | tf_op jit(solution)/shard_map/ppermute | solution.py:539
  93.8 0.7 copy-start.9
  94.5 0.7 copy-start.10

commit v8 on v7

--- a/solution.py
+++ b/solution.py
@@ -14,6 +14,7 @@
 DAMPING = 0.3
 SCALE = 32000.0
 FULL = 67_043_328
+FAR = [(pl.ds(a, n), pl.ds(b, n)) for a, b, n in ((56, 0, 6), (66, 6, 6), (75, 12, 7), (86, 19, 6))]
 
 
 def iota(shape, dim):
@@ -321,8 +322,8 @@
     out[114:120] = jnp.zeros((6, 128), f32)
 
 
-def weights_kernel(mag, own_low, own_high, z_low, z_high, stiff, sat, fields, aa):
-    m0, hh, wx, wy, wz, ss = parts_of(fields)
+def weights_kernel(mag, own_low, own_high, z_low, z_high, stiff, sat, near, far_hbm, fields, aa, sems):
+    m0, _, wx, wy, wz, ss = parts_of(fields)
     gx, gy, gz = (lax.axis_index(n) for n in ("gx", "gy", "gz"))
     row, col = iota((40, 384), 0), iota((40, 384), 1)
     inside = ((row < 32) | ((row < 36) & (gx < 7)) | ((row >= 36) & (gx > 0))) & (
@@ -360,11 +361,17 @@
         if p < 9:
             wz[p] = weight(here, aa[p + 1])
 
+    copies = [pltpu.make_async_copy(fields.at[a], far_hbm.at[b], sems.at[n]) for n, (a, b) in enumerate(FAR)]
+    for copy in copies:
+        copy.start()
     fz = [wz[0] * (m0[c, 1] - m0[c, 0]) for c in range(3)]
     for p in range(1, 9):
         for c in range(3):
             total, fz[c] = exchange(m0, wx, wy, wz, c, p, fz[c])
-            hh[c, p - 1] = total * ss[p]
+            near[24 + c * 8 + p - 1] = total * ss[p]
+            near[c * 8 + p - 1] = m0[c, p]
+    for copy in copies:
+        copy.wait()
 
 
 def exchange(src, wx, wy, wz, c, p, below):
@@ -378,14 +385,12 @@
 
 
 def substeps_kernel(
-    fields_hbm, d_own, d_low, d_high, state_out, demag_out, fields, m1, m2, fz, field, rows, sems
+    near, far_hbm, d_own, d_low, d_high, state_out, demag_out, far, m1, m2, fz, field, rows, sem
 ):
-    m0, hh, wx, wy, wz, ss = parts_of(fields)
-    spans = ((1, 8), (11, 8), (21, 8), (30, 24), (56, 6), (66, 6), (75, 7), (86, 6))
-    cuts = [pl.ds(first, count) for first, count in spans]
-    fetches = [pltpu.make_async_copy(fields_hbm.at[c], fields.at[c], sems.at[n]) for n, c in enumerate(cuts)]
-    for fetch in fetches:
-        fetch.start()
+    m0, hh = Planes(near, -1, 8), Planes(near, 24, 8)
+    wx, wy, wz, ss = (Planes(far, base) for base in (-2, 4, 11, 17))
+    fetch = pltpu.make_async_copy(far_hbm, far, sem)
+    fetch.start()
     for q in range(6):
         demag_out[q // 3, q % 3] = d_own[pl.ds(6 + q, 16, stride=6), :]
     lane24, row24 = iota((24, 128), 1), iota((24, 128), 0)
@@ -418,9 +423,8 @@
             field[g, q, 32:40, :] = jnp.where(row8 < 2, v[16:17], jnp.where(row8 >= 6, v[17:18], 0.0))
     for step in range(3):
         src, dst = ((m0, m1), (m1, m2), (m2, None))[step]
-        if step < 2:
-            for fetch in (fetches[:4], fetches[4:])[step]:
-                fetch.wait()
+        if step == 1:
+            fetch.wait()
         first, last = step + 1, 8 - step
 
         def plane(p, carry):
@@ -527,13 +531,15 @@
         FULL - (16 << 20),
     )(gathered, rc, kx, strip, wz)
     parts = lax.all_to_all(parts, "gz", 0, 0, tiled=True)
-    (fields,) = call(
+    near_fields, far_fields = call(
         weights_kernel,
-        shape((94, 40, 384), f32),
+        [shape((48, 40, 384), f32), shape((25, 40, 384), f32)],
         [VM] * 5 + [SM] * 2,
-        [pltpu.VMEM(big, f32)],
+        [pltpu.VMEM((94, 40, 384), f32), pltpu.VMEM(big, f32), pltpu.SemaphoreType.DMA((4,))],
         20_000_000,
         5_000_000,
+        FULL - 15_000_000,
+        [VM, HB],
     )(magnet, own_low, own_high, z_low, z_high, stiffness_table, saturation_table)
     (d_own,) = call(sum_kernel, shape((120, 128), f32), [VM], (), 100_000, 300_000, 8 << 20)(parts)
     d_low = lax.ppermute(d_own, "gz", up)
@@ -541,15 +547,15 @@
     state, demag = call(
         substeps_kernel,
         [shape((3, 4, 32, 256), f32), shape((2, 3, 16, 128), f32)],
-        [HB] + [VM] * 3,
-        [pltpu.VMEM((94, 40, 384), f32)]
+        [VM, HB] + [VM] * 3,
+        [pltpu.VMEM((25, 40, 384), f32)]
         + [pltpu.VMEM((3,) + big, f32)] * 2
         + [pltpu.VMEM((3, 40, 384), f32), pltpu.VMEM((12, 3, 40, 128), f32)]
-        + [pltpu.VMEM((288, 256), f32), pltpu.SemaphoreType.DMA((8,))],
+        + [pltpu.VMEM((288, 256), f32), pltpu.SemaphoreType.DMA],
         50_000_000,
         5_000_000,
-        FULL - 14_000_000,
-    )(fields, d_own, d_low, d_high)
+        FULL - 15_000_000,
+    )(near_fields, far_fields, d_own, d_low, d_high)
     return (state, demag)
 
 

time: 110 us -> 105 us (0.955)
  local copies, waits for them, and re-layouts: 6.83 us -> 2.69 us
    unnamed x22 -> x20, local copies, waits for them, and re-layouts: 6.83 us -> 2.69 us
where the time goes in v8:
time: 105 us
  starting transfers between devices  40 us (38%)
  blocking collectives  27.2 us (26%)
  Pallas kernels  25.1 us (24%)
  waiting for transfers between devices  8.94 us (9%)
  local copies, waits for them, and re-layouts  2.69 us (3%)
    ppermute x3, starting transfers between devices, swap(): return lax.ppermute(value, axis, [(i, i ^ bit) for i in range(8)])  18.6 us
    all_to_all x1, blocking collectives, step(): lax.all_to_all(pay, 'gx', 0, 0, tiled=True, axis_index_groups=groups)  16.2 us
    all_to_all x1, blocking collectives, step(): lax.all_to_all(pay, 'gy', 0, 0, tiled=True, axis_index_groups=groups)  10.9 us
    all_to_all x1, starting transfers between devices, step(): parts = lax.all_to_all(parts, 'gz', 0, 0, tiled=True)  9.69 us
    all_to_all x1, waiting for transfers between devices, step(): parts = lax.all_to_all(parts, 'gz', 0, 0, tiled=True)  7.75 us
    pallas_call x1, Pallas kernels, step(): call(substeps_kernel, [shape((3, 4, 32, 256), f32), shape((2, 3, 16, 128)...  7.1 us
    pallas_call x1, Pallas kernels, step(): call(weights_kernel, [shape((48, 40, 384), f32), shape((25, 40, 384), f32...  6.51 us
    pallas_call x1, Pallas kernels, step(): call(stages_kernel, shape((8, 120, 128), jnp.int16), [VM, VM, VM, HB, VM]...  5.12 us
  transfers between devices with their start and end apart: 8, of which 2 were waited for; matrix products, arithmetic and copies ran while one was open for 0% of the time, Pallas kernels for 10%

profile of v8, /device:TPU:32, one launch (start us, length us, event | category | flops | bytes accessed | tf_op | source)
XLA Modules:
  0.0 104.8 jit_solution(571963657697769204)
XLA Ops:
  0.6 0.0 copy-start.7
  0.6 0.0 copy-start.9
  0.7 0.0 copy-start.6
  0.7 0.0 copy-start.8
  0.7 2.1 %shard_map.95.own = bf16[128,128]{1,0:T(8,128)(2,1)} custom-call(f32[3,4,32,256]{3,2,1,0:T(8,128)} %mag.5, s32[4,32,256]{2,1,0:T(8,128)} %grains.3, f32[16]{0:T(128)} %sat.3), custom_call_target="tpu_custom_call" | custom-call | flops 20000000 | bytes 600000 | tf_op jit(solution)/shard_map/pallas_call | solution.py:468
  2.8 14.8 %collective-permute-start = (bf16[128,128]{1,0:T(8,128)(2,1)}, bf16[128,128]{1,0:T(8,128)(2,1)S(1)}, u32[]{:S(2)}, u32[]{:S(2)}) collective-permute-start(bf16[128,128]{1,0:T(8,128)(2,1)} %shard_map.95.own), channel_id=1, source_target_pairs={{0,32},{8,40},{16,48},{24,56},{32,0},{40,8},{48,16},{56,24},{1,33}... | collective-permute-start | bytes 98312 | tf_op jit(solution)/shard_map/ppermute | solution.py:460
  17.6 0.0 copy-start
  17.6 1.0 copy-done
  18.6 0.0 copy-start.2
  18.6 0.9 copy-done.2
  19.5 0.0 copy-start.3
  19.5 0.8 copy-done.3
  20.2 0.1 shard_map.96
  20.3 0.0 collective-permute-done.other
  20.3 10.9 %all_to_all.15.gathered = bf16[4,256,128]{2,1,0:T(8,128)(2,1)S(1)} all-to-all(bf16[4,256,128]{2,1,0:T(8,128)(2,1)S(1)} %shard_map.97), channel_id=1, replica_groups={{0,8,16,24},{32,40,48,56},{1,9,17,25},{33,41,49,57},{2,10,18,26},{34,42..., dimensions={0} | all-to-all | bytes 524288 | tf_op jit(solution)/shard_map/all_to_all | solution.py:498
  31.3 0.3 shard_map.98
  31.6 16.2 %all_to_all.16.own = bf16[4,912,128]{2,1,0:T(8,128)(2,1)S(1)} all-to-all(bf16[4,912,128]{2,1,0:T(8,128)(2,1)S(1)} %get-tuple-element.20), channel_id=1, replica_groups={{0,128,256,384},{64,192,320,448},{1,129,257,385},{65,193,321,449},{2,13..., dimensions={0} | all-to-all | bytes 1867776 | tf_op jit(solution)/shard_map/all_to_all | solution.py:509
  47.8 1.9 %collective-permute-start.2 = (bf16[4,912,128]{2,1,0:T(8,128)(2,1)S(1)}, bf16[4,912,128]{2,1,0:T(8,128)(2,1)S(1)}, u32[]{:S(2)}, u32[]{:S(2)}) collective-permute-start(bf16[4,912,128]{2,1,0:T(8,128)(2,1)S(1)} %all_to_all.16.own), channel_id=1, source_target_pairs={{0,64},{64,0},{128,192},{192,128},{256,320},{320,256},{384,448},{4... | collective-permute-start | bytes 2801672 | tf_op jit(solution)/shard_map/ppermute | solution.py:460
  49.8 0.0 copy-done.7
  49.8 0.0 copy-done.9
  49.8 0.0 copy-done.6
  49.8 0.0 copy-done.8
  49.8 3.5 %shard_map.101 = (bf16[8,128,2176]{2,1,0:T(8,128)(2,1)}, f32[192,128]{1,0:T(8,128)S(1)}, bf16[64,192]{1,0:T(8,128)(2,1)S(1)}) custom-call(bf16[8,256]{1,0:T(8,128)(2,1)S(1)} %copy-done.8, bf16[8,2048]{1,0:T(8,128)(2,1)S(1)} %copy-done.6, bf16[8,32]{1,0:T(8,128)(2,1)S(1)} %copy-done.9, f32[3,3,8]{2,1,0:T(4,128)S(1)} %bitcast.1), custom_call_target="tpu_custom_call" | custom-call | flops 20000000 | bytes 5000000 | tf_op jit(solution)/shard_map/pallas_call | solution.py:486
  53.3 0.0 collective-permute-done.2.rc
  53.3 0.0 copy-start.1
  53.3 0.0 copy-start.4
  53.4 0.0 copy-start.5
  53.4 5.1 %shard_map.102 = s16[8,120,128]{2,1,0:T(8,128)(2,1)} custom-call(bf16[4,912,128]{2,1,0:T(8,128)(2,1)S(1)} %all_to_all.16.own, bf16[4,912,128]{2,1,0:T(8,128)(2,1)S(1)} %collective-permute-done.2.rc, f32[192,128]{1,0:T(8,128)S(1)} %get-tuple-element.25.kx, bf16[8,128,2176]{2,1,0:T(8,128)(2,1)} %get-tuple-element.26.strip_hbm, ...), custom_call_target="tpu_custom_call" | custom-call | flops 2000000000 | bytes 10000000 | tf_op jit(solution)/shard_map/pallas_call | solution.py:523
  58.5 9.7 %all-to-all-start.2 = ((s16[8,120,128]{2,1,0:T(8,128)(2,1)}), s16[8,120,128]{2,1,0:T(8,128)(2,1)S(1)}, u32[]{:S(2)}, u32[]{:S(2)}) async-start(s16[8,120,128]{2,1,0:T(8,128)(2,1)} %shard_map.102), calls=%async_computation.2 | async-start | bytes 491520 | tf_op jit(solution)/shard_map/all_to_all | solution.py:533
  68.2 1.9 %collective-permute-start.1 = (bf16[144,128]{1,0:T(8,128)(2,1)S(1)}, bf16[144,128]{1,0:T(8,128)(2,1)S(1)}, u32[]{:S(2)}, u32[]{:S(2)}) collective-permute-start(bf16[144,128]{1,0:T(8,128)(2,1)S(1)} %get-tuple-element.19), channel_id=1, source_target_pairs={{0,64},{64,0},{128,192},{192,128},{256,320},{320,256},{384,448},{4... | collective-permute-start | bytes 110600 | tf_op jit(solution)/shard_map/ppermute | solution.py:460
  70.1 1.2 %collective-permute-done.1.near = bf16[144,128]{1,0:T(8,128)(2,1)S(1)} collective-permute-done((bf16[144,128]{1,0:T(8,128)(2,1)S(1)}, bf16[144,128]{1,0:T(8,128)(2,1)S(1)}, u32[]{:S(2)}, u32[]{:S(2)}) %collective-permute-start.1) | collective-permute-done | bytes 36896 | tf_op jit(solution)/shard_map/ppermute | solution.py:460
  71.3 0.3 shard_map.99
  71.6 1.9 %collective-permute-start.4 = (bf16[992,128]{1,0:T(8,128)(2,1)S(1)}, bf16[992,128]{1,0:T(8,128)(2,1)S(1)}, u32[]{:S(2)}, u32[]{:S(2)}) collective-permute-start(bf16[992,128]{1,0:T(8,128)(2,1)S(1)} %get-tuple-element.21.own_low), channel_id=1, source_target_pairs={{1,0},{2,1},{3,2},{4,3},{5,4},{6,5},{7,6},{9,8},{10,9},{11,10},{12... | collective-permute-start | bytes 761864 | tf_op jit(solution)/shard_map/ppermute | solution.py:522
  73.5 3.9 %collective-permute-start.3 = (bf16[992,128]{1,0:T(8,128)(2,1)S(1)}, bf16[992,128]{1,0:T(8,128)(2,1)S(1)}, u32[]{:S(2)}, u32[]{:S(2)}) collective-permute-start(bf16[992,128]{1,0:T(8,128)(2,1)S(1)} %get-tuple-element.22.own_high), channel_id=1, source_target_pairs={{0,1},{1,2},{2,3},{3,4},{4,5},{5,6},{6,7},{8,9},{9,10},{10,11},{11... | collective-permute-start | bytes 761864 | tf_op jit(solution)/shard_map/ppermute | solution.py:521
  77.4 7.8 %all-to-all-done.2.parts = s16[8,120,128]{2,1,0:T(8,128)(2,1)S(1)} async-done(((s16[8,120,128]{2,1,0:T(8,128)(2,1)}), s16[8,120,128]{2,1,0:T(8,128)(2,1)S(1)}, u32[]{:S(2)}, u32[]{:S(2)}) %all-to-all-start.2) | async-done | bytes 245792 | tf_op jit(solution)/shard_map/all_to_all | solution.py:533
  85.2 0.1 shard_map.103.d_own
  85.3 2.1 %collective-permute-start.6 = (f32[120,128]{1,0:T(8,128)S(1)}, f32[120,128]{1,0:T(8,128)S(1)}, u32[]{:S(2)}, u32[]{:S(2)}) collective-permute-start(f32[120,128]{1,0:T(8,128)S(1)} %shard_map.103.d_own), channel_id=1, source_target_pairs={{1,0},{2,1},{3,2},{4,3},{5,4},{6,5},{7,6},{9,8},{10,9},{11,10},{12... | collective-permute-start | bytes 184328 | tf_op jit(solution)/shard_map/ppermute | solution.py:546
  87.4 3.7 %collective-permute-start.5 = (f32[120,128]{1,0:T(8,128)S(1)}, f32[120,128]{1,0:T(8,128)S(1)}, u32[]{:S(2)}, u32[]{:S(2)}) collective-permute-start(f32[120,128]{1,0:T(8,128)S(1)} %shard_map.103.d_own), channel_id=1, source_target_pairs={{0,1},{1,2},{2,3},{3,4},{4,5},{5,6},{6,7},{8,9},{9,10},{10,11},{11... | collective-permute-start | bytes 184328 | tf_op jit(solution)/shard_map/ppermute | solution.py:545
  91.1 0.0 collective-permute-done.4.z_high
  91.1 0.0 collective-permute-done.3.z_low
  91.1 0.0 copy-done.1
  91.1 0.0 copy-done.4
  91.2 0.0 copy-done.5
  91.2 6.5 %shard_map.100 = (f32[48,40,384]{2,1,0:T(8,128)}, f32[25,40,384]{2,1,0:T(8,128)S(1)}) custom-call(f32[3,4,32,256]{3,2,1,0:T(8,128)S(1)} %copy-done.1, bf16[992,128]{1,0:T(8,128)(2,1)S(1)} %get-tuple-element.21.own_low, bf16[992,128]{1,0:T(8,128)(2,1)S(1)} %get-tuple-element.22.own_high, bf16[992,128]{1,0:T(8,128)(2,1)S(1)} %collective-permute-done.3.z_low, ...), custom_call_target="tpu_custom_call" | custom-call | flops 20000000 | bytes 5000000 | tf_op jit(solution)/shard_map/pallas_call | solution.py:534
  97.7 0.0 collective-permute-done.6.d_high
  97.7 0.0 collective-permute-done.5.d_low
  97.7 7.1 %shard_map.104 = (f32[3,4,32,256]{3,2,1,0:T(8,128)}, f32[2,3,16,128]{3,2,1,0:T(8,128)}) custom-call(f32[48,40,384]{2,1,0:T(8,128)} %get-tuple-element.23.near, f32[25,40,384]{2,1,0:T(8,128)S(1)} %get-tuple-element.24.far_hbm, f32[120,128]{1,0:T(8,128)S(1)} %shard_map.103.d_own, f32[120,128]{1,0:T(8,128)S(1)} %collective-permute-done.5.d_low, ...), custom_call_target="tpu_custom_call" | custom-call | flops 50000000 | bytes 5000000 | tf_op jit(solution)/shard_map/pallas_call | solution.py:547
  (1 shorter events, 0.0 us)
Async XLA Ops:
  0.6 49.1 %copy-start.7 = (f32[8,3,3]{0,2,1:T(4,128)S(1)}, f32[8,3,3]{0,2,1:T(4,128)}, u32[]{:S(2)}) copy-start(f32[8,3,3]{0,2,1:T(4,128)} %param.15) | copy-start | bytes 868
  0.6 49.1 %copy-start.9 = (bf16[8,32]{1,0:T(8,128)(2,1)S(1)}, bf16[8,32]{1,0:T(8,128)(2,1)}, u32[]{:S(2)}) copy-start(bf16[8,32]{1,0:T(8,128)(2,1)} %kernel_z.1) | copy-start | bytes 1540
  0.7 49.1 %copy-start.6 = (bf16[8,2048]{1,0:T(8,128)(2,1)S(1)}, bf16[8,2048]{1,0:T(8,128)(2,1)}, u32[]{:S(2)}) copy-start(bf16[8,2048]{1,0:T(8,128)(2,1)} %kernel_y.1) | copy-start | bytes 98308
  0.7 49.1 %copy-start.8 = (bf16[8,256]{1,0:T(8,128)(2,1)S(1)}, bf16[8,256]{1,0:T(8,128)(2,1)}, u32[]{:S(2)}) copy-start(bf16[8,256]{1,0:T(8,128)(2,1)} %kernel_x.1) | copy-start | bytes 12292
  2.8 17.6 %collective-permute-start = (bf16[128,128]{1,0:T(8,128)(2,1)}, bf16[128,128]{1,0:T(8,128)(2,1)S(1)}, u32[]{:S(2)}, u32[]{:S(2)}) collective-permute-start(bf16[128,128]{1,0:T(8,128)(2,1)} %shard_map.95.own), channel_id=1, source_target_pairs={{0,32},{8,40},{16,48},{24,56},{32,0},{40,8},{48,16},{56,24},{1,33}... | collective-permute-start | bytes 98312 | tf_op jit(solution)/shard_map/ppermute | solution.py:460
  17.6 1.0 copy-start
  18.6 0.9 copy-start.2
  19.5 0.8 copy-start.3
  47.8 5.5 %collective-permute-start.2 = (bf16[4,912,128]{2,1,0:T(8,128)(2,1)S(1)}, bf16[4,912,128]{2,1,0:T(8,128)(2,1)S(1)}, u32[]{:S(2)}, u32[]{:S(2)}) collective-permute-start(bf16[4,912,128]{2,1,0:T(8,128)(2,1)S(1)} %all_to_all.16.own), channel_id=1, source_target_pairs={{0,64},{64,0},{128,192},{192,128},{256,320},{320,256},{384,448},{4... | collective-permute-start | bytes 2801672 | tf_op jit(solution)/shard_map/ppermute | solution.py:460
  53.3 37.8 %copy-start.1 = (f32[3,4,32,256]{3,2,1,0:T(8,128)S(1)}, f32[3,4,32,256]{3,2,1,0:T(8,128)}, u32[]{:S(2)}) copy-start(f32[3,4,32,256]{3,2,1,0:T(8,128)} %mag.5) | copy-start | bytes 1179652
  53.3 37.8 %copy-start.4 = (f32[16]{0:T(128)S(1)}, f32[16]{0:T(128)}, u32[]{:S(2)}) copy-start(f32[16]{0:T(128)} %sat.3) | copy-start | bytes 196
  53.4 37.8 %copy-start.5 = (f32[16]{0:T(128)S(1)}, f32[16]{0:T(128)}, u32[]{:S(2)}) copy-start(f32[16]{0:T(128)} %stiff.1) | copy-start | bytes 196
  58.5 26.7 %all-to-all-start.2 = ((s16[8,120,128]{2,1,0:T(8,128)(2,1)}), s16[8,120,128]{2,1,0:T(8,128)(2,1)S(1)}, u32[]{:S(2)}, u32[]{:S(2)}) async-start(s16[8,120,128]{2,1,0:T(8,128)(2,1)} %shard_map.102), calls=%async_computation.2 | async-start | bytes 491520 | tf_op jit(solution)/shard_map/all_to_all | solution.py:533
  68.2 3.1 %collective-permute-start.1 = (bf16[144,128]{1,0:T(8,128)(2,1)S(1)}, bf16[144,128]{1,0:T(8,128)(2,1)S(1)}, u32[]{:S(2)}, u32[]{:S(2)}) collective-permute-start(bf16[144,128]{1,0:T(8,128)(2,1)S(1)} %get-tuple-element.19), channel_id=1, source_target_pairs={{0,64},{64,0},{128,192},{192,128},{256,320},{320,256},{384,448},{4... | collective-permute-start | bytes 110600 | tf_op jit(solution)/shard_map/ppermute | solution.py:460
  71.6 19.6 %collective-permute-start.4 = (bf16[992,128]{1,0:T(8,128)(2,1)S(1)}, bf16[992,128]{1,0:T(8,128)(2,1)S(1)}, u32[]{:S(2)}, u32[]{:S(2)}) collective-permute-start(bf16[992,128]{1,0:T(8,128)(2,1)S(1)} %get-tuple-element.21.own_low), channel_id=1, source_target_pairs={{1,0},{2,1},{3,2},{4,3},{5,4},{6,5},{7,6},{9,8},{10,9},{11,10},{12... | collective-permute-start | bytes 761864 | tf_op jit(solution)/shard_map/ppermute | solution.py:522
  73.5 17.6 %collective-permute-start.3 = (bf16[992,128]{1,0:T(8,128)(2,1)S(1)}, bf16[992,128]{1,0:T(8,128)(2,1)S(1)}, u32[]{:S(2)}, u32[]{:S(2)}) collective-permute-start(bf16[992,128]{1,0:T(8,128)(2,1)S(1)} %get-tuple-element.22.own_high), channel_id=1, source_target_pairs={{0,1},{1,2},{2,3},{3,4},{4,5},{5,6},{6,7},{8,9},{9,10},{10,11},{11... | collective-permute-start | bytes 761864 | tf_op jit(solution)/shard_map/ppermute | solution.py:521
  85.3 12.4 %collective-permute-start.6 = (f32[120,128]{1,0:T(8,128)S(1)}, f32[120,128]{1,0:T(8,128)S(1)}, u32[]{:S(2)}, u32[]{:S(2)}) collective-permute-start(f32[120,128]{1,0:T(8,128)S(1)} %shard_map.103.d_own), channel_id=1, source_target_pairs={{1,0},{2,1},{3,2},{4,3},{5,4},{6,5},{7,6},{9,8},{10,9},{11,10},{12... | collective-permute-start | bytes 184328 | tf_op jit(solution)/shard_map/ppermute | solution.py:546
  87.4 10.3 %collective-permute-start.5 = (f32[120,128]{1,0:T(8,128)S(1)}, f32[120,128]{1,0:T(8,128)S(1)}, u32[]{:S(2)}, u32[]{:S(2)}) collective-permute-start(f32[120,128]{1,0:T(8,128)S(1)} %shard_map.103.d_own), channel_id=1, source_target_pairs={{0,1},{1,2},{2,3},{3,4},{4,5},{5,6},{6,7},{8,9},{9,10},{10,11},{11... | collective-permute-start | bytes 184328 | tf_op jit(solution)/shard_map/ppermute | solution.py:545

commit v9 on v5

--- a/solution.py
+++ b/solution.py
@@ -324,7 +324,7 @@
                 m0[c, p, 0:32, 0:256] = mag[c, z]
         ids = whole[3].astype(i32)
         aa[p] = jnp.where(inside & ok, lookup(ids, stiff), 0.0)
-        ss[p] = 2.0 / lookup(ids, sat)
+        ss[p] = (2.0 * TIME_STEP) / lookup(ids, sat)
 
     def weight(u, v):
         den = u + v
@@ -356,47 +356,49 @@
 
 
 def substeps_kernel(
-    fields_hbm, d_own, d_low, d_high, state_out, demag_out, fields, m1, m2, fz, field, rows, spread, sems
+    fields_hbm, d_own, d_low, d_high, state_out, demag_out, fields, m1, m2, fz, field, rows, sems
 ):
     m0, hh, wx, wy, wz, ss = parts_of(fields)
-    cuts = (pl.ds(0, 54), pl.ds(54, 40))
+    spans = ((1, 8), (11, 8), (21, 8), (30, 24), (56, 6), (66, 6), (75, 7), (86, 6))
+    cuts = [pl.ds(first, count) for first, count in spans]
     fetches = [pltpu.make_async_copy(fields_hbm.at[c], fields.at[c], sems.at[n]) for n, c in enumerate(cuts)]
     for fetch in fetches:
         fetch.start()
     for q in range(6):
         demag_out[q // 3, q % 3] = d_own[pl.ds(6 + q, 16, stride=6), :]
-    lane24 = iota((24, 128), 1)
-    row24 = iota((24, 128), 0)
+    lane24, row24 = iota((24, 128), 1), iota((24, 128), 0)
+    coarse_x = jnp.where(row24 == 17, 0, row24 + 1)
     sources = [(d_low, 3), (d_own, 0), (d_own, 3), (d_high, 0)]
-    rows[...] = jnp.zeros_like(rows)
     for level in range(4):
         ref, first = sources[level]
         for i in range(3):
-            g = level * 3 + i
-            q = first + i
-            rows[g * 24 : g * 24 + 18, 0:128] = ref[pl.ds(q, 18, stride=6), :]
+            top, q = (level * 3 + i) * 24, first + i
+            rows[top : top + 16, 0:128] = ref[pl.ds(6 + q, 16, stride=6), :]
+            ends = jnp.where(row24[0:8] == 0, ref[102 + q : 103 + q, :], ref[q : q + 1, :])
+            rows[top + 16 : top + 24, 0:128] = ends
             rim = jnp.broadcast_to(ref[108 + q : 109 + q, :], (24, 128))
-            rows[g * 24 : g * 24 + 24, 128:256] = jnp.where(lane24 // 2 == row24, rim, 0.0)
+            rows[top : top + 24, 128:256] = jnp.where(lane24 // 2 == coarse_x, rim, 0.0)
     x = rows[...]
     hi = x.astype(bf16)
     lo = (x - hi.astype(f32)).astype(bf16)
-    a, b = iota((128, 256), 0), iota((128, 256), 1)
+    a, b = iota((256, 256), 0) % 128, iota((256, 256), 1)
     wide = one_hot(b // 2 == a)
-    a, b = iota((128, 128), 0), iota((128, 128), 1)
+    a, b = iota((256, 128), 0) % 128, iota((256, 128), 1)
     ends = one_hot(((a % 2 == 1) & (b < 2)) | ((a % 2 == 0) & (b >= 126)))
-    spread[:, 0:256] = dot(hi[:, :128], wide) + dot(lo[:, :128], wide)
-    spread[:, 256:384] = dot(hi[:, 128:], ends) + dot(lo[:, 128:], ends)
-    r40, c24 = iota((40, 24), 0), iota((40, 24), 1)
-    tall = one_hot(((r40 < 32) & (c24 == 1 + r40 // 2)) | ((r40 >= 32) & (r40 < 34) & (c24 == 17)) | ((r40 >= 38) & (c24 == 0)))
+    block = dot(jnp.concatenate([hi[:, :128], lo[:, :128]], axis=1), wide) * TIME_STEP
+    sides = dot(jnp.concatenate([hi[:, 128:], lo[:, 128:]], axis=1), ends) * TIME_STEP
+    row8 = iota((8, 128), 0)
     for g in range(12):
-        v = spread[g * 24 : (g + 1) * 24, :]
-        hi = v.astype(bf16)
-        lo = (v - hi.astype(f32)).astype(bf16)
-        field[g] = dot(tall, hi) + dot(tall, lo)
+        for q in range(3):
+            v = block[g * 24 : (g + 1) * 24, q * 128 : (q + 1) * 128] if q < 2 else sides[g * 24 : (g + 1) * 24]
+            field[g, q, pl.ds(0, 16, stride=2), :] = v[0:16]
+            field[g, q, pl.ds(1, 16, stride=2), :] = v[0:16]
+            field[g, q, 32:40, :] = jnp.where(row8 < 2, v[16:17], jnp.where(row8 >= 6, v[17:18], 0.0))
     for step in range(3):
         src, dst = ((m0, m1), (m1, m2), (m2, None))[step]
         if step < 2:
-            fetches[step].wait()
+            for fetch in (fetches[:4], fetches[4:])[step]:
+                fetch.wait()
         first, last = step + 1, 8 - step
 
         def plane(p, carry):
@@ -410,10 +412,10 @@
                     total, up = exchange(src, wx, wy, wz, c, p, fz[c])
                     fz[c] = up
                     total = total * ss[p]
-                h.append(total + field[level * 3 + c])
+                h.append(total + jnp.concatenate([field[level * 3 + c, q] for q in range(3)], axis=1))
             t = [m[1] * h[2] - m[2] * h[1], m[2] * h[0] - m[0] * h[2], m[0] * h[1] - m[1] * h[0]]
             u = [m[1] * t[2] - m[2] * t[1], m[2] * t[0] - m[0] * t[2], m[0] * t[1] - m[1] * t[0]]
-            raw = [m[c] - TIME_STEP * (t[c] + DAMPING * u[c]) for c in range(3)]
+            raw = [m[c] - (t[c] + DAMPING * u[c]) for c in range(3)]
             scale = lax.rsqrt(jnp.maximum(raw[0] * raw[0] + raw[1] * raw[1] + raw[2] * raw[2], 1e-30))
             for c in range(3):
                 if step < 2:
@@ -519,8 +521,8 @@
         [HB] + [VM] * 3,
         [pltpu.VMEM((94, 40, 384), f32)]
         + [pltpu.VMEM((3,) + big, f32)] * 2
-        + [pltpu.VMEM((3, 40, 384), f32), pltpu.VMEM((12, 40, 384), f32)]
-        + [pltpu.VMEM((288, 256), f32), pltpu.VMEM((288, 384), f32), pltpu.SemaphoreType.DMA((2,))],
+        + [pltpu.VMEM((3, 40, 384), f32), pltpu.VMEM((12, 3, 40, 128), f32)]
+        + [pltpu.VMEM((288, 256), f32), pltpu.SemaphoreType.DMA((8,))],
         50_000_000,
         5_000_000,
         FULL - 14_000_000,

time: 112 us -> 112 us (level)
  no operation moved by 1% of the time
where the time goes in v9:
time: 112 us; the launch traced here: 111 us
  starting transfers between devices  40 us (36%)
  Pallas kernels  27.5 us (25%)
  blocking collectives  27.2 us (24%)
  waiting for transfers between devices  9.04 us (8%)
  local copies, waits for them, and re-layouts  6.95 us (6%)
    ppermute x3, starting transfers between devices, swap(): return lax.ppermute(value, axis, [(i, i ^ bit) for i in range(8)])  18.6 us
    all_to_all x1, blocking collectives, step(): lax.all_to_all(pay, 'gx', 0, 0, tiled=True, axis_index_groups=groups)  16.3 us
    all_to_all x1, blocking collectives, step(): lax.all_to_all(pay, 'gy', 0, 0, tiled=True, axis_index_groups=groups)  10.9 us
    all_to_all x1, starting transfers between devices, step(): parts = lax.all_to_all(parts, 'gz', 0, 0, tiled=True)  9.69 us
    all_to_all x1, waiting for transfers between devices, step(): parts = lax.all_to_all(parts, 'gz', 0, 0, tiled=True)  7.84 us
    pallas_call x1, Pallas kernels, step(): call(weights_kernel, shape((94, 40, 384), f32), [VM] * 5 + [SM] * 2, [plt...  7.35 us
    unnamed x22, local copies, waits for them, and re-layouts  6.95 us
    pallas_call x1, Pallas kernels, step(): call(substeps_kernel, [shape((3, 4, 32, 256), f32), shape((2, 3, 16, 128)...  6.65 us
  transfers between devices with their start and end apart: 8, of which 2 were waited for; matrix products, arithmetic and copies ran while one was open for 0% of the time, Pallas kernels for 12%

profile of v9, /device:TPU:32, one launch (start us, length us, event | category | flops | bytes accessed | tf_op | source)
XLA Modules:
  0.0 111.5 jit_solution(2390626262888188283)
XLA Ops:
  0.6 2.1 %shard_map.95.own = bf16[128,128]{1,0:T(8,128)(2,1)} custom-call(f32[3,4,32,256]{3,2,1,0:T(8,128)} %mag.5, s32[4,32,256]{2,1,0:T(8,128)} %grains.3, f32[16]{0:T(128)} %sat.3), custom_call_target="tpu_custom_call" | custom-call | flops 20000000 | bytes 600000 | tf_op jit(solution)/shard_map/pallas_call | solution.py:442
  2.7 14.8 %collective-permute-start = (bf16[128,128]{1,0:T(8,128)(2,1)}, bf16[128,128]{1,0:T(8,128)(2,1)S(1)}, u32[]{:S(2)}, u32[]{:S(2)}) collective-permute-start(bf16[128,128]{1,0:T(8,128)(2,1)} %shard_map.95.own), channel_id=1, source_target_pairs={{0,32},{8,40},{16,48},{24,56},{32,0},{40,8},{48,16},{56,24},{1,33}... | collective-permute-start | bytes 98312 | tf_op jit(solution)/shard_map/ppermute | solution.py:434
  17.5 0.0 copy-start
  17.5 1.0 copy-done
  18.5 0.0 copy-start.1
  18.5 0.9 copy-done.1
  19.4 0.0 copy-start.4
  19.4 0.8 copy-done.4
  20.2 0.1 shard_map.96
  20.2 0.0 collective-permute-done.other
  20.3 10.9 %all_to_all.15.gathered = bf16[4,256,128]{2,1,0:T(8,128)(2,1)S(1)} all-to-all(bf16[4,256,128]{2,1,0:T(8,128)(2,1)S(1)} %shard_map.97), channel_id=1, replica_groups={{0,8,16,24},{32,40,48,56},{1,9,17,25},{33,41,49,57},{2,10,18,26},{34,42..., dimensions={0} | all-to-all | bytes 524288 | tf_op jit(solution)/shard_map/all_to_all | solution.py:471
  31.2 0.3 shard_map.98
  31.5 16.3 %all_to_all.16.own = bf16[4,912,128]{2,1,0:T(8,128)(2,1)S(1)} all-to-all(bf16[4,912,128]{2,1,0:T(8,128)(2,1)S(1)} %get-tuple-element.18), channel_id=1, replica_groups={{0,128,256,384},{64,192,320,448},{1,129,257,385},{65,193,321,449},{2,13..., dimensions={0} | all-to-all | bytes 1867776 | tf_op jit(solution)/shard_map/all_to_all | solution.py:482
  47.8 1.9 %collective-permute-start.2 = (bf16[4,912,128]{2,1,0:T(8,128)(2,1)S(1)}, bf16[4,912,128]{2,1,0:T(8,128)(2,1)S(1)}, u32[]{:S(2)}, u32[]{:S(2)}) collective-permute-start(bf16[4,912,128]{2,1,0:T(8,128)(2,1)S(1)} %all_to_all.16.own), channel_id=1, source_target_pairs={{0,64},{64,0},{128,192},{192,128},{256,320},{320,256},{384,448},{4... | collective-permute-start | bytes 2801672 | tf_op jit(solution)/shard_map/ppermute | solution.py:434
  49.7 0.0 copy-start.5
  49.7 0.7 copy-done.5
  50.5 0.0 copy-start.6
  50.5 0.7 copy-done.6
  51.1 0.0 copy-start.7
  51.2 0.7 copy-done.7
  51.8 0.0 copy-start.8
  51.8 0.7 copy-done.8
  52.5 5.7 %shard_map.101 = (bf16[8,128,2176]{2,1,0:T(8,128)(2,1)}, f32[192,128]{1,0:T(8,128)S(1)}, bf16[64,192]{1,0:T(8,128)(2,1)S(1)}) custom-call(bf16[8,256]{1,0:T(8,128)(2,1)S(1)} %copy-done.7, bf16[8,2048]{1,0:T(8,128)(2,1)S(1)} %copy-done.5, bf16[8,32]{1,0:T(8,128)(2,1)S(1)} %copy-done.8, f32[3,3,8]{2,1,0:T(4,128)S(1)} %bitcast.1), custom_call_target="tpu_custom_call" | custom-call | flops 20000000 | bytes 5000000 | tf_op jit(solution)/shard_map/pallas_call | solution.py:460
  58.2 0.0 collective-permute-done.2.rc
  58.2 5.1 %shard_map.102 = s16[8,120,128]{2,1,0:T(8,128)(2,1)} custom-call(bf16[4,912,128]{2,1,0:T(8,128)(2,1)S(1)} %all_to_all.16.own, bf16[4,912,128]{2,1,0:T(8,128)(2,1)S(1)} %collective-permute-done.2.rc, f32[192,128]{1,0:T(8,128)S(1)} %get-tuple-element.21.kx, bf16[8,128,2176]{2,1,0:T(8,128)(2,1)} %get-tuple-element.22.strip_hbm, ...), custom_call_target="tpu_custom_call" | custom-call | flops 2000000000 | bytes 10000000 | tf_op jit(solution)/shard_map/pallas_call | solution.py:496
  63.4 9.7 %all-to-all-start.2 = ((s16[8,120,128]{2,1,0:T(8,128)(2,1)}), s16[8,120,128]{2,1,0:T(8,128)(2,1)S(1)}, u32[]{:S(2)}, u32[]{:S(2)}) async-start(s16[8,120,128]{2,1,0:T(8,128)(2,1)} %shard_map.102), calls=%async_computation.2 | async-start | bytes 491520 | tf_op jit(solution)/shard_map/all_to_all | solution.py:506
  73.0 1.9 %collective-permute-start.1 = (bf16[144,128]{1,0:T(8,128)(2,1)S(1)}, bf16[144,128]{1,0:T(8,128)(2,1)S(1)}, u32[]{:S(2)}, u32[]{:S(2)}) collective-permute-start(bf16[144,128]{1,0:T(8,128)(2,1)S(1)} %get-tuple-element.17), channel_id=1, source_target_pairs={{0,64},{64,0},{128,192},{192,128},{256,320},{320,256},{384,448},{4... | collective-permute-start | bytes 110600 | tf_op jit(solution)/shard_map/ppermute | solution.py:434
  75.0 1.2 %collective-permute-done.1.near = bf16[144,128]{1,0:T(8,128)(2,1)S(1)} collective-permute-done((bf16[144,128]{1,0:T(8,128)(2,1)S(1)}, bf16[144,128]{1,0:T(8,128)(2,1)S(1)}, u32[]{:S(2)}, u32[]{:S(2)}) %collective-permute-start.1) | collective-permute-done | bytes 36896 | tf_op jit(solution)/shard_map/ppermute | solution.py:434
  76.1 0.2 shard_map.99
  76.3 0.0 copy-start.2
  76.3 0.0 copy-start.3
  76.3 1.9 %collective-permute-start.4 = (bf16[12,40,384]{2,1,0:T(8,128)(2,1)S(1)}, bf16[12,40,384]{2,1,0:T(8,128)(2,1)S(1)}, u32[]{:S(2)}, u32[]{:S(2)}) collective-permute-start(bf16[12,40,384]{2,1,0:T(8,128)(2,1)S(1)} %get-tuple-element.19.own_low), channel_id=1, source_target_pairs={{1,0},{2,1},{3,2},{4,3},{5,4},{6,5},{7,6},{9,8},{10,9},{11,10},{12... | collective-permute-start | bytes 1105928 | tf_op jit(solution)/shard_map/ppermute | solution.py:495
  78.3 3.9 %collective-permute-start.3 = (bf16[12,40,384]{2,1,0:T(8,128)(2,1)S(1)}, bf16[12,40,384]{2,1,0:T(8,128)(2,1)S(1)}, u32[]{:S(2)}, u32[]{:S(2)}) collective-permute-start(bf16[12,40,384]{2,1,0:T(8,128)(2,1)S(1)} %get-tuple-element.20.own_high), channel_id=1, source_target_pairs={{0,1},{1,2},{2,3},{3,4},{4,5},{5,6},{6,7},{8,9},{9,10},{10,11},{11... | collective-permute-start | bytes 1105928 | tf_op jit(solution)/shard_map/ppermute | solution.py:494
  82.2 7.8 %all-to-all-done.2.parts = s16[8,120,128]{2,1,0:T(8,128)(2,1)S(1)} async-done(((s16[8,120,128]{2,1,0:T(8,128)(2,1)}), s16[8,120,128]{2,1,0:T(8,128)(2,1)S(1)}, u32[]{:S(2)}, u32[]{:S(2)}) %all-to-all-start.2) | async-done | bytes 245792 | tf_op jit(solution)/shard_map/all_to_all | solution.py:506
  90.0 0.1 shard_map.103.d_own
  90.1 2.1 %collective-permute-start.6 = (f32[120,128]{1,0:T(8,128)S(1)}, f32[120,128]{1,0:T(8,128)S(1)}, u32[]{:S(2)}, u32[]{:S(2)}) collective-permute-start(f32[120,128]{1,0:T(8,128)S(1)} %shard_map.103.d_own), channel_id=1, source_target_pairs={{1,0},{2,1},{3,2},{4,3},{5,4},{6,5},{7,6},{9,8},{10,9},{11,10},{12... | collective-permute-start | bytes 184328 | tf_op jit(solution)/shard_map/ppermute | solution.py:517
  92.2 3.7 %collective-permute-start.5 = (f32[120,128]{1,0:T(8,128)S(1)}, f32[120,128]{1,0:T(8,128)S(1)}, u32[]{:S(2)}, u32[]{:S(2)}) collective-permute-start(f32[120,128]{1,0:T(8,128)S(1)} %shard_map.103.d_own), channel_id=1, source_target_pairs={{0,1},{1,2},{2,3},{3,4},{4,5},{5,6},{6,7},{8,9},{9,10},{10,11},{11... | collective-permute-start | bytes 184328 | tf_op jit(solution)/shard_map/ppermute | solution.py:516
  96.0 0.0 collective-permute-done.4.z_high
  96.0 0.0 copy-start.9
  96.0 0.0 collective-permute-done.3.z_low
  96.0 0.0 copy-done.2
  96.0 0.0 copy-done.3
  96.0 0.7 copy-done.9
  96.7 0.8 copy-done.10
  97.5 7.4 %shard_map.100.fields_hbm = f32[94,40,384]{2,1,0:T(8,128)} custom-call(f32[3,4,32,256]{3,2,1,0:T(8,128)} %mag.5, bf16[12,40,384]{2,1,0:T(8,128)(2,1)} %copy-done.2, bf16[12,40,384]{2,1,0:T(8,128)(2,1)} %copy-done.3, bf16[12,40,384]{2,1,0:T(8,128)(2,1)} %copy-done.10, bf16[12,40,384]{2,1,0:T(8,128)(2,1)} %copy-done.9, f32[16]{0:T(128)} %stiff.1, f32[16]{0:T(128)} %sat.3), custom_call_target="tpu_custom_call" | custom-call | flops 20000000 | bytes 5000000 | tf_op jit(solution)/shard_map/pallas_call | solution.py:507
  104.8 0.0 collective-permute-done.6.d_high
  104.8 0.0 collective-permute-done.5.d_low
  104.9 6.6 %shard_map.104 = (f32[3,4,32,256]{3,2,1,0:T(8,128)}, f32[2,3,16,128]{3,2,1,0:T(8,128)}) custom-call(f32[94,40,384]{2,1,0:T(8,128)} %shard_map.100.fields_hbm, f32[120,128]{1,0:T(8,128)S(1)} %shard_map.103.d_own, f32[120,128]{1,0:T(8,128)S(1)} %collective-permute-done.5.d_low, f32[120,128]{1,0:T(8,128)S(1)} %collective-permute-done.6.d_high), custom_call_target="tpu_custom_call" | custom-call | flops 50000000 | bytes 5000000 | tf_op jit(solution)/shard_map/pallas_call | solution.py:518
  (2 shorter events, 0.0 us)
Async XLA Ops:
  2.7 17.6 %collective-permute-start = (bf16[128,128]{1,0:T(8,128)(2,1)}, bf16[128,128]{1,0:T(8,128)(2,1)S(1)}, u32[]{:S(2)}, u32[]{:S(2)}) collective-permute-start(bf16[128,128]{1,0:T(8,128)(2,1)} %shard_map.95.own), channel_id=1, source_target_pairs={{0,32},{8,40},{16,48},{24,56},{32,0},{40,8},{48,16},{56,24},{1,33}... | collective-permute-start | bytes 98312 | tf_op jit(solution)/shard_map/ppermute | solution.py:434
  17.5 1.0 copy-start
  18.5 0.9 copy-start.1
  19.4 0.8 copy-start.4
  47.8 10.5 %collective-permute-start.2 = (bf16[4,912,128]{2,1,0:T(8,128)(2,1)S(1)}, bf16[4,912,128]{2,1,0:T(8,128)(2,1)S(1)}, u32[]{:S(2)}, u32[]{:S(2)}) collective-permute-start(bf16[4,912,128]{2,1,0:T(8,128)(2,1)S(1)} %all_to_all.16.own), channel_id=1, source_target_pairs={{0,64},{64,0},{128,192},{192,128},{256,320},{320,256},{384,448},{4... | collective-permute-start | bytes 2801672 | tf_op jit(solution)/shard_map/ppermute | solution.py:434
  49.7 0.8 copy-start.5
  50.5 0.7 copy-start.6
  51.1 0.7 copy-start.7
  51.8 0.7 copy-start.8
  63.4 26.7 %all-to-all-start.2 = ((s16[8,120,128]{2,1,0:T(8,128)(2,1)}), s16[8,120,128]{2,1,0:T(8,128)(2,1)S(1)}, u32[]{:S(2)}, u32[]{:S(2)}) async-start(s16[8,120,128]{2,1,0:T(8,128)(2,1)} %shard_map.102), calls=%async_computation.2 | async-start | bytes 491520 | tf_op jit(solution)/shard_map/all_to_all | solution.py:506
  73.0 3.1 %collective-permute-start.1 = (bf16[144,128]{1,0:T(8,128)(2,1)S(1)}, bf16[144,128]{1,0:T(8,128)(2,1)S(1)}, u32[]{:S(2)}, u32[]{:S(2)}) collective-permute-start(bf16[144,128]{1,0:T(8,128)(2,1)S(1)} %get-tuple-element.17), channel_id=1, source_target_pairs={{0,64},{64,0},{128,192},{192,128},{256,320},{320,256},{384,448},{4... | collective-permute-start | bytes 110600 | tf_op jit(solution)/shard_map/ppermute | solution.py:434
  76.3 19.7 %copy-start.2 = (bf16[12,40,384]{2,1,0:T(8,128)(2,1)}, bf16[12,40,384]{2,1,0:T(8,128)(2,1)S(1)}, u32[]{:S(2)}) copy-start(bf16[12,40,384]{2,1,0:T(8,128)(2,1)S(1)} %get-tuple-element.19.own_low) | copy-start | bytes 1105924
  76.3 19.7 %copy-start.3 = (bf16[12,40,384]{2,1,0:T(8,128)(2,1)}, bf16[12,40,384]{2,1,0:T(8,128)(2,1)S(1)}, u32[]{:S(2)}) copy-start(bf16[12,40,384]{2,1,0:T(8,128)(2,1)S(1)} %get-tuple-element.20.own_high) | copy-start | bytes 1105924
  76.3 19.6 %collective-permute-start.4 = (bf16[12,40,384]{2,1,0:T(8,128)(2,1)S(1)}, bf16[12,40,384]{2,1,0:T(8,128)(2,1)S(1)}, u32[]{:S(2)}, u32[]{:S(2)}) collective-permute-start(bf16[12,40,384]{2,1,0:T(8,128)(2,1)S(1)} %get-tuple-element.19.own_low), channel_id=1, source_target_pairs={{1,0},{2,1},{3,2},{4,3},{5,4},{6,5},{7,6},{9,8},{10,9},{11,10},{12... | collective-permute-start | bytes 1105928 | tf_op jit(solution)/shard_map/ppermute | solution.py:495
  78.3 17.7 %collective-permute-start.3 = (bf16[12,40,384]{2,1,0:T(8,128)(2,1)S(1)}, bf16[12,40,384]{2,1,0:T(8,128)(2,1)S(1)}, u32[]{:S(2)}, u32[]{:S(2)}) collective-permute-start(bf16[12,40,384]{2,1,0:T(8,128)(2,1)S(1)} %get-tuple-element.20.own_high), channel_id=1, source_target_pairs={{0,1},{1,2},{2,3},{3,4},{4,5},{5,6},{6,7},{8,9},{9,10},{10,11},{11... | collective-permute-start | bytes 1105928 | tf_op jit(solution)/shard_map/ppermute | solution.py:494
  90.1 14.7 %collective-permute-start.6 = (f32[120,128]{1,0:T(8,128)S(1)}, f32[120,128]{1,0:T(8,128)S(1)}, u32[]{:S(2)}, u32[]{:S(2)}) collective-permute-start(f32[120,128]{1,0:T(8,128)S(1)} %shard_map.103.d_own), channel_id=1, source_target_pairs={{1,0},{2,1},{3,2},{4,3},{5,4},{6,5},{7,6},{9,8},{10,9},{11,10},{12... | collective-permute-start | bytes 184328 | tf_op jit(solution)/shard_map/ppermute | solution.py:517
  92.2 12.6 %collective-permute-start.5 = (f32[120,128]{1,0:T(8,128)S(1)}, f32[120,128]{1,0:T(8,128)S(1)}, u32[]{:S(2)}, u32[]{:S(2)}) collective-permute-start(f32[120,128]{1,0:T(8,128)S(1)} %shard_map.103.d_own), channel_id=1, source_target_pairs={{0,1},{1,2},{2,3},{3,4},{4,5},{5,6},{6,7},{8,9},{9,10},{10,11},{11... | collective-permute-start | bytes 184328 | tf_op jit(solution)/shard_map/ppermute | solution.py:516
  96.0 0.7 copy-start.9
  96.7 0.8 copy-start.10
